TPU v7x, 32 devices: a whole 2x2x4 slice. The times are simulated.
32 devices in a mesh: replica: 4 (over x, core), fsdp: 8 (over z, y).
Axes of the slice: x: 2, y: 2, z: 4, core: 2. Of those that a mesh axis runs over, the one named last changes fastest.
Arguments:
- decoder_input: bfloat16 [64, 256, 1024], P(('replica', 'fsdp')), may hold values from -6 to 6
- encoder_out: bfloat16 [64, 512, 1024], P(('replica', 'fsdp')), may hold values from -6 to 6
- prefix_length: int32 [64], P(('replica', 'fsdp')), may hold values from 25 to 128
- output_grad: bfloat16 [64, 256, 1024], P(('replica', 'fsdp')), may hold values from -6 to 6
- self_query: bfloat16 [1024, 1024], P('fsdp'), may hold values from -0.1875 to 0.1875
- self_key: bfloat16 [1024, 1024], P('fsdp'), may hold values from -0.1875 to 0.1875
- self_value: bfloat16 [1024, 1024], P('fsdp'), may hold values from -0.1875 to 0.1875
- self_output: bfloat16 [1024, 1024], P('fsdp'), may hold values from -2 to 2
- selfquery_bias: bfloat16 [1024], P('fsdp'), may hold values from -2 to 2
- selfvalue_bias: bfloat16 [1024], P('fsdp'), may hold values from -0.19921875 to 0.19921875
- self_attention_output_bias: bfloat16 [1024], P('fsdp'), may hold values from -2 to 2
- cross_query: bfloat16 [1024, 1024], P('fsdp'), may hold values from -0.1875 to 0.1875
- cross_key: bfloat16 [1024, 1024], P('fsdp'), may hold values from -0.1875 to 0.1875
- cross_value: bfloat16 [1024, 1024], P('fsdp'), may hold values from -0.1875 to 0.1875
- cross_output: bfloat16 [1024, 1024], P('fsdp'), may hold values from -3 to 3
- crossquery_bias: bfloat16 [1024], P('fsdp'), may hold values from -2 to 2
- crossvalue_bias: bfloat16 [1024], P('fsdp'), may hold values from -0.19921875 to 0.19921875
- crossoutput_bias: bfloat16 [1024], P('fsdp'), may hold values from -2 to 2
- expand_weight: bfloat16 [1024, 4096], P('fsdp'), may hold values from -0.1875 to 0.1875
- expand_bias: bfloat16 [4096], P('fsdp'), may hold values from -2 to 2
- down_projection_weight: bfloat16 [4096, 1024], P('fsdp'), may hold values from -0.09375 to 0.09375
- reduce_bias: bfloat16 [1024], P('fsdp'), may hold values from -2 to 2
- selfnorm_gain: bfloat16 [1024], P('fsdp'), may hold values from 0.25 to 1.75
- selfnorm_bias: bfloat16 [1024], P('fsdp'), may hold values from -2 to 2
- crossnorm_gain: bfloat16 [1024], P('fsdp'), may hold values from 0.25 to 1.75
- crossnorm_bias: bfloat16 [1024], P('fsdp'), may hold values from -2 to 2
- finalnorm_gain: bfloat16 [1024], P('fsdp'), may hold values from 0.25 to 1.75
- finalnorm_bias: bfloat16 [1024], P('fsdp'), may hold values from -2 to 2
Outputs:
- layer_out: bfloat16 [64, 256, 1024], P(('replica', 'fsdp'))
- input_grad: float32 [64, 256, 1024], P(('replica', 'fsdp'))
- encoder_grad: float32 [64, 512, 1024], P(('replica', 'fsdp'))
- self_query_grad: float32 [1024, 1024], P('fsdp')
- self_key_grad: float32 [1024, 1024], P('fsdp')
- self_value_grad: float32 [1024, 1024], P('fsdp')
- self_output_grad: float32 [1024, 1024], P('fsdp')
- selfquery_bias_grad: float32 [1024], P('fsdp')
- selfvalue_bias_grad: float32 [1024], P('fsdp')
- selfoutput_bias_grad: float32 [1024], P('fsdp')
- cross_query_grad: float32 [1024, 1024], P('fsdp')
- cross_key_grad: float32 [1024, 1024], P('fsdp')
- cross_value_grad: float32 [1024, 1024], P('fsdp')
- cross_output_grad: float32 [1024, 1024], P('fsdp')
- crossquery_bias_grad: float32 [1024], P('fsdp')
- crossvalue_bias_grad: float32 [1024], P('fsdp')
- crossoutput_bias_grad: float32 [1024], P('fsdp')
- expand_weight_grad: float32 [1024, 4096], P('fsdp')
- expand_bias_grad: float32 [4096], P('fsdp')
- reduce_weight_grad: float32 [4096, 1024], P('fsdp')
- reduce_bias_grad: float32 [1024], P('fsdp')
- selfnorm_gain_grad: float32 [1024], P('fsdp')
- selfnorm_bias_grad: float32 [1024], P('fsdp')
- crossnorm_gain_grad: float32 [1024], P('fsdp')
- crossnorm_bias_grad: float32 [1024], P('fsdp')
- final_norm_gain_gradient: float32 [1024], P('fsdp')
- finalnorm_bias_grad: float32 [1024], P('fsdp')
All inputs are finite; a program needn't handle non-finite values.
Results may differ from a plain program's by a relative error of at most 0.023.
Values may be sent and summed in bfloat16 or wider, within the bound.
No kernel may reach another device: no remote copies, remote signals or barrier semaphores. Data moves between devices by JAX's collectives and lax.ppermute only.
A program may use at most 256 MiB of HBM per device.

v0:
```python
from functools import partial

import jax
import jax.numpy as jnp
from jax import lax
from jax.sharding import PartitionSpec as P

H = 16


EPSILON = 1e-05
MASKED = -1e30


def matmul(left, right):
    return jnp.dot(left, right, preferred_element_type=jnp.float32)


def transposed_left_product(left, right):
    return lax.dot_general(
        left, right, (((0,), (0,)), ((), ())), preferred_element_type=jnp.float32
    )


def matmul_nt(left, right):
    return lax.dot_general(
        left, right, (((1,), (1,)), ((), ())), preferred_element_type=jnp.float32
    )


def vector(weights, number):
    return weights[number].astype(jnp.float32)


def moments(values):
    average = jnp.mean(values, -1, keepdims=True)
    centered = values - average
    variance = jnp.mean(centered * centered, -1, keepdims=True)
    inverse = lax.rsqrt(variance + EPSILON)
    return (centered * inverse, inverse)


def norm_back(grad_out, normed, inverse, gain_vec):
    gain_grad = jnp.sum(grad_out * normed, 0)
    shift_grad = jnp.sum(grad_out, 0)
    scaled = grad_out * gain_vec
    mean_one = jnp.mean(scaled, -1, keepdims=True)
    mean_two = jnp.mean(scaled * normed, -1, keepdims=True)
    return (inverse * (scaled - mean_one - normed * mean_two), gain_grad, shift_grad)


def split_heads(values, head_count):
    return values.reshape(values.shape[0], head_count, values.shape[1] // head_count)


def masked_scores(queries, key_rows, allowed, head_count):
    query_h = split_heads(queries, head_count)
    factor = query_h.shape[2] ** (-0.5)
    scores = (
        jnp.einsum(
            "qhd,khd->hqk",
            query_h,
            split_heads(key_rows, head_count),
            preferred_element_type=jnp.float32,
        )
        * factor
    )
    if allowed is not None:
        scores = jnp.where(allowed, scores, MASKED)
    return scores


def attend_fwd(queries, key_rows, values, allowed, head_count):
    scores = masked_scores(queries, key_rows, allowed, head_count)
    row_max = jnp.max(scores, -1, keepdims=True)
    exponent = jnp.exp(scores - row_max)
    row_total = jnp.sum(exponent, -1, keepdims=True)
    probs_low = (exponent / row_total).astype(jnp.bfloat16)
    attended = jnp.einsum(
        "hqk,khd->qhd",
        probs_low,
        split_heads(values, head_count),
        preferred_element_type=jnp.float32,
    )
    return (attended.reshape(queries.shape[0], queries.shape[1]), row_max + jnp.log(row_total))


def attend_back(grad_attended, queries, key_rows, values, logsum, allowed, head_count):
    factor = (queries.shape[1] // head_count) ** (-0.5)
    probs_all = jnp.exp(masked_scores(queries, key_rows, allowed, head_count) - logsum)
    grad_h = split_heads(grad_attended, head_count)
    grad_probs = jnp.einsum(
        "qhd,khd->hqk", grad_h, split_heads(values, head_count), preferred_element_type=jnp.float32
    )
    grad_values = jnp.einsum(
        "hqk,qhd->khd", probs_all.astype(jnp.bfloat16), grad_h, preferred_element_type=jnp.float32
    )
    grad_scores = (
        probs_all * (grad_probs - jnp.sum(grad_probs * probs_all, -1, keepdims=True))
    ).astype(jnp.bfloat16)
    grad_queries = (
        jnp.einsum(
            "hqk,khd->qhd",
            grad_scores,
            split_heads(key_rows, head_count),
            preferred_element_type=jnp.float32,
        )
        * factor
    )
    grad_keys = (
        jnp.einsum(
            "hqk,qhd->khd",
            grad_scores,
            split_heads(queries, head_count),
            preferred_element_type=jnp.float32,
        )
        * factor
    )
    width = queries.shape[1]
    return (
        grad_queries.reshape(queries.shape[0], width).astype(jnp.bfloat16),
        grad_keys.reshape(key_rows.shape[0], width).astype(jnp.bfloat16),
        grad_values.reshape(key_rows.shape[0], width).astype(jnp.bfloat16),
    )


def collect_weights(shards):
    return (
        lax.all_gather(shards[0], "fsdp", axis=0, tiled=True),
        lax.all_gather(shards[1], "fsdp", axis=0, tiled=True),
        lax.all_gather(shards[2], "fsdp", axis=0, tiled=True),
        lax.all_gather(shards[3], "fsdp", axis=0, tiled=True),
        lax.all_gather(shards[4], "fsdp", axis=0, tiled=True),
        lax.all_gather(shards[5], "fsdp", axis=0, tiled=True),
        lax.all_gather(shards[6], "fsdp", axis=0, tiled=True),
        lax.all_gather(shards[7], "fsdp", axis=0, tiled=True),
        lax.all_gather(shards[8], "fsdp", axis=0, tiled=True),
        lax.all_gather(shards[9], "fsdp", axis=0, tiled=True),
        lax.all_gather(shards[10], "fsdp", axis=0, tiled=True),
        lax.all_gather(shards[11], "fsdp", axis=0, tiled=True),
        lax.all_gather(shards[12], "fsdp", axis=0, tiled=True),
        lax.all_gather(shards[13], "fsdp", axis=0, tiled=True),
        lax.all_gather(shards[14], "fsdp", axis=0, tiled=True),
        lax.all_gather(shards[15], "fsdp", axis=0, tiled=True),
        lax.all_gather(shards[16], "fsdp", axis=0, tiled=True),
        lax.all_gather(shards[17], "fsdp", axis=0, tiled=True),
        lax.all_gather(shards[18], "fsdp", axis=0, tiled=True),
        lax.all_gather(shards[19], "fsdp", axis=0, tiled=True),
        lax.all_gather(shards[20], "fsdp", axis=0, tiled=True),
        lax.all_gather(shards[21], "fsdp", axis=0, tiled=True),
        lax.all_gather(shards[22], "fsdp", axis=0, tiled=True),
        lax.all_gather(shards[23], "fsdp", axis=0, tiled=True),
    )


def reduce_rows(grads):
    return (
        lax.psum_scatter(grads[0], "fsdp", scatter_dimension=0, tiled=True),
        lax.psum_scatter(grads[1], "fsdp", scatter_dimension=0, tiled=True),
        lax.psum_scatter(grads[2], "fsdp", scatter_dimension=0, tiled=True),
        lax.psum_scatter(grads[3], "fsdp", scatter_dimension=0, tiled=True),
        lax.psum_scatter(grads[4], "fsdp", scatter_dimension=0, tiled=True),
        lax.psum_scatter(grads[5], "fsdp", scatter_dimension=0, tiled=True),
        lax.psum_scatter(grads[6], "fsdp", scatter_dimension=0, tiled=True),
        lax.psum_scatter(grads[7], "fsdp", scatter_dimension=0, tiled=True),
        lax.psum_scatter(grads[8], "fsdp", scatter_dimension=0, tiled=True),
        lax.psum_scatter(grads[9], "fsdp", scatter_dimension=0, tiled=True),
        lax.psum_scatter(grads[10], "fsdp", scatter_dimension=0, tiled=True),
        lax.psum_scatter(grads[11], "fsdp", scatter_dimension=0, tiled=True),
        lax.psum_scatter(grads[12], "fsdp", scatter_dimension=0, tiled=True),
        lax.psum_scatter(grads[13], "fsdp", scatter_dimension=0, tiled=True),
        lax.psum_scatter(grads[14], "fsdp", scatter_dimension=0, tiled=True),
        lax.psum_scatter(grads[15], "fsdp", scatter_dimension=0, tiled=True),
        lax.psum_scatter(grads[16], "fsdp", scatter_dimension=0, tiled=True),
        lax.psum_scatter(grads[17], "fsdp", scatter_dimension=0, tiled=True),
        lax.psum_scatter(grads[18], "fsdp", scatter_dimension=0, tiled=True),
        lax.psum_scatter(grads[19], "fsdp", scatter_dimension=0, tiled=True),
        lax.psum_scatter(grads[20], "fsdp", scatter_dimension=0, tiled=True),
        lax.psum_scatter(grads[21], "fsdp", scatter_dimension=0, tiled=True),
        lax.psum_scatter(grads[22], "fsdp", scatter_dimension=0, tiled=True),
        lax.psum_scatter(grads[23], "fsdp", scatter_dimension=0, tiled=True),
    )


def forward_one(weights, rows_in, memory, allowed, head_count):
    normed_one, inverse_one = moments(rows_in)
    first_activation = (normed_one * vector(weights, 18) + vector(weights, 19)).astype(jnp.bfloat16)
    queries = (matmul(first_activation, weights[0]) + vector(weights, 4)).astype(jnp.bfloat16)
    key_rows = matmul(first_activation, weights[1]).astype(jnp.bfloat16)
    values = (matmul(first_activation, weights[2]) + vector(weights, 5)).astype(jnp.bfloat16)
    attended, logsum_one = attend_fwd(queries, key_rows, values, allowed, head_count)
    attended = attended.astype(jnp.bfloat16)
    middle_one = rows_in + (matmul(attended, weights[3]) + vector(weights, 6))
    normed_two, inverse_two = moments(middle_one)
    act_two = (normed_two * vector(weights, 20) + vector(weights, 21)).astype(jnp.bfloat16)
    cross_queries = (matmul(act_two, weights[7]) + vector(weights, 11)).astype(jnp.bfloat16)
    cross_keys = matmul(memory, weights[8]).astype(jnp.bfloat16)
    cross_values = (matmul(memory, weights[9]) + vector(weights, 12)).astype(jnp.bfloat16)
    cross_attended, logsum_two = attend_fwd(
        cross_queries, cross_keys, cross_values, None, head_count
    )
    cross_attended = cross_attended.astype(jnp.bfloat16)
    middle_two = middle_one + (matmul(cross_attended, weights[10]) + vector(weights, 13))
    normed_three, inverse_three = moments(middle_two)
    act_three = (normed_three * vector(weights, 22) + vector(weights, 23)).astype(jnp.bfloat16)
    expanded = matmul(act_three, weights[14]) + vector(weights, 15)
    activated, gelu_back = jax.vjp(partial(jax.nn.gelu, approximate=False), expanded)
    hidden = activated.astype(jnp.bfloat16)
    result = middle_two + (matmul(hidden, weights[16]) + vector(weights, 17))
    kept_state = (
        normed_one,
        inverse_one,
        first_activation,
        queries,
        key_rows,
        values,
        attended,
        logsum_one,
        normed_two,
        inverse_two,
        act_two,
        cross_queries,
        cross_keys,
        cross_values,
        cross_attended,
        logsum_two,
        normed_three,
        inverse_three,
        act_three,
        gelu_back,
        hidden,
        memory,
        allowed,
    )
    return (result.astype(jnp.bfloat16), kept_state)


def backward_one(weights, kept_state, grad_out, head_count):
    (
        normed_one,
        inverse_one,
        first_activation,
        queries,
        key_rows,
        values,
        attended,
        logsum_one,
        normed_two,
        inverse_two,
        act_two,
        cross_queries,
        cross_keys,
        cross_values,
        cross_attended,
        logsum_two,
        normed_three,
        inverse_three,
        act_three,
        gelu_back,
        hidden,
        memory,
        allowed,
    ) = kept_state
    grad_low = grad_out.astype(jnp.bfloat16)
    reduce_grad = transposed_left_product(hidden, grad_low)
    reduceb_grad = jnp.sum(grad_low.astype(jnp.float32), 0)
    grad_expanded = gelu_back(matmul_nt(grad_low, weights[16]))[0].astype(jnp.bfloat16)
    expand_grad = transposed_left_product(act_three, grad_expanded)
    expandb_grad = jnp.sum(grad_expanded.astype(jnp.float32), 0)
    grad_norm, gain_three, shift_three = norm_back(
        matmul_nt(grad_expanded, weights[14]), normed_three, inverse_three, vector(weights, 22)
    )
    grad_middle_two = grad_out + grad_norm
    cross_low = grad_middle_two.astype(jnp.bfloat16)
    cout_grad = transposed_left_product(cross_attended, cross_low)
    coutb_grad = jnp.sum(cross_low.astype(jnp.float32), 0)
    grad_cross = matmul_nt(cross_low, weights[10]).astype(jnp.bfloat16)
    grad_cquery, grad_ckey, grad_cvalue = attend_back(
        grad_cross, cross_queries, cross_keys, cross_values, logsum_two, None, head_count
    )
    cquery_grad = transposed_left_product(act_two, grad_cquery)
    cqueryb_grad = jnp.sum(grad_cquery.astype(jnp.float32), 0)
    ckey_grad = transposed_left_product(memory, grad_ckey)
    cvalue_grad = transposed_left_product(memory, grad_cvalue)
    cvalueb_grad = jnp.sum(grad_cvalue.astype(jnp.float32), 0)
    encoder_grad = matmul_nt(grad_ckey, weights[8]) + matmul_nt(grad_cvalue, weights[9])
    grad_norm, gain_two, shift_two = norm_back(
        matmul_nt(grad_cquery, weights[7]), normed_two, inverse_two, vector(weights, 20)
    )
    grad_middle_one = grad_middle_two + grad_norm
    self_low = grad_middle_one.astype(jnp.bfloat16)
    sout_grad = transposed_left_product(attended, self_low)
    soutb_grad = jnp.sum(self_low.astype(jnp.float32), 0)
    grad_self = matmul_nt(self_low, weights[3]).astype(jnp.bfloat16)
    grad_query, key_gradient, grad_value = attend_back(
        grad_self, queries, key_rows, values, logsum_one, allowed, head_count
    )
    squery_grad = transposed_left_product(first_activation, grad_query)
    squeryb_grad = jnp.sum(grad_query.astype(jnp.float32), 0)
    self_key_gradient = transposed_left_product(first_activation, key_gradient)
    svalue_grad = transposed_left_product(first_activation, grad_value)
    svalueb_grad = jnp.sum(grad_value.astype(jnp.float32), 0)
    grad_act_one = (
        matmul_nt(grad_query, weights[0])
        + matmul_nt(key_gradient, weights[1])
        + matmul_nt(grad_value, weights[2])
    )
    grad_norm, gain_one, shift_one = norm_back(
        grad_act_one, normed_one, inverse_one, vector(weights, 18)
    )
    input_grad = grad_middle_one + grad_norm
    grads = [
        squery_grad,
        self_key_gradient,
        svalue_grad,
        sout_grad,
        squeryb_grad,
        svalueb_grad,
        soutb_grad,
        cquery_grad,
        ckey_grad,
        cvalue_grad,
        cout_grad,
        cqueryb_grad,
        cvalueb_grad,
        coutb_grad,
        expand_grad,
        expandb_grad,
        reduce_grad,
        reduceb_grad,
        gain_one,
        shift_one,
        gain_two,
        shift_two,
        gain_three,
        shift_three,
    ]
    return (input_grad, encoder_grad, grads)


def body(
    decoder_input,
    encoder_out,
    prefix_length,
    output_grad,
    self_query,
    self_key,
    self_value,
    self_output,
    selfquery_bias,
    selfvalue_bias,
    self_attention_output_bias,
    cross_query,
    cross_key,
    cross_value,
    cross_output,
    crossquery_bias,
    crossvalue_bias,
    crossoutput_bias,
    expand_weight,
    expand_bias,
    down_projection_weight,
    reduce_bias,
    selfnorm_gain,
    selfnorm_bias,
    crossnorm_gain,
    crossnorm_bias,
    finalnorm_gain,
    finalnorm_bias,
):
    shards = (
        self_query,
        self_key,
        self_value,
        self_output,
        selfquery_bias,
        selfvalue_bias,
        self_attention_output_bias,
        cross_query,
        cross_key,
        cross_value,
        cross_output,
        crossquery_bias,
        crossvalue_bias,
        crossoutput_bias,
        expand_weight,
        expand_bias,
        down_projection_weight,
        reduce_bias,
        selfnorm_gain,
        selfnorm_bias,
        crossnorm_gain,
        crossnorm_bias,
        finalnorm_gain,
        finalnorm_bias,
    )
    head_count = H
    batches = decoder_input.shape[0]
    seq_rows = decoder_input.shape[1]
    position = jnp.arange(seq_rows, dtype=jnp.int32)
    causal = position[None, :] <= position[:, None]
    outputs = []
    input_grads = []
    encoder_grads = []
    totals = None
    for sample in range(batches):
        weights = collect_weights(shards)
        allowed = causal | (position[None, :] < prefix_length[sample])
        result, kept_state = forward_one(
            weights,
            decoder_input[sample].astype(jnp.float32),
            encoder_out[sample],
            allowed,
            head_count,
        )
        outputs.append(result)
        weights = collect_weights(shards)
        grad_input, grad_encoder, grads = backward_one(
            weights, kept_state, output_grad[sample].astype(jnp.float32), head_count
        )
        input_grads.append(grad_input)
        encoder_grads.append(grad_encoder)
        totals = (
            list(grads)
            if totals is None
            else [earlier + latest for earlier, latest in zip(totals, grads)]
        )
    totals = reduce_rows(totals)
    summed = (
        lax.psum(totals[0].astype(jnp.bfloat16), "replica").astype(jnp.float32),
        lax.psum(totals[1].astype(jnp.bfloat16), "replica").astype(jnp.float32),
        lax.psum(totals[2].astype(jnp.bfloat16), "replica").astype(jnp.float32),
        lax.psum(totals[3].astype(jnp.bfloat16), "replica").astype(jnp.float32),
        lax.psum(totals[4].astype(jnp.bfloat16), "replica").astype(jnp.float32),
        lax.psum(totals[5].astype(jnp.bfloat16), "replica").astype(jnp.float32),
        lax.psum(totals[6].astype(jnp.bfloat16), "replica").astype(jnp.float32),
        lax.psum(totals[7].astype(jnp.bfloat16), "replica").astype(jnp.float32),
        lax.psum(totals[8].astype(jnp.bfloat16), "replica").astype(jnp.float32),
        lax.psum(totals[9].astype(jnp.bfloat16), "replica").astype(jnp.float32),
        lax.psum(totals[10].astype(jnp.bfloat16), "replica").astype(jnp.float32),
        lax.psum(totals[11].astype(jnp.bfloat16), "replica").astype(jnp.float32),
        lax.psum(totals[12].astype(jnp.bfloat16), "replica").astype(jnp.float32),
        lax.psum(totals[13].astype(jnp.bfloat16), "replica").astype(jnp.float32),
        lax.psum(totals[14].astype(jnp.bfloat16), "replica").astype(jnp.float32),
        lax.psum(totals[15].astype(jnp.bfloat16), "replica").astype(jnp.float32),
        lax.psum(totals[16].astype(jnp.bfloat16), "replica").astype(jnp.float32),
        lax.psum(totals[17].astype(jnp.bfloat16), "replica").astype(jnp.float32),
        lax.psum(totals[18].astype(jnp.bfloat16), "replica").astype(jnp.float32),
        lax.psum(totals[19].astype(jnp.bfloat16), "replica").astype(jnp.float32),
        lax.psum(totals[20].astype(jnp.bfloat16), "replica").astype(jnp.float32),
        lax.psum(totals[21].astype(jnp.bfloat16), "replica").astype(jnp.float32),
        lax.psum(totals[22].astype(jnp.bfloat16), "replica").astype(jnp.float32),
        lax.psum(totals[23].astype(jnp.bfloat16), "replica").astype(jnp.float32),
    )
    return (jnp.stack(outputs), jnp.stack(input_grads), jnp.stack(encoder_grads)) + tuple(summed)


def solution(mesh):
    in_specs = (
        P(("replica", "fsdp"), None, None),
        P(("replica", "fsdp"), None, None),
        P(("replica", "fsdp")),
        P(("replica", "fsdp"), None, None),
        P("fsdp", None),
        P("fsdp", None),
        P("fsdp", None),
        P("fsdp", None),
        P("fsdp"),
        P("fsdp"),
        P("fsdp"),
        P("fsdp", None),
        P("fsdp", None),
        P("fsdp", None),
        P("fsdp", None),
        P("fsdp"),
        P("fsdp"),
        P("fsdp"),
        P("fsdp", None),
        P("fsdp"),
        P("fsdp", None),
        P("fsdp"),
        P("fsdp"),
        P("fsdp"),
        P("fsdp"),
        P("fsdp"),
        P("fsdp"),
        P("fsdp"),
    )
    out_specs = (
        P(("replica", "fsdp"), None, None),
        P(("replica", "fsdp"), None, None),
        P(("replica", "fsdp"), None, None),
        P("fsdp", None),
        P("fsdp", None),
        P("fsdp", None),
        P("fsdp", None),
        P("fsdp"),
        P("fsdp"),
        P("fsdp"),
        P("fsdp", None),
        P("fsdp", None),
        P("fsdp", None),
        P("fsdp", None),
        P("fsdp"),
        P("fsdp"),
        P("fsdp"),
        P("fsdp", None),
        P("fsdp"),
        P("fsdp", None),
        P("fsdp"),
        P("fsdp"),
        P("fsdp"),
        P("fsdp"),
        P("fsdp"),
        P("fsdp"),
        P("fsdp"),
    )
    return jax.shard_map(body, mesh=mesh, in_specs=in_specs, out_specs=out_specs, check_vma=False)
```

profile of v0, /device:TPU:0, one launch (start us, length us, event | category | flops | bytes accessed | tf_op | source)
XLA Modules:
  0.0 2119.8 jit_solution(11274777563939490372)
XLA Ops:
  14.9 22.2 %all-gather = bf16[8,1,128]{2,1,0:T(2,128)(2,1)S(1)} all-gather(bf16[1,1,128]{2,1,0:T(2,128)(2,1)S(1)} %bitcast.497), channel_id=1, replica_groups=mesh['replica'=4,'fsdp'=8] {'fsdp'}, dimensions={0}, use_global_device_ids=true | all-gather | bytes 2304 | tf_op jit(solution)/shard_map/all_gather | solution.py:147
  37.1 16.3 all-gather.1
  53.4 18.4 all-gather.3
  89.3 18.4 all-gather.4
  123.9 18.2 all-gather.7
  158.4 18.3 all-gather.5
  193.0 18.3 all-gather.10
  227.5 26.4 %all-gather.12 = bf16[8,1,512]{2,1,0:T(2,128)(2,1)S(1)} all-gather(bf16[1,1,512]{2,1,0:T(2,128)(2,1)S(1)} %reshape.556), channel_id=1, replica_groups=mesh['replica'=4,'fsdp'=8] {'fsdp'}, dimensions={0}, use_global_device_ids=true | all-gather | bytes 9216 | tf_op jit(solution)/shard_map/all_gather | solution.py:144
  290.1 22.0 %all-gather.33.cloned.1.call-done = bf16[1024,1024]{1,0:T(8,128)(2,1)} async-done(((bf16[128,1024]{1,0:T(8,128)(2,1)}), bf16[1024,1024]{1,0:T(8,128)(2,1)}) %all-gather.33.cloned.1.call-update) | async-done | bytes 2097168 | tf_op jit(solution)/shard_map/all_gather | solution.py:138
  316.5 45.6 %all-gather.35.cloned.1.call-done = bf16[1024,1024]{1,0:T(8,128)(2,1)} async-done(((bf16[128,1024]{1,0:T(8,128)(2,1)}), bf16[1024,1024]{1,0:T(8,128)(2,1)}) %all-gather.35.cloned.1.call-update) | async-done | bytes 2097168 | tf_op jit(solution)/shard_map/all_gather | solution.py:136
  424.8 112.8 %all-gather.41.cloned.1.call-done = bf16[1024,4096]{1,0:T(8,128)(2,1)} async-done(((bf16[128,4096]{1,0:T(8,128)(2,1)}), bf16[1024,4096]{1,0:T(8,128)(2,1)}) %all-gather.41.cloned.1.call-update) | async-done | bytes 8388624 | tf_op jit(solution)/shard_map/all_gather | solution.py:143
  537.6 16.8 multiply_convert_fusion.5
  554.5 16.6 multiply_convert_fusion.4
  571.1 91.6 %all-gather.43.cloned.1.call-done = bf16[4096,1024]{1,0:T(8,128)(2,1)} async-done(((bf16[512,1024]{1,0:T(8,128)(2,1)}), bf16[4096,1024]{1,0:T(8,128)(2,1)}) %all-gather.43.cloned.1.call-update) | async-done | bytes 8388624 | tf_op jit(solution)/shard_map/all_gather | solution.py:145
  871.7 17.8 all-gather.13
  900.4 36.7 %all-reduce.14 = (bf16[1024]{0:T(1024)(128)(2,1)S(1)}, bf16[1024]{0:T(1024)(128)(2,1)S(1)}, bf16[1024]{0:T(1024)(128)(2,1)S(1)}, bf16[1024]{0:T(1024)(128)(2,1)S...) all-reduce(f32[1024]{0:T(1024)S(1)} %add.555, ...), channel_id=6, replica_groups=mesh['replica'=4,'fsdp'=8] {'fsdp'}, use_global_device_ids=true, to_apply=%region_46.47.clone | all-reduce | flops 17408 | bytes 104448
  979.6 90.0 %reduce-scatter.15.cloned.1.call-done = f32[128,1024]{1,0:T(8,128)} async-done(((f32[1024,1024]{1,0:T(8,128)}), f32[128,1024]{1,0:T(8,128)}) %reduce-scatter.15.cloned.1.call-update) | async-done | bytes 524304 | tf_op jit(solution)/shard_map/reduce_scatter | solution.py:160
  1071.4 89.4 %reduce-scatter.13.cloned.1.call-done = f32[128,1024]{1,0:T(8,128)} async-done(((f32[1024,1024]{1,0:T(8,128)}), f32[128,1024]{1,0:T(8,128)}) %reduce-scatter.13.cloned.1.call-update) | async-done | bytes 524304 | tf_op jit(solution)/shard_map/reduce_scatter | solution.py:159
  1162.6 89.8 %reduce-scatter.11.cloned.1.call-done = f32[128,1024]{1,0:T(8,128)} async-done(((f32[1024,1024]{1,0:T(8,128)}), f32[128,1024]{1,0:T(8,128)}) %reduce-scatter.11.cloned.1.call-update) | async-done | bytes 524304 | tf_op jit(solution)/shard_map/reduce_scatter | solution.py:158
  1254.2 89.9 %reduce-scatter.23.cloned.1.call-done = f32[128,1024]{0,1:T(8,128)} async-done(((f32[1024,1024]{0,1:T(8,128)}), f32[128,1024]{0,1:T(8,128)}) %reduce-scatter.23.cloned.1.call-update) | async-done | bytes 524304 | tf_op jit(solution)/shard_map/reduce_scatter | solution.py:167
  1345.9 90.8 %reduce-scatter.21.cloned.1.call-done = f32[128,1024]{0,1:T(8,128)} async-done(((f32[1024,1024]{0,1:T(8,128)}), f32[128,1024]{0,1:T(8,128)}) %reduce-scatter.21.cloned.1.call-update) | async-done | bytes 524304 | tf_op jit(solution)/shard_map/reduce_scatter | solution.py:166
  1438.5 284.5 %reduce-scatter.27.cloned.1.call-done = f32[128,4096]{1,0:T(8,128)} async-done(((f32[1024,4096]{1,0:T(8,128)}), f32[128,4096]{1,0:T(8,128)}) %reduce-scatter.27.cloned.1.call-update) | async-done | bytes 2097168 | tf_op jit(solution)/shard_map/reduce_scatter | solution.py:172
  1725.7 283.2 %reduce-scatter.29.cloned.1.call-done = f32[512,1024]{1,0:T(8,128)} async-done(((f32[4096,1024]{1,0:T(8,128)}), f32[512,1024]{1,0:T(8,128)}) %reduce-scatter.29.cloned.1.call-update) | async-done | bytes 2097168 | tf_op jit(solution)/shard_map/reduce_scatter | solution.py:174
  2022.6 77.4 %all-reduce.19.cloned.1.call-done = (bf16[128,1024]{0,1:T(8,128)(2,1)}, bf16[128,1024]{0,1:T(8,128)(2,1)}, bf16[128,1024]{1,0:T(8,128)(2,1)}, bf16[128,1024]{1,0...) async-done(((bf16[128,1024]{0,1:T(8,128)(2,1)}, ...) | async-done | bytes 4194320 | tf_op jit(solution)/shard_map/psum | solution.py:438
  (680 shorter events, 489.8 us)
Async XLA Ops:
  7.4 247.4 %all-gather.27.cloned.1.call-start = ((), (), s32[]{:S(2)}) async-start(), calls=%async_computation.11 | async-start | bytes 2359296 | tf_op jit(solution)/shard_map/all_gather | solution.py:129
  8.1 249.2 %all-gather.29.cloned.1.call-start = ((), (), s32[]{:S(2)}) async-start(), calls=%async_computation.12 | async-start | bytes 2359296 | tf_op jit(solution)/shard_map/all_gather | solution.py:130
  8.8 251.3 %all-gather.25.cloned.1.call-start = ((), (), s32[]{:S(2)}) async-start(), calls=%async_computation.10 | async-start | bytes 2359296 | tf_op jit(solution)/shard_map/all_gather | solution.py:131
  9.6 257.1 %all-gather.31.cloned.1.call-start = ((), (), s32[]{:S(2)}) async-start(), calls=%async_computation.13 | async-start | bytes 2359296 | tf_op jit(solution)/shard_map/all_gather | solution.py:132
  10.2 276.8 %all-gather.37.cloned.1.call-start = ((), (), s32[]{:S(2)}) async-start(), calls=%async_computation.16 | async-start | bytes 2359296 | tf_op jit(solution)/shard_map/all_gather | solution.py:137
  10.7 301.4 %all-gather.33.cloned.1.call-start = ((), (), s32[]{:S(2)}) async-start(), calls=%async_computation.14 | async-start | bytes 2359296 | tf_op jit(solution)/shard_map/all_gather | solution.py:138
  11.3 350.8 %all-gather.35.cloned.1.call-start = ((), (), s32[]{:S(2)}) async-start(), calls=%async_computation.15 | async-start | bytes 2359296 | tf_op jit(solution)/shard_map/all_gather | solution.py:136
  12.1 400.0 %all-gather.39.cloned.1.call-start = ((), (), s32[]{:S(2)}) async-start(), calls=%async_computation.17 | async-start | bytes 2359296 | tf_op jit(solution)/shard_map/all_gather | solution.py:139
  12.8 524.8 %all-gather.41.cloned.1.call-start = ((), (), s32[]{:S(2)}) async-start(), calls=%async_computation.18 | async-start | bytes 9437184 | tf_op jit(solution)/shard_map/all_gather | solution.py:143
  13.6 649.2 %all-gather.43.cloned.1.call-start = ((), (), s32[]{:S(2)}) async-start(), calls=%async_computation.19 | async-start | bytes 9437184 | tf_op jit(solution)/shard_map/all_gather | solution.py:145
  14.1 951.4 %reduce-scatter.25.cloned.1.call-start = ((), (), s32[]{:S(2)}) async-start(), calls=%async_computation.27 | async-start | bytes 4718592 | tf_op jit(solution)/shard_map/reduce_scatter | solution.py:168
  706.2 261.2 %reduce-scatter.19.cloned.1.call-start = ((), (), s32[]{:S(2)}) async-start(), calls=%async_computation.24 | async-start | bytes 4718592 | tf_op jit(solution)/shard_map/reduce_scatter | solution.py:165
  753.3 224.5 %reduce-scatter.17.cloned.1.call-start = ((), (), s32[]{:S(2)}) async-start(), calls=%async_computation.23 | async-start | bytes 4718592 | tf_op jit(solution)/shard_map/reduce_scatter | solution.py:161
  763.9 305.7 %reduce-scatter.15.cloned.1.call-start = ((), (), s32[]{:S(2)}) async-start(), calls=%async_computation.22 | async-start | bytes 4718592 | tf_op jit(solution)/shard_map/reduce_scatter | solution.py:160
  784.3 376.5 %reduce-scatter.13.cloned.1.call-start = ((), (), s32[]{:S(2)}) async-start(), calls=%async_computation.21 | async-start | bytes 4718592 | tf_op jit(solution)/shard_map/reduce_scatter | solution.py:159
  799.0 453.4 %reduce-scatter.11.cloned.1.call-start = ((), (), s32[]{:S(2)}) async-start(), calls=%async_computation.20 | async-start | bytes 4718592 | tf_op jit(solution)/shard_map/reduce_scatter | solution.py:158
  809.8 534.4 %reduce-scatter.23.cloned.1.call-start = ((), (), s32[]{:S(2)}) async-start(), calls=%async_computation.26 | async-start | bytes 4718592 | tf_op jit(solution)/shard_map/reduce_scatter | solution.py:167
  828.6 608.1 %reduce-scatter.21.cloned.1.call-start = ((), (), s32[]{:S(2)}) async-start(), calls=%async_computation.25 | async-start | bytes 4718592 | tf_op jit(solution)/shard_map/reduce_scatter | solution.py:166
  840.2 882.8 %reduce-scatter.27.cloned.1.call-start = ((), (), s32[]{:S(2)}) async-start(), calls=%async_computation.28 | async-start | bytes 18874368 | tf_op jit(solution)/shard_map/reduce_scatter | solution.py:172
  855.1 1153.8 %reduce-scatter.29.cloned.1.call-start = ((), (), s32[]{:S(2)}) async-start(), calls=%async_computation.29 | async-start | bytes 18874368 | tf_op jit(solution)/shard_map/reduce_scatter | solution.py:174
  869.3 1230.7 %all-reduce.19.cloned.1.call-start = ((), (), s32[]{:S(2)}) async-start(), calls=%async_computation.30 | async-start | bytes 8388608 | tf_op jit(solution)/shard_map/psum | solution.py:438
  1725.7 286.0 %copy-start.91 = (bf16[1,256,1024]{2,1,0:T(8,128)(2,1)S(1)}, bf16[1,256,1024]{2,1,0:T(8,128)(2,1)}, u32[]{:S(2)}) copy-start(bf16[1,256,1024]{2,1,0:T(8,128)(2,1)} %fusion.88) | copy-start | bytes 1572868
  1725.7 287.1 %copy-start.63 = (f32[1,256,1024]{2,1,0:T(8,128)S(1)}, f32[1,256,1024]{2,1,0:T(8,128)}, u32[]{:S(2)}) copy-start(f32[1,256,1024]{2,1,0:T(8,128)} %get-tuple-element.190) | copy-start | bytes 3145732
  1725.7 287.1 %copy-start.64 = (f32[1,256,1024]{2,1,0:T(8,128)S(1)}, f32[1,256,1024]{2,1,0:T(8,128)}, u32[]{:S(2)}) copy-start(f32[1,256,1024]{2,1,0:T(8,128)} %get-tuple-element.191) | copy-start | bytes 3145732
  (191 other events, 5450.6 us)
Sparse Core Ops, SparseCore 0:
  10.3 52.0 all-gather.26
  64.5 47.8 all-gather.28
  114.5 47.8 all-gather.24
  164.4 47.8 all-gather.30
  214.3 48.0 all-gather.36
  264.4 47.7 all-gather.32
  314.3 47.7 all-gather.34
  364.2 47.7 all-gather.38
  414.2 123.4 all-gather.40
  539.6 123.0 all-gather.42
  706.3 86.0 reduce-scatter.24
  796.3 87.6 reduce-scatter.18
  887.6 90.1 reduce-scatter.16
  981.8 87.8 reduce-scatter.14
  1073.1 87.6 reduce-scatter.12
  1164.7 87.6 reduce-scatter.10
  1255.9 88.2 reduce-scatter.22
  1348.6 88.0 reduce-scatter.20
  1440.5 282.4 reduce-scatter.26
  1727.1 281.7 reduce-scatter.28
  2013.7 86.2 all-reduce.18
where the time goes:
time: 2120 us
  waiting for transfers between devices  1400 us (66%)
  blocking collectives  298 us (14%)
  matrix products  282 us (13%)
  other arithmetic  70.7 us (3%)
  local copies, waits for them, and re-layouts  50.6 us (2%)
    reduce_scatter x1, waiting for transfers between devices, reduce_rows(): lax.psum_scatter(grads[14], 'fsdp', scatter_dimension=0, tiled=True)  284 us
    reduce_scatter x1, waiting for transfers between devices, reduce_rows(): lax.psum_scatter(grads[16], 'fsdp', scatter_dimension=0, tiled=True)  283 us
    all_gather x1, waiting for transfers between devices, collect_weights(): lax.all_gather(shards[14], 'fsdp', axis=0, tiled=True)  113 us
    all_gather x1, waiting for transfers between devices, collect_weights(): lax.all_gather(shards[16], 'fsdp', axis=0, tiled=True)  91.6 us
    reduce_scatter x1, waiting for transfers between devices, reduce_rows(): lax.psum_scatter(grads[8], 'fsdp', scatter_dimension=0, tiled=True)  90.8 us
    reduce_scatter x1, waiting for transfers between devices, reduce_rows(): lax.psum_scatter(grads[2], 'fsdp', scatter_dimension=0, tiled=True)  90 us
    reduce_scatter x1, waiting for transfers between devices, reduce_rows(): lax.psum_scatter(grads[9], 'fsdp', scatter_dimension=0, tiled=True)  89.9 us
    reduce_scatter x1, waiting for transfers between devices, reduce_rows(): lax.psum_scatter(grads[0], 'fsdp', scatter_dimension=0, tiled=True)  89.8 us
  transfers between devices with their start and end apart: 21, of which 14 were waited for; matrix products, arithmetic and copies ran while one was open for 15% of the time, Pallas kernels for 0%

commit v1 on v0

v1 whole, which is shorter than its diff:
```python
from functools import partial

import jax
import jax.numpy as jnp
import numpy as np
from jax import lax
from jax.experimental import pallas as pl
from jax.experimental.pallas import tpu as pltpu
from jax.sharding import PartitionSpec as P

H = 16
EPSILON = 1e-05
MASKED = -1e30
BF = jnp.bfloat16
F32 = jnp.float32


class Place:
    def __init__(self, groups, rows):
        self.groups = groups
        self.rows = rows
        self.ring = rows // 2
        rep = lax.axis_index("replica")
        row = lax.axis_index("fsdp")
        self.c = lax.rem(rep, 2)
        self.x = lax.div(rep, 2)
        self.y = lax.rem(row, 2)
        self.z = lax.div(row, 2)

    def core(self, v):
        return lax.ppermute(v, "replica", [(i, i ^ 1) for i in range(self.groups)])

    def across(self, v):
        return lax.ppermute(v, "replica", [(i, i ^ 2) for i in range(self.groups)])

    def pair(self, v):
        return lax.ppermute(v, "fsdp", [(i, i ^ 1) for i in range(self.rows)])

    def next(self, v):
        return lax.ppermute(v, "fsdp", [(i, (i + 2) % self.rows) for i in range(self.rows)])

    def ring_members(self):
        return [[2 * k + side for k in range(self.ring)] for side in range(2)]


def at(v, i, axis=0):
    return lax.dynamic_index_in_dim(v, i, axis, keepdims=False)


class Lane:
    def __init__(self, width):
        self.width = width
        self.past = []

    def __call__(self, send, v):
        if len(self.past) >= self.width:
            v, _ = lax.optimization_barrier((v, self.past[-self.width]))
        got = send(v)
        self.past.append(got)
        return got


def ring_gather(place, piece):
    if place.ring <= 4:
        copies = jnp.broadcast_to(piece[None], (place.ring,) + piece.shape)
        return lax.all_to_all(copies, "fsdp", 0, 0, axis_index_groups=place.ring_members())
    return lax.all_gather(piece, "fsdp", axis_index_groups=place.ring_members())


def order_kernel(ring, split, mine, theirs, out, sems):
    rep = lax.axis_index("replica")
    c, x = lax.rem(rep, 2), lax.div(rep, 2)
    y = lax.rem(lax.axis_index("fsdp"), 2)
    copies = []
    for dc, block in enumerate((mine, theirs)):
        cc = 1 - c if dc else c
        for dx in range(2 if split else 1):
            for dy in range(2):
                yy = 1 - y if dy else y
                for z in range(ring):
                    if split:
                        xx = 1 - x if dx else x
                        src, dst = block.at[dx, dy, z], out.at[z, yy, xx, cc]
                    else:
                        src, dst = block.at[dy, z], out.at[z, yy, cc]
                    copies.append(pltpu.make_async_copy(src, dst, sems.at[len(copies)]))
    for copy in copies:
        copy.start()
    for copy in copies:
        copy.wait()


def in_order(place, split, mine, theirs):
    ring, rows, n = mine.shape[-3:]
    dims = (ring, 2, 2, 2) if split else (ring, 2, 2)
    if rows % 16 == 0:
        count = 2 * mine.size // (rows * n)
        out = pl.pallas_call(
            partial(order_kernel, ring, split),
            out_shape=jax.ShapeDtypeStruct(dims + (rows, n), mine.dtype),
            in_specs=[pl.BlockSpec(memory_space=pl.ANY)] * 2,
            out_specs=pl.BlockSpec(memory_space=pltpu.VMEM),
            scratch_shapes=[pltpu.SemaphoreType.DMA((count,))],
            cost_estimate=pl.CostEstimate(
                flops=0, transcendentals=0, bytes_accessed=4 * count * rows * n
            ),
            name="order",
        )(mine, theirs)
    else:
        both = jnp.stack([mine, theirs])
        at_c = (place.c, 1 - place.c)
        both = jnp.stack([at(both, i, 0) for i in at_c])
        if split:
            both = jnp.stack([at(both, i, 1) for i in (place.x, 1 - place.x)], 1)
        both = jnp.stack([at(both, i, both.ndim - 4) for i in (place.y, 1 - place.y)], both.ndim - 4)
        out = jnp.transpose(both, (3, 2, 1, 0, 4, 5) if split else (2, 1, 0, 3, 4))
    return out.reshape(-1, n)


class Gather:
    def __init__(self, place, lane, ring_lane, shard, split):
        self.place, self.lane, self.ring_lane, self.split = place, lane, ring_lane, split
        m, n = shard.shape
        if split:
            self.v = at(shard.reshape(4, m // 4, n), 2 * place.x + place.c)
        else:
            self.v = at(shard.reshape(2, m // 2, n), place.c)
        self.steps = [self.ring, self.pair] + ([self.across] if split else []) + [self.core]

    def ring(self):
        self.v = self.ring_lane(partial(ring_gather, self.place), self.v)

    def pair(self):
        self.v = jnp.stack([self.v, self.lane(self.place.pair, self.v)])

    def across(self):
        self.v = jnp.stack([self.v, self.lane(self.place.across, self.v)])

    def core(self):
        self.v = in_order(self.place, self.split, self.v, self.lane(self.place.core, self.v))


def run_steps(units):
    last = max(i + len(u.steps) for i, u in enumerate(units))
    for t in range(last):
        for i, u in enumerate(units):
            if 0 <= t - i < len(u.steps):
                u.steps[t - i]()


def gather_vectors(place, packed):
    a = ring_gather(place, packed)
    b = place.pair(a)
    both = jnp.stack([jnp.where(place.y == 0, a, b), jnp.where(place.y == 0, b, a)], 1)
    return both.reshape((place.rows,) + packed.shape)


def product_t(left, right):
    return lax.dot_general(
        left, right, (((0,), (0,)), ((), ())), preferred_element_type=F32
    )


def columns(v, k, i):
    w = v.shape[1] // k
    return lax.dynamic_slice(v, (0, i * w), (v.shape[0], w))


def join2(own, other, bit):
    first = jnp.where(bit == 0, own, other)
    second = jnp.where(bit == 0, other, own)
    return jnp.concatenate([first, second], -1)


def ring_sum(place, parts):
    if place.ring <= 4:
        came = lax.all_to_all(parts, "fsdp", 0, 0, axis_index_groups=place.ring_members())
        return jnp.sum(came.astype(F32), 0).astype(BF)
    return lax.psum_scatter(
        parts, "fsdp", scatter_dimension=0, axis_index_groups=place.ring_members()
    )


class Scatter:
    def __init__(self, place, lane, ring_lane, left, right, split):
        self.place, self.lane, self.ring_lane, self.split = place, lane, ring_lane, split
        self.left, self.right = left, right
        self.steps = [self.core] + ([self.across] if split else []) + [self.pair, self.ring]

    def core(self):
        c = self.place.c
        away = product_t(self.left, columns(self.right, 2, 1 - c)).astype(BF)
        self.right = columns(self.right, 2, c)
        self.came = self.lane(self.place.core, away)

    def across(self):
        x = self.place.x
        away = product_t(self.left, columns(self.right, 2, 1 - x))
        away = (away + columns(self.came, 2, 1 - x).astype(F32)).astype(BF)
        self.right, self.came = columns(self.right, 2, x), columns(self.came, 2, x)
        self.came_x = self.lane(self.place.across, away)

    def pair(self):
        part = product_t(self.left, self.right) + self.came.astype(F32)
        if self.split:
            part = part + self.came_x.astype(F32)
        part = part.astype(BF)
        part = part.reshape(self.place.ring, 2, -1, part.shape[1])
        y = self.place.y
        came = self.lane(self.place.pair, at(part, 1 - y, 1))
        self.kept = (at(part, y, 1).astype(F32) + came.astype(F32)).astype(BF)

    def ring(self):
        self.own = self.ring_lane(partial(ring_sum, self.place), self.kept)


def finish(place, lane, units):
    flat = [u.own.reshape(-1, 128) for u in units]
    sizes = [f.shape[0] for f in flat]
    own = jnp.concatenate(flat)
    came = lane(place.across, own)
    pieces, at_row = [], 0
    for u, size in zip(units, sizes):
        mine, other = own[at_row : at_row + size], came[at_row : at_row + size]
        at_row += size
        mine, other = mine.reshape(u.own.shape), other.reshape(u.own.shape)
        if u.split:
            pieces.append(join2(mine, other, place.x))
        else:
            pieces.append((mine.astype(F32) + other.astype(F32)).astype(BF))
    own = jnp.concatenate([p.reshape(-1, 128) for p in pieces])
    came = lane(place.core, own)
    out, at_row = [], 0
    for p in pieces:
        size = p.size // 128
        out.append(join2(p, came[at_row : at_row + size].reshape(p.shape), place.c).astype(F32))
        at_row += size
    return out


def scatter_vectors(place, lane, ring_lane, v):
    own = v.astype(BF)
    own = (own.astype(F32) + lane(place.core, own).astype(F32)).astype(BF)
    own = (own.astype(F32) + lane(place.across, own).astype(F32)).astype(BF)
    own = own.reshape((place.ring, 2) + own.shape[1:])
    came = lane(place.pair, at(own, 1 - place.y, 1))
    own = (at(own, place.y, 1).astype(F32) + came.astype(F32)).astype(BF)
    return ring_lane(partial(ring_sum, place), own).astype(F32)


PAIR = 128


def half_masks(rows):
    lane = lax.broadcasted_iota(jnp.int32, (rows, PAIR), 1)
    return (lane < PAIR // 2, lane >= PAIR // 2)


def dot_nt(a, b):
    return lax.dot_general(a, b, (((1,), (1,)), ((), ())), preferred_element_type=F32)


def attend_kernel(masked, scale, prefix_ref, q_ref, k_ref, v_ref, o_ref, p_ref):
    rows, keys = q_ref.shape[0], k_ref.shape[0]
    masks = half_masks(rows)
    if masked:
        i = lax.broadcasted_iota(jnp.int32, (rows, keys), 0)
        j = lax.broadcasted_iota(jnp.int32, (rows, keys), 1)
        allowed = (j <= i) | (j < prefix_ref[pl.program_id(0)])
    for pair in range(q_ref.shape[1] // PAIR):
        lanes = slice(pair * PAIR, (pair + 1) * PAIR)
        q, k, v = q_ref[:, lanes], k_ref[:, lanes], v_ref[:, lanes]
        both = []
        for h in range(2):
            s = dot_nt(jnp.where(masks[h], q, jnp.zeros_like(q)), k)
            if masked:
                s = jnp.where(allowed, s, MASKED)
            e = jnp.exp((s - jnp.max(s, -1, keepdims=True)) * scale)
            p = (e * (1.0 / jnp.sum(e, -1, keepdims=True))).astype(BF)
            p_ref[2 * pair + h] = p
            both.append(jnp.dot(p, v, preferred_element_type=F32))
        o_ref[:, lanes] = jnp.where(masks[0], both[0], both[1]).astype(BF)


def attend(q, k, v, prefix, batch, masked, group=4):
    rows, keys, d = q.shape[0] // batch, k.shape[0] // batch, q.shape[1]
    wide = group * d // H
    spec = lambda n: pl.BlockSpec((n, wide), lambda b, g, *_: (b, g))
    return pl.pallas_call(
        partial(attend_kernel, masked, (d // H) ** -0.5),
        grid_spec=pltpu.PrefetchScalarGridSpec(
            num_scalar_prefetch=1,
            grid=(batch, H // group),
            in_specs=[spec(rows), spec(keys), spec(keys)],
            out_specs=[
                spec(rows),
                pl.BlockSpec((None, group, rows, keys), lambda b, g, *_: (b, g, 0, 0)),
            ],
        ),
        out_shape=[
            jax.ShapeDtypeStruct(q.shape, BF),
            jax.ShapeDtypeStruct((batch, H, rows, keys), BF),
        ],
        compiler_params=pltpu.CompilerParams(vmem_limit_bytes=40 * 2**20),
        cost_estimate=pl.CostEstimate(
            flops=16 * q.size * keys,
            transcendentals=batch * H * rows * keys,
            bytes_accessed=4 * q.size + 4 * k.size + 2 * batch * H * rows * keys,
        ),
        name="attend",
    )(prefix, q, k, v)


def attend_back_kernel(scale, do_ref, q_ref, k_ref, v_ref, p_ref, dq_ref, dk_ref, dv_ref):
    rows = q_ref.shape[0]
    half = PAIR // 2
    masks = half_masks(rows)
    for pair in range(q_ref.shape[1] // PAIR):
        lanes = slice(pair * PAIR, (pair + 1) * PAIR)
        do, q, k, v = do_ref[:, lanes], q_ref[:, lanes], k_ref[:, lanes], v_ref[:, lanes]
        do_t, q_t = do.T, q.T
        dq, dk_t, dv_t = [], [], []
        for h in range(2):
            p = p_ref[2 * pair + h]
            dp = dot_nt(jnp.where(masks[h], do, jnp.zeros_like(do)), v)
            pf = p.astype(F32)
            ds = (pf * (dp - jnp.sum(dp * pf, -1, keepdims=True))).astype(BF)
            dq.append(jnp.dot(ds, k, preferred_element_type=F32))
            part = slice(h * half, (h + 1) * half)
            dk_t.append(jnp.dot(q_t[part], ds, preferred_element_type=F32))
            dv_t.append(jnp.dot(do_t[part], p, preferred_element_type=F32))
        dq_ref[:, lanes] = (jnp.where(masks[0], dq[0], dq[1]) * scale).astype(BF)
        dk_ref[:, lanes] = (jnp.concatenate(dk_t, 0) * scale).astype(BF).T
        dv_ref[:, lanes] = jnp.concatenate(dv_t, 0).astype(BF).T


def attend_back(do, q, k, v, p, batch, group=4):
    rows, keys, d = q.shape[0] // batch, k.shape[0] // batch, q.shape[1]
    wide = group * d // H
    spec = lambda n: pl.BlockSpec((n, wide), lambda b, g: (b, g))
    return pl.pallas_call(
        partial(attend_back_kernel, (d // H) ** -0.5),
        grid=(batch, H // group),
        in_specs=[
            spec(rows), spec(rows), spec(keys), spec(keys),
            pl.BlockSpec((None, group, rows, keys), lambda b, g: (b, g, 0, 0)),
        ],
        out_specs=[spec(rows), spec(keys), spec(keys)],
        out_shape=[
            jax.ShapeDtypeStruct(q.shape, BF),
            jax.ShapeDtypeStruct(k.shape, BF),
            jax.ShapeDtypeStruct(v.shape, BF),
        ],
        compiler_params=pltpu.CompilerParams(vmem_limit_bytes=40 * 2**20),
        cost_estimate=pl.CostEstimate(
            flops=32 * q.size * keys,
            transcendentals=0,
            bytes_accessed=6 * q.size + 8 * k.size + 2 * batch * H * rows * keys,
        ),
        name="attend_back",
    )(do, q, k, v, p)


def product(left, right):
    return jnp.dot(left, right, preferred_element_type=F32)


def product_nt(left, right):
    return lax.dot_general(
        left, right, (((1,), (1,)), ((), ())), preferred_element_type=F32
    )


def moments(values):
    average = jnp.mean(values, -1, keepdims=True)
    centered = values - average
    variance = jnp.mean(centered * centered, -1, keepdims=True)
    inverse = lax.rsqrt(variance + EPSILON)
    return (centered * inverse, inverse)


def norm_back(grad_out, normed, inverse, gain_vec):
    gain_grad = jnp.sum(grad_out * normed, 0)
    shift_grad = jnp.sum(grad_out, 0)
    scaled = grad_out * gain_vec
    mean_one = jnp.mean(scaled, -1, keepdims=True)
    mean_two = jnp.mean(scaled * normed, -1, keepdims=True)
    return (inverse * (scaled - mean_one - normed * mean_two), gain_grad, shift_grad)


def gelu_both(u):
    cdf = 0.5 * (1.0 + lax.erf(u * np.float32(0.5**0.5)))
    pdf = jnp.exp(-0.5 * u * u) * np.float32((2 * np.pi) ** -0.5)
    return (u * cdf).astype(BF), (cdf + u * pdf).astype(BF)


def body(
    groups,
    rows,
    decoder_input,
    encoder_out,
    prefix_length,
    output_grad,
    self_query,
    self_key,
    self_value,
    self_output,
    selfquery_bias,
    selfvalue_bias,
    self_attention_output_bias,
    cross_query,
    cross_key,
    cross_value,
    cross_output,
    crossquery_bias,
    crossvalue_bias,
    crossoutput_bias,
    expand_weight,
    expand_bias,
    down_projection_weight,
    reduce_bias,
    selfnorm_gain,
    selfnorm_bias,
    crossnorm_gain,
    crossnorm_bias,
    finalnorm_gain,
    finalnorm_bias,
):
    place = Place(groups, rows)
    batch, seq, d = decoder_input.shape
    m = self_query.shape[0]
    ff = expand_weight.shape[1]
    fl = ff // rows // 2
    k4 = ff // d

    small = [
        selfnorm_gain, selfnorm_bias, selfquery_bias, selfvalue_bias, self_attention_output_bias,
        crossnorm_gain, crossnorm_bias, crossquery_bias, crossvalue_bias, crossoutput_bias,
        finalnorm_gain, finalnorm_bias, reduce_bias,
    ]
    packed = jnp.concatenate([jnp.stack(small), expand_bias.reshape(k4, m)])
    vecs = gather_vectors(place, packed).astype(F32)
    (g1, b1, bq, bv, bo, g2, b2, bcq, bcv, bco, g3, b3, br) = [
        vecs[:, i].reshape(d) for i in range(13)
    ]
    be = vecs[:, 13:].reshape(rows, 2, fl)

    expand_halves = [
        expand_weight.reshape(m, rows, 2, fl)[:, :, h].reshape(m, rows * fl) for h in range(2)
    ]
    down_halves = [down_projection_weight[h * fl : (h + 1) * fl] for h in range(2)]

    lane, ring_lane = Lane(4), Lane(2)
    gathers = [
        Gather(place, lane, ring_lane, shard, split)
        for shard, split in (
            (jnp.concatenate([self_query, self_key], 1), True),
            (self_value, False),
            (jnp.concatenate([cross_key, cross_value], 1), True),
            (self_output, False),
            (jnp.concatenate([cross_query, cross_output], 1), True),
            (expand_halves[0], True),
            (expand_halves[1], True),
            (down_halves[0], False),
            (down_halves[1], True),
        )
    ]
    run_steps(gathers)
    w_qk, w_v, w_ckv, w_o, w_cqo, *w_ff = [u.v for u in gathers]
    w_e, w_d = w_ff[:2], w_ff[2:]

    x = decoder_input.reshape(batch * seq, d).astype(F32)
    e = encoder_out.reshape(-1, d)
    dy = output_grad.reshape(batch * seq, d)

    n1, i1 = moments(x)
    act1 = (n1 * g1 + b1).astype(BF)
    qk = product(act1, w_qk)
    q = (qk[:, :d] + bq).astype(BF)
    k = qk[:, d:].astype(BF)
    v = (product(act1, w_v) + bv).astype(BF)
    o, p = attend(q, k, v, prefix_length, batch, True)
    mid1 = x + (product(o, w_o) + bo)
    n2, i2 = moments(mid1)
    act2 = (n2 * g2 + b2).astype(BF)
    w_cq, w_co = w_cqo[:, :d], w_cqo[:, d:]
    cq = (product(act2, w_cq) + bcq).astype(BF)
    ckv = product(e, w_ckv)
    ck = ckv[:, :d].astype(BF)
    cv = (ckv[:, d:] + bcv).astype(BF)
    co, cp = attend(cq, ck, cv, prefix_length, batch, False)
    mid2 = mid1 + (product(co, w_co) + bco)
    n3, i3 = moments(mid2)
    act3 = (n3 * g3 + b3).astype(BF)
    hidden, slope = [], []
    for h in range(2):
        hid, slo = gelu_both(product(act3, w_e[h]) + be[:, h].reshape(-1))
        hidden.append(hid)
        slope.append(slo)
    layer_out = (mid2 + (product(hidden[0], w_d[0]) + product(hidden[1], w_d[1]) + br)).astype(BF)

    scatter = partial(Scatter, place, lane, ring_lane)
    dyf = dy.astype(F32)
    g_down = [scatter(hidden[0], dy, True), scatter(hidden[1], dy, False)]
    dexp = [(product_nt(dy, w_d[h]) * slope[h].astype(F32)).astype(BF) for h in range(2)]
    g_exp = [scatter(act3, dexp[0], True), scatter(act3, dexp[1], False)]
    dact3 = product_nt(dexp[0], w_e[0]) + product_nt(dexp[1], w_e[1])
    dn, gg3, gb3 = norm_back(dact3, n3, i3, g3)
    dmid2 = dyf + dn
    dcross = dmid2.astype(BF)
    g_co = scatter(co, dcross, True)
    dco = product_nt(dcross, w_co).astype(BF)
    dcq, dck, dcv = attend_back(dco, cq, ck, cv, cp, batch)
    g_ck = scatter(e, dck, True)
    g_cv = scatter(e, dcv, False)
    g_cq = scatter(act2, dcq, False)
    encoder_grad = product_nt(jnp.concatenate([dck, dcv], 1), w_ckv)
    dn, gg2, gb2 = norm_back(product_nt(dcq, w_cq), n2, i2, g2)
    dmid1 = dmid2 + dn
    dself = dmid1.astype(BF)
    g_so = scatter(o, dself, True)
    dao = product_nt(dself, w_o).astype(BF)
    dq, dk, dv = attend_back(dao, q, k, v, p, batch)
    g_sv = scatter(act1, dv, False)
    g_sq = scatter(act1, dq, True)
    g_sk = scatter(act1, dk, True)
    dact1 = product_nt(jnp.concatenate([dq, dk], 1), w_qk) + product_nt(dv, w_v)
    dn, gg1, gb1 = norm_back(dact1, n1, i1, g1)
    input_grad = dmid1 + dn

    def column_sum(t):
        return jnp.sum(t.astype(F32), 0)

    dbe = jnp.stack([column_sum(t).reshape(rows, fl) for t in dexp], 1).reshape(rows, k4, m)
    early = [
        gg2, gb2, column_sum(dcq), column_sum(dcv), column_sum(dcross),
        gg3, gb3, column_sum(dy), column_sum(dself),
    ]
    early = jnp.concatenate([jnp.stack([t.reshape(rows, m) for t in early], 1), dbe], 1)
    late = [gg1, gb1, column_sum(dq), column_sum(dv)]
    late = jnp.stack([t.reshape(rows, m) for t in late], 1)

    first = g_down + g_exp + [g_co, g_cv, g_ck, g_cq, g_so]
    second = [g_sv, g_sq, g_sk]
    run_steps(first + second)
    early = scatter_vectors(place, lane, ring_lane, early)
    (*g_ff, g_co, g_cv, g_ck, g_cq, g_so) = finish(place, lane, first)
    g_down, g_exp = g_ff[:2], g_ff[2:]
    late = scatter_vectors(place, lane, ring_lane, late)
    g_sv, g_sq, g_sk = finish(place, lane, second)

    g_exp = jnp.stack([t.reshape(m, rows, fl) for t in g_exp], 2).reshape(m, ff)
    g_down = jnp.concatenate(g_down, 0)
    return (
        layer_out.reshape(batch, seq, d),
        input_grad.reshape(batch, seq, d),
        encoder_grad.reshape(encoder_out.shape),
        g_sq, g_sk, g_sv, g_so,
        late[2], late[3], early[8],
        g_cq, g_ck, g_cv, g_co,
        early[2], early[3], early[4],
        g_exp, early[9:].reshape(-1), g_down, early[7],
        late[0], late[1], early[0], early[1], early[5], early[6],
    )


def solution(mesh):
    groups, rows = mesh.shape["replica"], mesh.shape["fsdp"]
    data = P(("replica", "fsdp"), None, None)
    mat, vec = P("fsdp", None), P("fsdp")
    weights = (
        (mat,) * 4 + (vec,) * 3 + (mat,) * 4 + (vec,) * 3 + (mat, vec, mat, vec) + (vec,) * 6
    )
    return jax.shard_map(
        partial(body, groups, rows),
        mesh=mesh,
        in_specs=(data, data, P(("replica", "fsdp")), data) + weights,
        out_specs=(data, data, data) + weights,
        check_vma=False,
    )
```

time: 2120 us -> 942 us (0.44)
  waiting for transfers between devices: 1400 us -> 193 us
  blocking collectives: 298 us -> 0 us
  starting transfers between devices: 1.59 us -> 156 us
  local copies, waits for them, and re-layouts: 50.6 us -> 169 us
  matrix products: 282 us -> 166 us
  Pallas kernels: 0 us -> 96.6 us
  other arithmetic: 70.7 us -> 144 us
    reduce_scatter x10 -> x0, waiting for transfers between devices: 1030 us -> none  [the longest x1 284 us: reduce_rows(): lax.psum_scatter(grads[14], 'fsdp', scatter_dimension=0, tiled=True)]
    all_gather x10 -> x0, waiting for transfers between devices: 288 us -> none  [the longest x1 113 us: collect_weights(): lax.all_gather(shards[14], 'fsdp', axis=0, tiled=True)]
    all_gather x14 -> x0, blocking collectives: 255 us -> none  [the longest x1 26.4 us: collect_weights(): lax.all_gather(shards[15], 'fsdp', axis=0, tiled=True)]
    ppermute x0 -> x66, waiting for transfers between devices: none -> 135 us  [the longest x17 79.5 us: across(): return lax.ppermute(v, 'replica', [(i, i ^ 2) for i in range(self.groups)])]
    dot_general x84 -> x51, matrix products: 282 us -> 166 us  [the longest x31 79.7 us: product_t(): lax.dot_general(left, right, (((0,), (0,)), ((), ())), preferred_element_...]
    all_to_all x0 -> x24, starting transfers between devices: none -> 111 us  [the longest x14 65 us: ring_sum(): lax.all_to_all(parts, 'fsdp', 0, 0, axis_index_groups=place.ring_members())]
    pallas_call x0 -> x13, Pallas kernels: none -> 96.6 us  [the longest x9 37.3 us: in_order(): pl.pallas_call(partial(order_kernel, ring, split), out_shape=jax.ShapeDty...]
    psum x1 -> x0, waiting for transfers between devices: 77.4 us -> none  [body(): lax.psum(totals[8].astype(jnp.bfloat16), 'replica').astype(jnp.float32)]
  transfers between devices with their start and end apart: 21 -> 90, of which waited for: 14 -> 30; matrix products, arithmetic and copies ran while one was open for 15% -> 44% of each run, Pallas kernels for 0% -> 10%
where the time goes in v1:
time: 942 us; the launch traced here: 928 us
  waiting for transfers between devices  193 us (20%)
  local copies, waits for them, and re-layouts  169 us (18%)
  matrix products  166 us (18%)
  starting transfers between devices  156 us (17%)
  other arithmetic  144 us (15%)
  Pallas kernels  96.6 us (10%)
    dot_general x31, matrix products, product_t(): lax.dot_general(left, right, (((0,), (0,)), ((), ())), preferred_element_...  79.7 us
    ppermute x17, waiting for transfers between devices, across(): return lax.ppermute(v, 'replica', [(i, i ^ 2) for i in range(self.groups)])  79.5 us
    all_to_all x14, starting transfers between devices, ring_sum(): lax.all_to_all(parts, 'fsdp', 0, 0, axis_index_groups=place.ring_members())  65 us
    ppermute x24, waiting for transfers between devices, pair(): return lax.ppermute(v, 'fsdp', [(i, i ^ 1) for i in range(self.rows)])  55.5 us
    unnamed x392, local copies, waits for them, and re-layouts  49.6 us
    dot_general x10, matrix products, product(): return jnp.dot(left, right, preferred_element_type=F32)  48.9 us
    all_to_all x10, starting transfers between devices, ring_gather(): lax.all_to_all(copies, 'fsdp', 0, 0, axis_index_groups=place.ring_members())  45.5 us
    dot_general x10, matrix products, product_nt(): lax.dot_general(left, right, (((1,), (1,)), ((), ())), preferred_element_...  37.8 us
  transfers between devices with their start and end apart: 90, of which 30 were waited for; matrix products, arithmetic and copies ran while one was open for 44% of the time, Pallas kernels for 10%

profile of v1, /device:TPU:0, one launch (start us, length us, event | category | flops | bytes accessed | tf_op | source)
XLA Modules:
  0.0 928.4 jit_solution(10790547031150937713)
XLA Ops:
  3.8 6.3 all-to-all-start
  25.6 8.5 all-to-all-done.1
  39.1 7.0 slice_reduce_fusion.1
  64.2 7.9 all-to-all-done.4
  128.1 8.2 all-to-all-done.6
  176.1 10.3 %attend.2 = (bf16[512,1024]{1,0:T(8,128)(2,1)S(1)}, bf16[2,16,256,256]{3,2,1,0:T(8,128)(2,1)S(1)}) custom-call(s32[2]{0:T(128)S(1)} %copy-done.16, bf16[512,1024]{1,0:T(8,128)(2,1)S(1)} %fusion.13.q_ref, bf16[512,1024]{1,0:T(8,128)(2,1)S(1)} %slice.383.k_ref, bf16[512,1024]{1,0:T(8,128)(2,1)S(1)} %copy-done.25), custom_call_target="tpu_custom_call" | custom-call | flops 2147483648 | bytes 8388608 | tf_op jit(solution)/shard_map/attend/pallas_call | solution.py:289
  202.3 8.9 convolution_bitcast_fusion
  228.5 17.1 %collective-permute-done.15 = bf16[2,4,32,2048]{3,2,1,0:T(8,128)(2,1)S(1)} collective-permute-done((bf16[2,4,32,2048]{3,2,1,0:T(8,128)(2,1)S(1)}, bf16[2,4,32,2048]{3,2,1,0:T(8,128)(2,1)S(1)}, u32[]{:S(2)}, u32[]{:S(2)}) %collective-permute-start.15) | collective-permute-done | bytes 1048608 | tf_op jit(solution)/shard_map/ppermute | solution.py:34
  262.9 18.1 %attend.3 = (bf16[512,1024]{1,0:T(8,128)(2,1)S(1)}, bf16[2,16,256,512]{3,2,1,0:T(8,128)(2,1)}) custom-call(s32[2]{0:T(128)S(1)} %copy-done.16, bf16[512,1024]{1,0:T(8,128)(2,1)S(1)} %add_convert_fusion.10.q_ref, bf16[1024,1024]{1,0:T(8,128)(2,1)S(1)} %copy-done.4, bf16[1024,1024]{1,0:T(8,128)(2,1)S(1)} %copy-done.6), custom_call_target="tpu_custom_call" | custom-call | flops 4294967296 | bytes 14680064 | tf_op jit(solution)/shard_map/attend/pallas_call | solution.py:289
  289.9 11.0 %collective-permute-done.22 = bf16[4,64,1024]{2,1,0:T(8,128)(2,1)S(1)} collective-permute-done((bf16[4,64,1024]{2,1,0:T(8,128)(2,1)}, bf16[4,64,1024]{2,1,0:T(8,128)(2,1)S(1)}, u32[]{:S(2)}, u32[]{:S(2)}) %collective-permute-start.22) | collective-permute-done | bytes 524320 | tf_op jit(solution)/shard_map/ppermute | solution.py:37
  312.5 7.2 multiply_convert_fusion.1
  322.3 6.2 collective-permute-done.23
  335.8 7.1 multiply_convert_fusion
  350.3 7.4 fusion.213
  366.5 6.6 fusion.215
  389.5 17.7 %attend_back.2 = (bf16[512,1024]{1,0:T(8,128)(2,1)S(1)}, bf16[1024,1024]{1,0:T(8,128)(2,1)S(1)}, bf16[1024,1024]{1,0:T(8,128)(2,1)S(1)}) custom-call(bf16[512,1024]{1,0:T(8,128)(2,1)S(1)} %fusion.50.do_ref, bf16[512,1024]{1,0:T(8,128)(2,1)S(1)} %add_convert_fusion.10.q_ref, bf16[1024,1024]{1,0:T(8,128)(2,1)S(1)} %copy-done.5, ...), custom_call_target="tpu_custom_call" | custom-call | flops 8589934592 | bytes 19922944 | tf_op jit(solution)/shard_map/attend_back/pallas_call | solution.py:341
  417.8 13.2 %attend_back.3 = (bf16[512,1024]{1,0:T(8,128)(2,1)S(1)}, bf16[512,1024]{1,0:T(8,128)(2,1)S(1)}, bf16[512,1024]{1,0:T(8,128)(2,1)S(1)}) custom-call(bf16[512,1024]{1,0:T(8,128)(2,1)S(1)} %convolution_convert_fusion.6.do_ref, bf16[512,1024]{1,0:T(8,128)(2,1)S(1)} %copy-done.15, bf16[512,1024]{1,0:T(8,128)(2,1)S(1)} %copy-done.13, ...), custom_call_target="tpu_custom_call" | custom-call | flops 4294967296 | bytes 11534336 | tf_op jit(solution)/shard_map/attend_back/pallas_call | solution.py:341
  443.1 6.5 fusion.218
  460.7 16.9 %collective-permute-done.26 = bf16[2048,256]{1,0:T(8,128)(2,1)S(1)} collective-permute-done((bf16[2048,256]{1,0:T(8,128)(2,1)S(1)}, bf16[2048,256]{1,0:T(8,128)(2,1)S(1)}, u32[]{:S(2)}, u32[]{:S(2)}) %collective-permute-start.26) | collective-permute-done | bytes 1048608 | tf_op jit(solution)/shard_map/ppermute | solution.py:34
  489.1 9.1 collective-permute-done.31
  517.7 13.3 %collective-permute-done.29 = bf16[1024,512]{1,0:T(8,128)(2,1)} collective-permute-done((bf16[1024,512]{1,0:T(8,128)(2,1)}, bf16[1024,512]{1,0:T(8,128)(2,1)}, u32[]{:S(2)}, u32[]{:S(2)}) %collective-permute-start.29) | collective-permute-done | bytes 1048608 | tf_op jit(solution)/shard_map/ppermute | solution.py:34
  556.2 24.1 %collective-permute-done.36 = bf16[4,128,512]{2,1,0:T(8,128)(2,1)} collective-permute-done((bf16[4,128,512]{2,1,0:T(8,128)(2,1)}, bf16[4,128,512]{2,1,0:T(8,128)(2,1)}, u32[]{:S(2)}, u32[]{:S(2)}) %collective-permute-start.36) | collective-permute-done | bytes 524320 | tf_op jit(solution)/shard_map/ppermute | solution.py:37
  783.7 16.9 %collective-permute-done.60 = bf16[8,13,128]{2,1,0:T(8,128)(2,1)} collective-permute-done((bf16[8,13,128]{2,1,0:T(8,128)(2,1)}, bf16[8,13,128]{2,1,0:T(8,128)(2,1)}, u32[]{:S(2)}, u32[]{:S(2)}) %collective-permute-start.60) | collective-permute-done | bytes 26656 | tf_op jit(solution)/shard_map/ppermute | solution.py:34
  851.5 7.2 all-to-all-done.21
  (869 shorter events, 661.8 us)
Async XLA Ops:
  89.8 58.0 %collective-permute-start.3 = (bf16[2,2,4,32,2048]{4,3,2,1,0:T(8,128)(2,1)}, bf16[2,2,4,32,2048]{4,3,2,1,0:T(8,128)(2,1)}, u32[]{:S(2)}, u32[]{:S(2)}) collective-permute-start(bf16[2,2,4,32,2048]{4,3,2,1,0:T(8,128)(2,1)} %pad_maximum_fusion.1.mine), channel_id=1, source_target_pairs={{0,8},{8,0},{16,24},{24,16},{1,9},{9,1},{17,25},{25,17},{2,10},{10... | collective-permute-start | bytes 6291464 | tf_op jit(solution)/shard_map/ppermute | solution.py:31
  107.9 33.5 %collective-permute-start.9 = (bf16[2,4,32,2048]{3,2,1,0:T(8,128)(2,1)}, bf16[2,4,32,2048]{3,2,1,0:T(8,128)(2,1)}, u32[]{:S(2)}, u32[]{:S(2)}) collective-permute-start(bf16[2,4,32,2048]{3,2,1,0:T(8,128)(2,1)} %get-tuple-element.127), channel_id=1, source_target_pairs={{0,16},{8,24},{16,0},{24,8},{1,17},{9,25},{17,1},{25,9},{2,18},{10... | collective-permute-start | bytes 3145736 | tf_op jit(solution)/shard_map/ppermute | solution.py:34
  144.1 44.3 %collective-permute-start.13 = (bf16[2,2,4,32,2048]{4,3,2,1,0:T(8,128)(2,1)}, bf16[2,2,4,32,2048]{4,3,2,1,0:T(8,128)(2,1)}, u32[]{:S(2)}, u32[]{:S(2)}) collective-permute-start(bf16[2,2,4,32,2048]{4,3,2,1,0:T(8,128)(2,1)} %pad_maximum_fusion.3.mine), channel_id=1, source_target_pairs={{0,8},{8,0},{16,24},{24,16},{1,9},{9,1},{17,25},{25,17},{2,10},{10... | collective-permute-start | bytes 6291464 | tf_op jit(solution)/shard_map/ppermute | solution.py:31
  156.9 90.1 %all-to-all-start.7 = ((bf16[4,128,1024]{2,1,0:T(8,128)(2,1)}), bf16[4,128,1024]{2,1,0:T(8,128)(2,1)}, u32[]{:S(2)}, u32[]{:S(2)}) async-start(bf16[4,128,1024]{2,1,0:T(8,128)(2,1)} %broadcast_in_dim.33), calls=%async_computation.7 | async-start | bytes 2097152 | tf_op jit(solution)/shard_map/all_to_all | solution.py:66
  197.4 57.1 %collective-permute-start.12 = (bf16[2,2,4,32,2048]{4,3,2,1,0:T(8,128)(2,1)}, bf16[2,2,4,32,2048]{4,3,2,1,0:T(8,128)(2,1)}, u32[]{:S(2)}, u32[]{:S(2)}) collective-permute-start(bf16[2,2,4,32,2048]{4,3,2,1,0:T(8,128)(2,1)} %pad_maximum_fusion.2.mine), channel_id=1, source_target_pairs={{0,8},{8,0},{16,24},{24,16},{1,9},{9,1},{17,25},{25,17},{2,10},{10... | collective-permute-start | bytes 6291464 | tf_op jit(solution)/shard_map/ppermute | solution.py:31
  247.0 60.9 %collective-permute-start.16 = (bf16[2,2,4,32,2048]{4,3,2,1,0:T(8,128)(2,1)}, bf16[2,2,4,32,2048]{4,3,2,1,0:T(8,128)(2,1)}, u32[]{:S(2)}, u32[]{:S(2)}) collective-permute-start(bf16[2,2,4,32,2048]{4,3,2,1,0:T(8,128)(2,1)} %pad_maximum_fusion.4.mine), channel_id=1, source_target_pairs={{0,8},{8,0},{16,24},{24,16},{1,9},{9,1},{17,25},{25,17},{2,10},{10... | collective-permute-start | bytes 6291464 | tf_op jit(solution)/shard_map/ppermute | solution.py:31
  247.9 38.4 %all-to-all-start.9 = ((bf16[4,64,1024]{2,1,0:T(8,128)(2,1)}), bf16[4,64,1024]{2,1,0:T(8,128)(2,1)}, u32[]{:S(2)}, u32[]{:S(2)}) async-start(bf16[4,64,1024]{2,1,0:T(8,128)(2,1)} %broadcast_in_dim.35), calls=%async_computation.9 | async-start | bytes 1048576 | tf_op jit(solution)/shard_map/all_to_all | solution.py:66
  252.9 50.5 %collective-permute-start.17 = (bf16[4,128,1024]{2,1,0:T(8,128)(2,1)}, bf16[4,128,1024]{2,1,0:T(8,128)(2,1)}, u32[]{:S(2)}, u32[]{:S(2)}) collective-permute-start(bf16[4,128,1024]{2,1,0:T(8,128)(2,1)} %all-to-all-done.7), channel_id=1, source_target_pairs={{0,1},{1,0},{2,3},{3,2},{4,5},{5,4},{6,7},{7,6},{8,9},{9,8},{10,11... | collective-permute-start | bytes 3145736 | tf_op jit(solution)/shard_map/ppermute | solution.py:37
  285.9 45.3 %collective-permute-start.21 = (bf16[2,2,4,32,2048]{4,3,2,1,0:T(8,128)(2,1)}, bf16[2,2,4,32,2048]{4,3,2,1,0:T(8,128)(2,1)}, u32[]{:S(2)}, u32[]{:S(2)}) collective-permute-start(bf16[2,2,4,32,2048]{4,3,2,1,0:T(8,128)(2,1)} %pad_maximum_fusion.6.mine), channel_id=1, source_target_pairs={{0,8},{8,0},{16,24},{24,16},{1,9},{9,1},{17,25},{25,17},{2,10},{10... | collective-permute-start | bytes 6291464 | tf_op jit(solution)/shard_map/ppermute | solution.py:31
  307.9 38.1 %collective-permute-start.18 = (bf16[2,4,128,1024]{3,2,1,0:T(8,128)(2,1)}, bf16[2,4,128,1024]{3,2,1,0:T(8,128)(2,1)}, u32[]{:S(2)}, u32[]{:S(2)}) collective-permute-start(bf16[2,4,128,1024]{3,2,1,0:T(8,128)(2,1)} %pad_maximum_fusion.5.mine), channel_id=1, source_target_pairs={{0,8},{8,0},{16,24},{24,16},{1,9},{9,1},{17,25},{25,17},{2,10},{10... | collective-permute-start | bytes 6291464 | tf_op jit(solution)/shard_map/ppermute | solution.py:31
  331.3 30.8 %collective-permute-start.24 = (bf16[2,2,4,64,1024]{4,3,2,1,0:T(8,128)(2,1)}, bf16[2,2,4,64,1024]{4,3,2,1,0:T(8,128)(2,1)}, u32[]{:S(2)}, u32[]{:S(2)}) collective-permute-start(bf16[2,2,4,64,1024]{4,3,2,1,0:T(8,128)(2,1)} %pad_maximum_fusion.7.mine), channel_id=1, source_target_pairs={{0,8},{8,0},{16,24},{24,16},{1,9},{9,1},{17,25},{25,17},{2,10},{10... | collective-permute-start | bytes 6291464 | tf_op jit(solution)/shard_map/ppermute | solution.py:31
  345.6 140.6 %collective-permute-start.28 = (bf16[2048,512]{1,0:T(8,128)(2,1)}, bf16[2048,512]{1,0:T(8,128)(2,1)}, u32[]{:S(2)}, u32[]{:S(2)}) collective-permute-start(bf16[2048,512]{1,0:T(8,128)(2,1)} %convolution_convert_fusion), channel_id=1, source_target_pairs={{0,8},{8,0},{16,24},{24,16},{1,9},{9,1},{17,25},{25,17},{2,10},{10... | collective-permute-start | bytes 6291464 | tf_op jit(solution)/shard_map/ppermute | solution.py:31
  357.8 91.9 %collective-permute-start.25 = (bf16[2048,512]{1,0:T(8,128)(2,1)}, bf16[2048,512]{1,0:T(8,128)(2,1)}, u32[]{:S(2)}, u32[]{:S(2)}) collective-permute-start(bf16[2048,512]{1,0:T(8,128)(2,1)} %convolution_convert_fusion.1), channel_id=1, source_target_pairs={{0,8},{8,0},{16,24},{24,16},{1,9},{9,1},{17,25},{25,17},{2,10},{10... | collective-permute-start | bytes 6291464 | tf_op jit(solution)/shard_map/ppermute | solution.py:31
  498.3 40.5 %collective-permute-start.32 = (bf16[1024,1024]{1,0:T(8,128)(2,1)}, bf16[1024,1024]{1,0:T(8,128)(2,1)}, u32[]{:S(2)}, u32[]{:S(2)}) collective-permute-start(bf16[1024,1024]{1,0:T(8,128)(2,1)} %convolution_convert_fusion.2), channel_id=1, source_target_pairs={{0,8},{8,0},{16,24},{24,16},{1,9},{9,1},{17,25},{25,17},{2,10},{10... | collective-permute-start | bytes 6291464 | tf_op jit(solution)/shard_map/ppermute | solution.py:31
  533.5 49.1 %all-to-all-start.16 = ((bf16[4,256,512]{2,1,0:T(8,128)(2,1)}), bf16[4,256,512]{2,1,0:T(8,128)(2,1)}, u32[]{:S(2)}, u32[]{:S(2)}) async-start(bf16[4,256,512]{2,1,0:T(8,128)(2,1)} %fusion.18), calls=%async_computation.16 | async-start | bytes 2097152 | tf_op jit(solution)/shard_map/all_to_all | solution.py:177
  543.5 51.2 %collective-permute-start.40 = (bf16[4,128,1024]{2,1,0:T(8,128)(2,1)}, bf16[4,128,1024]{2,1,0:T(8,128)(2,1)}, u32[]{:S(2)}, u32[]{:S(2)}) collective-permute-start(bf16[4,128,1024]{2,1,0:T(8,128)(2,1)} %dynamic-slice_bitcast_fusion), channel_id=1, source_target_pairs={{0,1},{1,0},{2,3},{3,2},{4,5},{5,4},{6,7},{7,6},{8,9},{9,8},{10,11... | collective-permute-start | bytes 3145736 | tf_op jit(solution)/shard_map/ppermute | solution.py:37
  548.3 32.0 %collective-permute-start.36 = (bf16[4,128,512]{2,1,0:T(8,128)(2,1)}, bf16[4,128,512]{2,1,0:T(8,128)(2,1)}, u32[]{:S(2)}, u32[]{:S(2)}) collective-permute-start(bf16[4,128,512]{2,1,0:T(8,128)(2,1)} %dynamic-slice_bitcast_fusion.4), channel_id=1, source_target_pairs={{0,1},{1,0},{2,3},{3,2},{4,5},{5,4},{6,7},{7,6},{8,9},{9,8},{10,11... | collective-permute-start | bytes 1572872 | tf_op jit(solution)/shard_map/ppermute | solution.py:37
  551.8 30.7 %collective-permute-start.33 = (bf16[1024,256]{1,0:T(8,128)(2,1)}, bf16[1024,256]{1,0:T(8,128)(2,1)}, u32[]{:S(2)}, u32[]{:S(2)}) collective-permute-start(bf16[1024,256]{1,0:T(8,128)(2,1)} %add_convert_fusion.22), channel_id=1, source_target_pairs={{0,16},{8,24},{16,0},{24,8},{1,17},{9,25},{17,1},{25,9},{2,18},{10... | collective-permute-start | bytes 1572872 | tf_op jit(solution)/shard_map/ppermute | solution.py:34
  602.6 35.2 %all-to-all-start.17 = ((bf16[4,128,1024]{2,1,0:T(8,128)(2,1)}), bf16[4,128,1024]{2,1,0:T(8,128)(2,1)}, u32[]{:S(2)}, u32[]{:S(2)}) async-start(bf16[4,128,1024]{2,1,0:T(8,128)(2,1)} %fusion.19), calls=%async_computation.17 | async-start | bytes 2097152 | tf_op jit(solution)/shard_map/all_to_all | solution.py:177
  635.9 40.6 %collective-permute-start.39 = (bf16[1024,512]{1,0:T(8,128)(2,1)}, bf16[1024,512]{1,0:T(8,128)(2,1)}, u32[]{:S(2)}, u32[]{:S(2)}) collective-permute-start(bf16[1024,512]{1,0:T(8,128)(2,1)} %convolution_convert_fusion.11), channel_id=1, source_target_pairs={{0,8},{8,0},{16,24},{24,16},{1,9},{9,1},{17,25},{25,17},{2,10},{10... | collective-permute-start | bytes 3145736 | tf_op jit(solution)/shard_map/ppermute | solution.py:31
  694.7 32.9 %collective-permute-start.47 = (bf16[1024,512]{1,0:T(8,128)(2,1)}, bf16[1024,512]{1,0:T(8,128)(2,1)}, u32[]{:S(2)}, u32[]{:S(2)}) collective-permute-start(bf16[1024,512]{1,0:T(8,128)(2,1)} %convolution_convert_fusion.8), channel_id=1, source_target_pairs={{0,8},{8,0},{16,24},{24,16},{1,9},{9,1},{17,25},{25,17},{2,10},{10... | collective-permute-start | bytes 3145736 | tf_op jit(solution)/shard_map/ppermute | solution.py:31
  771.3 34.8 %collective-permute-start.56 = (bf16[4864,128]{1,0:T(8,128)(2,1)}, bf16[4864,128]{1,0:T(8,128)(2,1)S(1)}, u32[]{:S(2)}, u32[]{:S(2)}) collective-permute-start(bf16[4864,128]{1,0:T(8,128)(2,1)} %constant_dynamic-update-slice_fusion), channel_id=1, source_target_pairs={{0,16},{8,24},{16,0},{24,8},{1,17},{9,25},{17,1},{25,9},{2,18},{10... | collective-permute-start | bytes 3735560 | tf_op jit(solution)/shard_map/ppermute | solution.py:34
  778.4 56.9 %all-to-all-start.15 = ((bf16[4,128,256]{2,1,0:T(8,128)(2,1)}), bf16[4,128,256]{2,1,0:T(8,128)(2,1)}, u32[]{:S(2)}, u32[]{:S(2)}) async-start(bf16[4,128,256]{2,1,0:T(8,128)(2,1)} %fusion.77), calls=%async_computation.15 | async-start | bytes 524288 | tf_op jit(solution)/shard_map/all_to_all | solution.py:177
  834.4 38.0 %collective-permute-start.58 = (bf16[6656,128]{1,0:T(8,128)(2,1)}, bf16[6656,128]{1,0:T(8,128)(2,1)}, u32[]{:S(2)}, u32[]{:S(2)}) collective-permute-start(bf16[6656,128]{1,0:T(8,128)(2,1)} %constant_dynamic-update-slice_fusion.9), channel_id=1, source_target_pairs={{0,8},{8,0},{16,24},{24,16},{1,9},{9,1},{17,25},{25,17},{2,10},{10... | collective-permute-start | bytes 5111816 | tf_op jit(solution)/shard_map/ppermute | solution.py:31
  (252 other events, 3270.9 us)

commit v2 on v1

--- a/solution.py
+++ b/solution.py
@@ -214,7 +214,7 @@
         self.own = self.ring_lane(partial(ring_sum, self.place), self.kept)
 
 
-def finish(place, lane, units):
+def finish_all(place, lane, units):
     flat = [u.own.reshape(-1, 128) for u in units]
     sizes = [f.shape[0] for f in flat]
     own = jnp.concatenate(flat)
@@ -359,6 +359,653 @@
         ),
         name="attend_back",
     )(do, q, k, v, p)
+
+
+BIG = pltpu.CompilerParams(vmem_limit_bytes=58 * 2**20)
+SPOT = pl.BlockSpec(memory_space=pl.ANY)
+WHOLE = pl.BlockSpec(memory_space=pltpu.VMEM)
+CHUNK = 128
+
+
+def here():
+    rep, row = lax.axis_index("replica"), lax.axis_index("fsdp")
+    return lax.div(rep, 2), lax.rem(rep, 2), lax.div(row, 2), lax.rem(row, 2)
+
+
+def flip(bit, by):
+    return 1 - bit if by else bit
+
+
+def pieces_of(refs, number, w, sems, act):
+    x, c, _, y = here()
+    rows, half = w.shape[2], w.shape[3] // 2
+    dx, dc = flip(x, number // 2), flip(c, number % 2)
+
+    def copy(ref, i, dy, g):
+        src, to = ref.at[i, :, pl.ds(0, rows)], w.at[:, flip(y, dy), :, pl.ds(g * half, half)]
+        getattr(pltpu.make_async_copy(src, to, sems.at[2 * dy + g]), act)()
+
+    if act == "wait":
+        for dy in range(2):
+            for g in range(2):
+                copy(refs[0], 0, dy, g)
+        return
+    for far in range(2):
+        p0, q0, p1, q1 = refs[4 * far : 4 * far + 4]
+
+        @pl.when(dc == far)
+        def _(p1=p1, q1=q1):
+            copy(p1, dx, 0, 1)
+            copy(q1, dx, 1, 1)
+
+        for ref, side in ((p0, 0), (q0, 1)):
+
+            @pl.when((dc == far) & (dx == side))
+            def _(ref=ref):
+                copy(ref, 0, 0, 0)
+                copy(ref, 1, 1, 0)
+
+
+def row_sum(v):
+    return jnp.sum(v, 0, keepdims=True)
+
+
+def normal(v):
+    centered = v - jnp.mean(v, -1, keepdims=True)
+    inverse = lax.rsqrt(jnp.mean(centered * centered, -1, keepdims=True) + EPSILON)
+    return centered * inverse, inverse
+
+
+def chunks(rows, step, do):
+    def one(i, carry):
+        do(pl.ds(pl.multiple_of(i * step, step), step))
+        return carry
+
+    lax.fori_loop(0, rows // step, one, 0)
+
+
+def weight(w_ref, *lead):
+    v = w_ref[lead] if lead else w_ref[...]
+    return v.reshape(v.shape[-4] * v.shape[-3] * v.shape[-2], v.shape[-1])
+
+
+def times(a_ref, w_ref, put, tile=256):
+    def one(i, carry):
+        lanes = pl.ds(pl.multiple_of(i * tile, tile), tile)
+        w = w_ref[:, :, :, lanes]
+        w = w.reshape(w.shape[0] * w.shape[1] * w.shape[2], tile)
+        put(lanes, jnp.dot(a_ref[...], w, preferred_element_type=F32))
+        return carry
+
+    lax.fori_loop(0, w_ref.shape[3] // tile, one, 0)
+
+
+def times_t(pairs, put):
+    wide = pairs[0][1].shape[1] * pairs[0][1].shape[2]
+
+    def one(i, carry):
+        total = None
+        for a_ref, w_ref in pairs:
+            w = w_ref[i].reshape(wide, w_ref.shape[3])
+            part = dot_nt(a_ref[...], w)
+            total = part if total is None else total + part
+        put(pl.ds(pl.multiple_of(i * wide, wide), wide), total)
+        return carry
+
+    lax.fori_loop(0, pairs[0][1].shape[0], one, 0)
+
+
+def loaded(m, n, count):
+    return [pltpu.VMEM((4, 2, m, n), BF)] * count + [pltpu.SemaphoreType.DMA((count, 4))]
+
+
+def cost(flops, *arrays):
+    return pl.CostEstimate(
+        flops=flops,
+        transcendentals=0,
+        bytes_accessed=sum(a.size * a.dtype.itemsize for a in arrays),
+    )
+
+
+def shape(dims, dtype):
+    return jax.ShapeDtypeStruct(dims, dtype)
+
+
+def first_kernel(x_ref, vec_ref, *rest):
+    refs, (act_ref, q_ref, k_ref, v_ref), (wq, wk, wv, sems) = rest[:8], rest[8:12], rest[12:]
+    for i, w in enumerate((wq, wk, wv)):
+        pieces_of(refs, i, w, sems.at[i], "start")
+
+    def norm(rows):
+        n, _ = normal(x_ref[rows, :].astype(F32))
+        act_ref[rows, :] = (n * vec_ref[0:1] + vec_ref[1:2]).astype(BF)
+
+    chunks(x_ref.shape[0], CHUNK, norm)
+    for i, (w, out, bias) in enumerate(((wq, q_ref, 2), (wk, k_ref, None), (wv, v_ref, 3))):
+        pieces_of(refs, i, w, sems.at[i], "wait")
+
+        def put(lanes, v, out=out, bias=bias):
+            if bias is not None:
+                v = v + vec_ref[bias : bias + 1, lanes]
+            out[:, lanes] = v.astype(BF)
+
+        times(act_ref, w, put)
+
+
+def first(x, vecs, unit, m):
+    like = shape(x.shape, BF)
+    return pl.pallas_call(
+        first_kernel,
+        in_specs=[WHOLE, WHOLE] + [SPOT] * 8,
+        out_specs=[WHOLE] * 4,
+        out_shape=[like] * 4,
+        scratch_shapes=loaded(m, x.shape[1], 3),
+        compiler_params=BIG,
+        cost_estimate=cost(6 * x.size * x.shape[1], x, x, x, x, x, *unit),
+        name="first",
+    )(x, vecs, *unit)
+
+
+def project_kernel(second, numbers, rows_of, a_ref, res_ref, vec_ref, *rest):
+    refs = rest[:16] if second else rest[:8]
+    rest = rest[len(refs) :]
+    outs, (w1, *rest) = rest[: 3 if second else 2], rest[3 if second else 2 :]
+    mid_ref, act_ref = outs[:2]
+    sems = rest[-1]
+    bias, gain, shift, bias2 = rows_of
+    pieces_of(refs[:8], numbers[0], w1, sems.at[0], "start")
+    if second:
+        w2 = rest[0]
+        pieces_of(refs[8:], numbers[1], w2, sems.at[1], "start")
+    pieces_of(refs[:8], numbers[0], w1, sems.at[0], "wait")
+
+    def put(lanes, v):
+        mid_ref[:, lanes] = res_ref[:, lanes].astype(F32) + (v + vec_ref[bias : bias + 1, lanes])
+
+    times(a_ref, w1, put)
+
+    def norm(rows):
+        n, _ = normal(mid_ref[rows, :])
+        act_ref[rows, :] = (n * vec_ref[gain : gain + 1] + vec_ref[shift : shift + 1]).astype(BF)
+
+    chunks(a_ref.shape[0], CHUNK, norm)
+    if second:
+        pieces_of(refs[8:], numbers[1], w2, sems.at[1], "wait")
+
+        def put2(lanes, v):
+            outs[2][:, lanes] = (v + vec_ref[bias2 : bias2 + 1, lanes]).astype(BF)
+
+        times(act_ref, w2, put2)
+
+
+def project(a, residual, vecs, rows_of, units, numbers, m, name):
+    second = len(units) == 2
+    refs = [r for u in units for r in u]
+    return pl.pallas_call(
+        partial(project_kernel, second, numbers, rows_of),
+        in_specs=[WHOLE] * 3 + [SPOT] * len(refs),
+        out_specs=[WHOLE] * (3 if second else 2),
+        out_shape=[shape(a.shape, F32), shape(a.shape, BF)] + ([shape(a.shape, BF)] if second else []),
+        scratch_shapes=loaded(m, a.shape[1], len(units)),
+        compiler_params=BIG,
+        cost_estimate=cost(2 * len(units) * a.size * a.shape[1], a, a, a, a, a, a, *refs[:4]),
+        name=name,
+    )(a, residual, vecs, *refs)
+
+
+def query_kernel(bias, a_ref, vec_ref, *rest):
+    refs, out_ref, (w, sems) = rest[:8], rest[8], rest[9:]
+    pieces_of(refs, 0, w, sems.at[0], "start")
+    pieces_of(refs, 0, w, sems.at[0], "wait")
+
+    def put(lanes, v):
+        out_ref[:, lanes] = (v + vec_ref[bias : bias + 1, lanes]).astype(BF)
+
+    times(a_ref, w, put)
+
+
+def query(a, vecs, bias, unit, m):
+    return pl.pallas_call(
+        partial(query_kernel, bias),
+        in_specs=[WHOLE] * 2 + [SPOT] * 8,
+        out_specs=WHOLE,
+        out_shape=shape(a.shape, BF),
+        scratch_shapes=loaded(m, a.shape[1], 1),
+        compiler_params=BIG,
+        cost_estimate=cost(2 * a.size * a.shape[1], a, a, *unit[:2]),
+        name="query",
+    )(a, vecs, *unit)
+
+
+def memory_kernel(e_ref, vec_ref, *rest):
+    refs, (k_ref, v_ref), (wk, wv, sems) = rest[:8], rest[8:10], rest[10:]
+
+    @pl.when(pl.program_id(0) == 0)
+    def _():
+        for i, w in enumerate((wk, wv)):
+            pieces_of(refs, i + 1, w, sems.at[i], "start")
+        for i, w in enumerate((wk, wv)):
+            pieces_of(refs, i + 1, w, sems.at[i], "wait")
+
+    def put_k(lanes, v):
+        k_ref[:, lanes] = v.astype(BF)
+
+    def put_v(lanes, v):
+        v_ref[:, lanes] = (v + vec_ref[8:9, lanes]).astype(BF)
+
+    times(e_ref, wk, put_k)
+    times(e_ref, wv, put_v)
+
+
+def memory(e, vecs, unit, m, step=512):
+    d = e.shape[1]
+    blk = pl.BlockSpec((step, d), lambda i: (i, 0))
+    return pl.pallas_call(
+        memory_kernel,
+        grid=(e.shape[0] // step,),
+        in_specs=[blk, pl.BlockSpec(vecs.shape, lambda i: (0, 0))] + [SPOT] * 8,
+        out_specs=[blk, blk],
+        out_shape=[shape(e.shape, BF)] * 2,
+        scratch_shapes=loaded(m, d, 2),
+        compiler_params=BIG,
+        cost_estimate=cost(4 * e.size * d, e, e, e, *unit),
+        name="memory",
+    )(e, vecs, *unit)
+
+
+def memory_back_kernel(dk_ref, dv_ref, *rest):
+    refs, (out_ref, sum_ref), (wk, wv, sems) = rest[:8], rest[8:10], rest[10:]
+
+    @pl.when(pl.program_id(0) == 0)
+    def _():
+        for i, w in enumerate((wk, wv)):
+            pieces_of(refs, i + 1, w, sems.at[i], "start")
+        sum_ref[...] = jnp.zeros_like(sum_ref)
+        for i, w in enumerate((wk, wv)):
+            pieces_of(refs, i + 1, w, sems.at[i], "wait")
+
+    def put(lanes, v):
+        out_ref[:, lanes] = v
+
+    times_t([(dk_ref, wk), (dv_ref, wv)], put)
+    sum_ref[0:1] += row_sum(dv_ref[...].astype(F32))
+
+
+def memory_back(dk, dv, unit, m, step=512):
+    d = dk.shape[1]
+    blk = pl.BlockSpec((step, d), lambda i: (i, 0))
+    return pl.pallas_call(
+        memory_back_kernel,
+        grid=(dk.shape[0] // step,),
+        in_specs=[blk, blk] + [SPOT] * 8,
+        out_specs=[blk, pl.BlockSpec((8, d), lambda i: (0, 0))],
+        out_shape=[shape(dk.shape, F32), shape((8, d), F32)],
+        scratch_shapes=loaded(m, d, 2),
+        compiler_params=BIG,
+        cost_estimate=cost(4 * dk.size * d, dk, dk, dk, dk, *unit),
+        name="memory_back",
+    )(dk, dv, *unit)
+
+
+def apply_norm_back(rows, dact, v, gain, residual, sums):
+    n, inverse = normal(v)
+    sums[0:1] += row_sum(dact * n)
+    sums[1:2] += row_sum(dact)
+    q = dact * gain
+    mean_one = jnp.mean(q, -1, keepdims=True)
+    mean_two = jnp.mean(q * n, -1, keepdims=True)
+    return residual + inverse * (q - mean_one - n * mean_two)
+
+
+def cross_back_kernel(dq_ref, mid_ref, dmid_ref, vec_ref, *rest):
+    refs, (out_ref, low_ref, do_ref, sum_ref), (dact, w1, w2, sems) = rest[:16], rest[16:20], rest[20:]
+    pieces_of(refs[:8], 0, w1, sems.at[0], "start")
+    pieces_of(refs[8:], 3, w2, sems.at[1], "start")
+    sum_ref[...] = jnp.zeros_like(sum_ref)
+    sum_ref[2:3] = row_sum(dq_ref[...].astype(F32))
+    pieces_of(refs[:8], 0, w1, sems.at[0], "wait")
+
+    def put(lanes, v):
+        dact[:, lanes] = v
+
+    times_t([(dq_ref, w1)], put)
+
+    def back(rows):
+        total = apply_norm_back(
+            rows, dact[rows, :], mid_ref[rows, :], vec_ref[5:6], dmid_ref[rows, :], sum_ref
+        )
+        out_ref[rows, :] = total
+        low = total.astype(BF)
+        low_ref[rows, :] = low
+        sum_ref[3:4] += row_sum(low.astype(F32))
+
+    chunks(dq_ref.shape[0], CHUNK, back)
+    pieces_of(refs[8:], 3, w2, sems.at[1], "wait")
+
+    def put2(lanes, v):
+        do_ref[:, lanes] = v.astype(BF)
+
+    times_t([(low_ref, w2)], put2)
+
+
+def cross_back(dq, mid, dmid, vecs, cross_unit, self_unit, m):
+    d = dq.shape[1]
+    return pl.pallas_call(
+        cross_back_kernel,
+        in_specs=[WHOLE] * 4 + [SPOT] * 16,
+        out_specs=[WHOLE] * 4,
+        out_shape=[shape(dq.shape, F32), shape(dq.shape, BF), shape(dq.shape, BF), shape((8, d), F32)],
+        scratch_shapes=[pltpu.VMEM(dq.shape, F32)] + loaded(m, d, 2),
+        compiler_params=BIG,
+        cost_estimate=cost(4 * dq.size * d, mid, mid, mid, dq, dq, dq, *cross_unit[:4]),
+        name="cross_back",
+    )(dq, mid, dmid, vecs, *cross_unit, *self_unit)
+
+
+def self_back_kernel(dq_ref, dk_ref, dv_ref, x_ref, dmid_ref, vec_ref, *rest):
+    refs, (out_ref, sum_ref), (dact, wq, wk, wv, sems) = rest[:8], rest[8:10], rest[10:]
+    for i, w in enumerate((wq, wk, wv)):
+        pieces_of(refs, i, w, sems.at[i], "start")
+    sum_ref[...] = jnp.zeros_like(sum_ref)
+    sum_ref[2:3] = row_sum(dq_ref[...].astype(F32))
+    sum_ref[3:4] = row_sum(dv_ref[...].astype(F32))
+    for i, w in enumerate((wq, wk, wv)):
+        pieces_of(refs, i, w, sems.at[i], "wait")
+
+    def put(lanes, v):
+        dact[:, lanes] = v
+
+    times_t([(dq_ref, wq), (dk_ref, wk), (dv_ref, wv)], put)
+
+    def back(rows):
+        out_ref[rows, :] = apply_norm_back(
+            rows, dact[rows, :], x_ref[rows, :].astype(F32), vec_ref[0:1], dmid_ref[rows, :], sum_ref
+        )
+
+    chunks(dq_ref.shape[0], CHUNK, back)
+
+
+def self_back(dq, dk, dv, x, dmid, vecs, unit, m):
+    d = dq.shape[1]
+    return pl.pallas_call(
+        self_back_kernel,
+        in_specs=[WHOLE] * 6 + [SPOT] * 8,
+        out_specs=[WHOLE] * 2,
+        out_shape=[shape(dq.shape, F32), shape((8, d), F32)],
+        scratch_shapes=[pltpu.VMEM(dq.shape, F32)] + loaded(m, d, 3),
+        compiler_params=BIG,
+        cost_estimate=cost(6 * dq.size * d, dmid, dmid, dq, dq, dq, dq, *unit),
+        name="self_back",
+    )(dq, dk, dv, x, dmid, vecs, *unit)
+
+
+def output_back_kernel(d_ref, *rest):
+    refs, do_ref, (w, sems) = rest[:8], rest[8], rest[9:]
+    pieces_of(refs, 3, w, sems.at[0], "start")
+    pieces_of(refs, 3, w, sems.at[0], "wait")
+
+    def put(lanes, v):
+        do_ref[:, lanes] = v.astype(BF)
+
+    times_t([(d_ref, w)], put)
+
+
+def output_back(dlow, unit, m):
+    d = dlow.shape[1]
+    return pl.pallas_call(
+        output_back_kernel,
+        in_specs=[WHOLE] + [SPOT] * 8,
+        out_specs=WHOLE,
+        out_shape=shape(dlow.shape, BF),
+        scratch_shapes=loaded(m, d, 1),
+        compiler_params=BIG,
+        cost_estimate=cost(2 * dlow.size * d, dlow, dlow, *unit[:2]),
+        name="output_back",
+    )(dlow, *unit)
+
+
+def send_off(block, away, keep, dx, dc, spot, sem):
+    @pl.when(dc == 1)
+    def _():
+        pltpu.make_async_copy(block, away.at[(dx,) + spot], sem).start()
+
+    @pl.when(dc == 0)
+    def _():
+        pltpu.make_async_copy(block, keep.at[(dx,) + spot], sem).start()
+
+
+def grads_kernel(sides, *rest):
+    lefts = sorted({l for l, _ in sides})
+    n_in = len(lefts) + len(sides)
+    left_refs, right_refs = rest[: len(lefts)], rest[len(lefts) : n_in]
+    away, keep = rest[n_in : n_in + 2]
+    out, sems = rest[-2], rest[-1]
+    turned = rest[n_in + 2 : -2]
+    x, c, z, y = here()
+    done = set()
+    for number, (l, _) in enumerate(sides):
+        t_ref = turned[l]
+        if l not in done:
+            done.add(l)
+            for f in range(left_refs[l].shape[1] // 256):
+                t_ref[f * 256 : (f + 1) * 256, :] = left_refs[l][:, f * 256 : (f + 1) * 256].T
+        r_ref = right_refs[number]
+        half = out.shape[-1]
+        for g in range(2):
+
+            def one(zz, carry, g=g, number=number, t_ref=t_ref, r_ref=r_ref):
+                rows = t_ref[pl.ds(pl.multiple_of(zz * 256, 256), 256), :]
+                v = jnp.dot(rows, r_ref[:, g * half : (g + 1) * half], preferred_element_type=F32).astype(BF)
+                out[number, g, y, zz] = v[:128]
+                out[number, g, 1 - y, zz] = v[128:]
+                return carry
+
+            lax.fori_loop(0, 4, one, 0)
+        dx, dc = flip(x, number // 2), flip(c, number % 2)
+        send_off(out.at[number], away, keep, dx, dc, (), sems.at[number])
+    for number in range(4):
+        pltpu.make_async_copy(out.at[number], keep.at[0], sems.at[number]).wait()
+
+
+def grads(lefts, rights, sides, name):
+    d, n = lefts[0].shape[1], rights[0].shape[1]
+    dims = (2, 2, 2, 4, d // 8, n // 2)
+    sides = tuple((l, i) for i, l in enumerate(sides))
+    return pl.pallas_call(
+        partial(grads_kernel, sides),
+        in_specs=[WHOLE] * (len(lefts) + 4),
+        out_specs=[SPOT] * 2,
+        out_shape=[shape(dims, BF)] * 2,
+        scratch_shapes=[pltpu.VMEM((d, l.shape[0]), BF) for l in lefts]
+        + [pltpu.VMEM((4,) + dims[1:], BF), pltpu.SemaphoreType.DMA((4,))],
+        compiler_params=BIG,
+        cost_estimate=cost(2 * sum(r.size for r in rights) * d, *lefts, *rights, *rights, *rights),
+        name=name,
+    )(*lefts, *rights)
+
+
+def grads_of(left, lefts, rights, sides, name):
+    return grads([left] + list(lefts), rights, sides, name)
+
+
+def ffn_kernel(last, first_row, act_ref, dy_ref, mid_ref, vec_ref, *rest):
+    begin = rest[:2] if last else ()
+    rest = rest[len(begin) :]
+    refs, rest = rest[:8], rest[8:]
+    outs, rest = rest[: 4 if last else 2], rest[4 if last else 2 :]
+    dbe_ref, away, keep = rest[:3]
+    act_t, hid_ref, dexp_ref, acc, dact, out, we0, wd0, we1, wd1, sems, out_sems = rest[3:]
+    i = pl.program_id(0)
+    s = lax.rem(i, 2)
+    rows, d = act_ref.shape
+    ff = d // 2
+    x, c, z, y = here()
+    mats = ((we0, wd0), (we1, wd1))
+
+    @pl.when(i == 0)
+    def _():
+        for t in range(2):
+            for n in range(2):
+                pieces_of(refs, 2 * t + n, mats[t][n], sems.at[2 * t + n], "start")
+        for f in range(d // 256):
+            act_t[f * 256 : (f + 1) * 256, :] = act_ref[:, f * 256 : (f + 1) * 256].T
+        if last:
+            acc[...] = begin[0][...]
+            dact[...] = begin[1][...]
+            outs[3][...] = jnp.zeros_like(outs[3])
+        else:
+            acc[...] = jnp.zeros_like(acc)
+            dact[...] = jnp.zeros_like(dact)
+
+    dbe_ref[...] = jnp.zeros_like(dbe_ref)
+
+    def block(t):
+        we_ref, wd_ref = mats[t]
+
+        @pl.when(s == 0)
+        def _():
+            for n in range(2):
+                pieces_of(refs, 2 * t + n, mats[t][n], sems.at[2 * t + n], "wait")
+
+        lanes = pl.ds(pl.multiple_of(s * ff, ff), ff)
+        bias = vec_ref[first_row + t : first_row + t + 1, lanes]
+
+        def half(r):
+            we = we_ref[:, :, :, lanes].reshape(d, ff)
+            wd = wd_ref[pl.ds(2 * s, 2)].reshape(ff, d)
+            u = jnp.dot(act_ref[r, :], we, preferred_element_type=F32) + bias
+            cdf = 0.5 * (1.0 + lax.erf(u * np.float32(0.5**0.5)))
+            pdf = jnp.exp(-0.5 * u * u) * np.float32((2 * np.pi) ** -0.5)
+            hid = (u * cdf).astype(BF)
+            hid_ref[r, :] = hid
+            dexp = (dot_nt(dy_ref[r, :], wd) * (cdf + u * pdf)).astype(BF)
+            dexp_ref[r, :] = dexp
+            dbe_ref[0] += row_sum(dexp.astype(F32))
+            acc[r, :] += jnp.dot(hid, wd, preferred_element_type=F32)
+            dact[r, :] += dot_nt(dexp, we)
+
+        chunks(rows, 256, half)
+
+        def e_part(zz, carry):
+            at_rows = pl.ds(pl.multiple_of(zz * 256, 256), 256)
+            v = jnp.dot(act_t[at_rows, :], dexp_ref[...], preferred_element_type=F32).astype(BF)
+            out[2 * t, s, y, zz] = v[:128]
+            out[2 * t, s, 1 - y, zz] = v[128:]
+            return carry
+
+        lax.fori_loop(0, 4, e_part, 0)
+        hid_t = hid_ref[...].T
+        for zz in range(2):
+            for yy in range(2):
+                n = 2 * zz + yy
+                v = jnp.dot(hid_t[n * 128 : (n + 1) * 128], dy_ref[...], preferred_element_type=F32).astype(BF)
+                for g in range(2):
+                    out[2 * t + 1, g, flip(y, yy), 2 * s + zz] = v[:, g * ff : (g + 1) * ff]
+
+        @pl.when(s == 1)
+        def _():
+            for n in range(2):
+                number = 2 * t + n
+                dx, dc = flip(x, number // 2), flip(c, number % 2)
+                send_off(out.at[number], away, keep, dx, dc, (), out_sems.at[number])
+
+    for t in range(2):
+        pl.when(lax.div(i, 2) == t)(partial(block, t))
+
+    @pl.when(i == pl.num_programs(0) - 1)
+    def _():
+        if last:
+            out_ref, dmid_ref, low_ref, sum_ref = outs
+
+            def back(r):
+                mid = mid_ref[r, :]
+                out_ref[r, :] = (mid + (acc[r, :] + vec_ref[12:13])).astype(BF)
+                dy = dy_ref[r, :].astype(F32)
+                total = apply_norm_back(r, dact[r, :], mid, vec_ref[10:11], dy, sum_ref)
+                dmid_ref[r, :] = total
+                low = total.astype(BF)
+                low_ref[r, :] = low
+                sum_ref[2:3] += row_sum(dy)
+                sum_ref[3:4] += row_sum(low.astype(F32))
+
+            chunks(rows, CHUNK, back)
+        else:
+            outs[0][...] = acc[...]
+            outs[1][...] = dact[...]
+        for number in range(4):
+            pltpu.make_async_copy(out.at[number], keep.at[0], out_sems.at[number]).wait()
+
+
+def ffn(act, dy, mid, vecs, unit, m, begin, first_row):
+    rows, d = act.shape
+    last = bool(begin)
+    still = lambda s: pl.BlockSpec(s.shape, lambda j: (0,) * len(s.shape))
+    dims = (2, 2, 2, 4, m, d // 2)
+    if last:
+        heads = [shape(act.shape, BF), shape(act.shape, F32), shape(act.shape, BF), shape((8, d), F32)]
+    else:
+        heads = [shape(act.shape, F32)] * 2
+    return pl.pallas_call(
+        partial(ffn_kernel, last, first_row),
+        grid=(4,),
+        in_specs=[still(v) for v in (act, dy, mid, vecs, *begin)] + [SPOT] * 8,
+        out_specs=[still(s) for s in heads]
+        + [pl.BlockSpec((1, 1, d // 2), lambda j: (j, 0, 0))]
+        + [SPOT] * 2,
+        out_shape=heads + [shape((4, 1, d // 2), F32)] + [shape(dims, BF)] * 2,
+        scratch_shapes=[
+            pltpu.VMEM((d, rows), BF),
+            pltpu.VMEM((rows, d // 2), BF),
+            pltpu.VMEM((rows, d // 2), BF),
+            pltpu.VMEM((rows, d), F32),
+            pltpu.VMEM((rows, d), F32),
+            pltpu.VMEM((4,) + dims[1:], BF),
+        ]
+        + loaded(m, d, 4)
+        + [pltpu.SemaphoreType.DMA((4,))],
+        compiler_params=BIG,
+        cost_estimate=cost(24 * act.size * d, *unit, *unit, mid, mid),
+        name="ffn",
+    )(act, dy, mid, vecs, *begin, *unit)
+
+
+def finish_kernel(count, *rest):
+    units, outs, held = [rest[3 * i : 3 * i + 3] for i in range(count)], rest[3 * count : -1], rest[-1]
+    x, c, _, _ = here()
+    half = units[0][0].shape[-1]
+    for i, (own_ref, x_ref, core_ref) in enumerate(units):
+        held[0], held[2] = own_ref[...], x_ref[...]
+        held[1], held[3] = core_ref[0], core_ref[1]
+        for number in range(4):
+            j = flip(x, number // 2) * 2 + flip(c, number % 2)
+            for g in range(2):
+                v = held[j, g].astype(F32)
+                if count == 1:
+                    outs[number][:, g * half : (g + 1) * half] = v
+                elif number % 2:
+                    t = 2 * i + number // 2
+                    outs[1][t * v.shape[0] : (t + 1) * v.shape[0], g * half : (g + 1) * half] = v
+                else:
+                    t = 2 * i + number // 2
+                    for f in range(half // 128):
+                        to = ((g * (half // 128) + f) * 4 + t) * 128
+                        outs[0][:, to : to + 128] = v[:, f * 128 : (f + 1) * 128]
+
+
+def finish(*units):
+    _, m, half = units[0][0].shape
+    n = 2 * half
+    dims = [(m, n)] * 4 if len(units) == 1 else [(m, 4 * n), (4 * m, n)]
+    return pl.pallas_call(
+        partial(finish_kernel, len(units)),
+        in_specs=[WHOLE] * (3 * len(units)),
+        out_specs=[WHOLE] * len(dims),
+        out_shape=[shape(s, F32) for s in dims],
+        scratch_shapes=[pltpu.VMEM((4, 2, m, half), BF)],
+        compiler_params=BIG,
+        cost_estimate=cost(0, *[v for u in units for v in u] * 3),
+        name="finish",
+    )(*[v for u in units for v in u])
 
 
 def product(left, right):
@@ -544,10 +1191,10 @@
     second = [g_sv, g_sq, g_sk]
     run_steps(first + second)
     early = scatter_vectors(place, lane, ring_lane, early)
-    (*g_ff, g_co, g_cv, g_ck, g_cq, g_so) = finish(place, lane, first)
+    (*g_ff, g_co, g_cv, g_ck, g_cq, g_so) = finish_all(place, lane, first)
     g_down, g_exp = g_ff[:2], g_ff[2:]
     late = scatter_vectors(place, lane, ring_lane, late)
-    g_sv, g_sq, g_sk = finish(place, lane, second)
+    g_sv, g_sq, g_sk = finish_all(place, lane, second)
 
     g_exp = jnp.stack([t.reshape(m, rows, fl) for t in g_exp], 2).reshape(m, ff)
     g_down = jnp.concatenate(g_down, 0)
@@ -564,6 +1211,263 @@
     )
 
 
+class Order:
+    def __init__(self, width):
+        self.width, self.past, self.sent, self.ran = width, [], [], []
+
+    def send(self, move, v):
+        after = list(self.ran)
+        if len(self.past) >= self.width:
+            after.append(self.past[-self.width])
+        if after:
+            v, *_ = lax.optimization_barrier((v, *after))
+        got = move(v)
+        self.past.append(got)
+        self.sent.append(v)
+        return got
+
+    def swap(self, move, v):
+        if self.ran:
+            v, *_ = lax.optimization_barrier((v, *self.ran))
+        self.sent.append(v)
+        return move(v)
+
+    def run(self, kernel, v, *rest, **named):
+        if self.sent or self.ran:
+            v, *_ = lax.optimization_barrier((v, *self.sent, *self.ran))
+        out = kernel(v, *rest, **named)
+        self.sent, self.ran = [], [out[0] if isinstance(out, (list, tuple)) else out]
+        return out
+
+
+class Unit:
+    def __init__(self, place, order, piece):
+        self.place, self.order, self.piece = place, order, piece
+        self.steps = [self.ring, self.one, self.two, self.core]
+
+    def ring(self):
+        a = self.order.swap(partial(ring_gather, self.place), self.piece)
+        self.a0, self.a1 = a[:, 0], a[:, 1]
+
+    def one(self):
+        self.p0 = jnp.stack([self.a0, self.order.send(self.place.pair, self.a0)])
+        self.p1 = jnp.stack([self.a1, self.order.send(self.place.across, self.a1)])
+
+    def two(self):
+        self.q0 = self.order.send(self.place.across, self.p0)
+        self.q1 = self.order.send(self.place.pair, self.p1)
+        self.c0 = self.order.send(self.place.core, self.p0)
+        self.c1 = self.order.send(self.place.core, self.p1)
+
+    def core(self):
+        d0 = self.order.send(self.place.core, self.q0)
+        d1 = self.order.send(self.place.core, self.q1)
+        self.refs = (self.p0, self.q0, self.p1, self.q1, self.c0, d0, self.c1, d1)
+
+
+def low_sum(*parts):
+    total = parts[0].astype(F32)
+    for p in parts[1:]:
+        total = total + p.astype(F32)
+    return total.astype(BF)
+
+
+class Sum:
+    def __init__(self, place, order, away, keep):
+        self.place, self.order = place, order
+        self.away, self.keep = away, keep
+        self.steps = [self.core, self.one, self.two, self.ring, self.last_x, self.last_core]
+
+    def core(self):
+        self.came = self.order.send(self.place.core, self.away)
+
+    def one(self):
+        k, r = self.keep, self.came
+        self.from_x = self.order.send(self.place.across, low_sum(k[1, 0], r[1, 0]))
+        self.from_y = self.order.send(self.place.pair, low_sum(k[:, 1, 1], r[:, 1, 1]))
+
+    def two(self):
+        k, r, fx, fy = self.keep, self.came, self.from_x, self.from_y
+        self.next_y = self.order.send(self.place.pair, low_sum(k[0, 0, 1], r[0, 0, 1], fx[1]))
+        self.next_x = self.order.send(self.place.across, low_sum(k[1, 1, 0], r[1, 1, 0], fy[1]))
+
+    def ring(self):
+        k, r, fx, fy = self.keep, self.came, self.from_x, self.from_y
+        first = low_sum(k[0, 0, 0], r[0, 0, 0], fx[0], self.next_y)
+        second = low_sum(k[0, 1, 0], r[0, 1, 0], fy[0], self.next_x)
+        self.own = self.order.swap(partial(ring_sum, self.place), jnp.stack([first, second], 1))
+
+    def last_x(self):
+        self.own_x = self.order.send(self.place.across, self.own)
+
+    def last_core(self):
+        came = self.order.send(self.place.core, jnp.stack([self.own, self.own_x]))
+        self.parts = (self.own, self.own_x, came)
+
+
+def fast_body(
+    groups,
+    rows,
+    decoder_input,
+    encoder_out,
+    prefix_length,
+    output_grad,
+    self_query,
+    self_key,
+    self_value,
+    self_output,
+    selfquery_bias,
+    selfvalue_bias,
+    self_attention_output_bias,
+    cross_query,
+    cross_key,
+    cross_value,
+    cross_output,
+    crossquery_bias,
+    crossvalue_bias,
+    crossoutput_bias,
+    expand_weight,
+    expand_bias,
+    down_projection_weight,
+    reduce_bias,
+    selfnorm_gain,
+    selfnorm_bias,
+    crossnorm_gain,
+    crossnorm_bias,
+    finalnorm_gain,
+    finalnorm_bias,
+):
+    place = Place(groups, rows)
+    batch, seq, d = decoder_input.shape
+    m = self_query.shape[0]
+    ff = expand_weight.shape[1]
+    rank = 2 * place.x + place.c
+    order = Order(5)
+
+    small = [
+        selfnorm_gain, selfnorm_bias, selfquery_bias, selfvalue_bias, self_attention_output_bias,
+        crossnorm_gain, crossnorm_bias, crossquery_bias, crossvalue_bias, crossoutput_bias,
+        finalnorm_gain, finalnorm_bias, reduce_bias, expand_bias,
+    ]
+    packed = jnp.concatenate(small)
+    count = 13 + ff // d
+    packed = jnp.pad(packed, (0, 8 * d - packed.shape[0])).reshape(2, 8, d // 2)
+
+    def pick(*shards):
+        v = at(jnp.stack(shards), rank)
+        return v.reshape(m, 2, d // 2).transpose(1, 0, 2)
+
+    w_e = expand_weight.reshape(m, rows, 4, -1).transpose(2, 0, 1, 3).reshape(4, m, d)
+    w_d = down_projection_weight.reshape(4, m, d)
+    unit = partial(Unit, place, order)
+    u_self = unit(jnp.concatenate([pick(self_query, self_key, self_value, self_output), packed], 1))
+    u_cross = unit(pick(cross_query, cross_key, cross_value, cross_output))
+    u_low = unit(pick(w_e[0], w_d[0], w_e[1], w_d[1]))
+    u_high = unit(pick(w_e[2], w_d[2], w_e[3], w_d[3]))
+
+    x = decoder_input.reshape(batch * seq, d)
+    e = encoder_out.reshape(-1, d)
+    dy = output_grad.reshape(batch * seq, d)
+    run = order.run
+
+    u_self.ring()
+    u_self.one()
+    u_cross.ring()
+    u_self.two()
+    u_low.ring()
+    u_self.core()
+    u_cross.one()
+    self_w = u_self.refs
+    both = jnp.stack([v[:, :, m:] for v in (u_self.p0[:, :, :], jnp.stack([u_self.p1[0], u_self.q1[0]]))])
+    both = both.transpose(2, 1, 0, 3, 4)
+    both = jnp.where(place.y == 0, both, both[:, ::-1]).transpose(0, 1, 2, 3, 4).reshape(rows, -1)
+    vecs = both[:, : count * m].reshape(rows, count, m).transpose(1, 0, 2).reshape(count, d).astype(F32)
+    act1, q, k, v = run(first, x, vecs, self_w, m)
+    u_cross.two()
+    o, p = run(attend, q, k, v, prefix_length, batch, True)
+    u_high.ring()
+    u_cross.core()
+    cross_w = u_cross.refs
+    u_low.one()
+    mid1, act2 = run(project, o, x, vecs, (4, 5, 6, None), (self_w,), (3,), m, "self_out")
+    u_low.two()
+    ck, cv = run(memory, e, vecs, cross_w, m)
+    cq = run(query, act2, vecs, 7, cross_w, m)
+    u_low.core()
+    u_high.one()
+    co, cp = run(attend, cq, ck, cv, prefix_length, batch, False)
+    u_high.two()
+    mid2, act3 = run(project, co, mid1, vecs, (9, 10, 11, None), (cross_w,), (3,), m, "cross_out")
+    low_w = u_low.refs
+
+    *begin, dbe_low, away, keep = run(ffn, act3, dy, mid2, vecs, low_w, m, (), 13)
+    total = partial(Sum, place, order)
+    g_low = total(away, keep)
+    u_high.core()
+    g_low.core()
+    layer_out, dmid2, dcross, sums3, dbe_high, away, keep = run(
+        ffn, act3, dy, mid2, vecs, u_high.refs, m, tuple(begin), 15
+    )
+    g_high = total(away, keep)
+    g_low.one()
+    g_high.core()
+    dco = run(output_back, dcross, cross_w, m)
+    dcq, dck, dcv = run(attend_back, dco, cq, ck, cv, cp, batch)
+    g_low.two()
+    g_high.one()
+    g_cross = total(*run(grads_of, act2, [e, co], [dcq, dck, dcv, dcross], (0, 1, 1, 2), "cross_grads"))
+    g_cross.core()
+    g_low.ring()
+    dmid1, dself, dao, sums2 = run(cross_back, dcq, mid1, dmid2, vecs, cross_w, self_w, m)
+    g_high.two()
+    dq, dk, dv = run(attend_back, dao, q, k, v, p, batch)
+    g_cross.one()
+    g_high.ring()
+    g_self = total(*run(grads_of, act1, [o], [dq, dk, dv, dself], (0, 0, 0, 1), "self_grads"))
+    g_self.core()
+    g_cross.two()
+    encoder_grad, sums_e = run(memory_back, dck, dcv, cross_w, m)
+    g_self.one()
+    g_cross.ring()
+    input_grad, sums1 = run(self_back, dq, dk, dv, x, dmid1, vecs, self_w, m)
+    g_self.two()
+
+    def by_shard(v):
+        return v.reshape(-1, rows, m).transpose(1, 0, 2)
+
+    dbe = jnp.concatenate([dbe_low, dbe_high]).reshape(4, d)
+    sums = by_shard(jnp.concatenate([sums1[:4], sums2[:4], sums3[:4], sums_e[:1], dbe]))
+    sums = (sums.astype(BF).astype(F32) + order.send(place.core, sums.astype(BF)).astype(F32)).astype(BF)
+    g_low.last_x()
+    g_high.last_x()
+    sums = (sums.astype(F32) + order.send(place.across, sums).astype(F32)).astype(BF)
+    g_self.ring()
+    g_low.last_core()
+    g_high.last_core()
+    sums = sums.reshape((place.ring, 2) + sums.shape[1:])
+    came = order.send(place.pair, at(sums, 1 - place.y, 1))
+    sums = (at(sums, place.y, 1).astype(F32) + came.astype(F32)).astype(BF)
+    g_expand, g_down = finish(g_low.parts, g_high.parts)
+    g_cross.last_x()
+    sums = order.swap(partial(ring_sum, place), sums).astype(F32)
+    g_cross.last_core()
+    g_cq, g_ck, g_cv, g_co = finish(g_cross.parts)
+    g_self.last_x()
+    g_self.last_core()
+    g_sq, g_sk, g_sv, g_so = finish(g_self.parts)
+    return (
+        layer_out.reshape(batch, seq, d),
+        input_grad.reshape(batch, seq, d),
+        encoder_grad.reshape(encoder_out.shape),
+        g_sq, g_sk, g_sv, g_so,
+        sums[2], sums[3], sums[7],
+        g_cq, g_ck, g_cv, g_co,
+        sums[6], sums[12], sums[11],
+        g_expand, sums[13:].reshape(-1), g_down, sums[10],
+        sums[0], sums[1], sums[4], sums[5], sums[8], sums[9],
+    )
+
+
 def solution(mesh):
     groups, rows = mesh.shape["replica"], mesh.shape["fsdp"]
     data = P(("replica", "fsdp"), None, None)
@@ -572,7 +1476,7 @@
         (mat,) * 4 + (vec,) * 3 + (mat,) * 4 + (vec,) * 3 + (mat, vec, mat, vec) + (vec,) * 6
     )
     return jax.shard_map(
-        partial(body, groups, rows),
+        partial(fast_body if rows == 8 else body, groups, rows),
         mesh=mesh,
         in_specs=(data, data, P(("replica", "fsdp")), data) + weights,
         out_specs=(data, data, data) + weights,

time: 942 us -> 619 us (0.66)
  matrix products: 166 us -> 0 us
  Pallas kernels: 96.6 us -> 250 us
  local copies, waits for them, and re-layouts: 169 us -> 57.4 us
  starting transfers between devices: 156 us -> 76.7 us
  other arithmetic: 144 us -> 65 us
  waiting for transfers between devices: 193 us -> 117 us
  blocking collectives: 0 us -> 41.2 us
    dot_general x51 -> x0, matrix products: 166 us -> none  [the longest x31 79.7 us: product_t(): lax.dot_general(left, right, (((0,), (0,)), ((), ())), preferred_element_...]
    pallas_call x9 -> x16, Pallas kernels: 37.3 us -> 192 us  [the longest x2 63.8 us: ffn(): pl.pallas_call(partial(ffn_kernel, last, first_row), grid=(4,), in_specs=...]
    all_to_all x14 -> x4, starting transfers between devices: 65 us -> 18.9 us  [ring_sum(): lax.all_to_all(parts, 'fsdp', 0, 0, axis_index_groups=place.ring_members())]
    reshape x49 -> x6, local copies, waits for them, and re-layouts: 49.1 us -> 3.7 us  [the longest x2 2.86 us: fast_body(): expand_weight.reshape(m, rows, 4, -1).transpose(2, 0, 1, 3).reshape(4, m, d)]
    all_to_all x0 -> x2, blocking collectives: none -> 41.2 us  [the longest x1 32.4 us: ring_gather(): lax.all_to_all(copies, 'fsdp', 0, 0, axis_index_groups=place.ring_members())]
    ppermute x17 -> x21, waiting for transfers between devices: 79.5 us -> 41.9 us  [across(): return lax.ppermute(v, 'replica', [(i, i ^ 2) for i in range(self.groups)])]
    all_to_all x10 -> x3, waiting for transfers between devices: 35.3 us -> 0.01 us  [ring_gather(): lax.all_to_all(copies, 'fsdp', 0, 0, axis_index_groups=place.ring_members())]
    all_to_all x10 -> x3, starting transfers between devices: 45.5 us -> 13.8 us  [ring_gather(): lax.all_to_all(copies, 'fsdp', 0, 0, axis_index_groups=place.ring_members())]
  transfers between devices with their start and end apart: 90 -> 70, of which waited for: 30 -> 22; matrix products, arithmetic and copies ran while one was open for 44% -> 14% of each run, Pallas kernels for 10% -> 35%
where the time goes in v2:
time: 619 us; the launch traced here: 610 us
  Pallas kernels  250 us (40%)
  waiting for transfers between devices  117 us (19%)
  starting transfers between devices  76.7 us (12%)
  other arithmetic  65 us (11%)
  local copies, waits for them, and re-layouts  57.4 us (9%)
  blocking collectives  41.2 us (7%)
    ppermute x17, waiting for transfers between devices, pair(): return lax.ppermute(v, 'fsdp', [(i, i ^ 1) for i in range(self.rows)])  66.2 us
    pallas_call x2, Pallas kernels, ffn(): pl.pallas_call(partial(ffn_kernel, last, first_row), grid=(4,), in_specs=...  63.8 us
    ppermute x21, waiting for transfers between devices, across(): return lax.ppermute(v, 'replica', [(i, i ^ 2) for i in range(self.groups)])  41.9 us
    pallas_call x2, Pallas kernels, grads(): pl.pallas_call(partial(grads_kernel, sides), in_specs=[WHOLE] * (len(left...  33.3 us
    all_to_all x1, blocking collectives, ring_gather(): lax.all_to_all(copies, 'fsdp', 0, 0, axis_index_groups=place.ring_members())  32.4 us
    convert_element_type x12, other arithmetic, low_sum(): return total.astype(BF)  31.6 us
    pallas_call x2, Pallas kernels, attend_back(): pl.pallas_call(partial(attend_back_kernel, (d // H) ** (-0.5)), grid=(bat...  30.7 us
    unnamed x187, local copies, waits for them, and re-layouts  29.9 us
  transfers between devices with their start and end apart: 70, of which 22 were waited for; matrix products, arithmetic and copies ran while one was open for 14% of the time, Pallas kernels for 35%

profile of v2, /device:TPU:0, one launch (start us, length us, event | category | flops | bytes accessed | tf_op | source)
XLA Modules:
  0.0 609.7 jit_solution(8481140775535565574)
XLA Ops:
  13.6 32.4 %all_to_all.45 = bf16[4,2,136,512]{3,2,1,0:T(8,128)(2,1)S(1)} all-to-all(bf16[4,2,136,512]{3,2,1,0:T(8,128)(2,1)S(1)} %broadcast_in_dim.8), channel_id=1, replica_groups={{0,2,4,6},{1,3,5,7},{8,10,12,14},{9,11,13,15},{16,18,20,22},{17,19,21,2..., dimensions={0} | all-to-all | bytes 2228224 | tf_op jit(solution)/shard_map/all_to_all | solution.py:66
  69.4 18.4 %collective-permute-done.3.rest_3_.rest_11_ = bf16[2,4,136,512]{3,2,1,0:T(8,128)(2,1)} collective-permute-done((bf16[2,4,136,512]{3,2,1,0:T(8,128)(2,1)S(1)}, bf16[2,4,136,512]{3,2,1,0:T(8,128)(2,1)}, u32[]{:S(2)}, u32[]{:S(2)}) %collective-permute-start.3) | collective-permute-done | bytes 1114144 | tf_op jit(solution)/shard_map/ppermute | solution.py:37
  105.2 10.5 %collective-permute-done.8 = bf16[4,128,512]{2,1,0:T(8,128)(2,1)} collective-permute-done((bf16[4,128,512]{2,1,0:T(8,128)(2,1)}, bf16[4,128,512]{2,1,0:T(8,128)(2,1)}, u32[]{:S(2)}, u32[]{:S(2)}) %collective-permute-start.8) | collective-permute-done | bytes 524320 | tf_op jit(solution)/shard_map/ppermute | solution.py:37
  117.1 10.2 %first.1 = (bf16[512,1024]{1,0:T(8,128)(2,1)}, bf16[512,1024]{1,0:T(8,128)(2,1)}, bf16[512,1024]{1,0:T(8,128)(2,1)}, bf16[512,1024]{1,0:T(8,128)(2,1)}) custom-call(bf16[512,1024]{1,0:T(8,128)(2,1)} %bitcast.355, f32[17,1024]{1,0:T(8,128)} %bitcast.358, bf16[2,4,136,512]{3,2,1,0:T(8,128)(2,1)} %copy-done.27, ...), custom_call_target="tpu_custom_call" | custom-call | flops 3221225472 | bytes 14155776 | tf_op jit(solution)/shard_map/first/pallas_call | solution.py:497
  135.4 10.3 %attend.2 = (bf16[512,1024]{1,0:T(8,128)(2,1)S(1)}, bf16[2,16,256,256]{3,2,1,0:T(8,128)(2,1)S(1)}) custom-call(s32[2]{0:T(128)S(1)} %copy-done.10, bf16[512,1024]{1,0:T(8,128)(2,1)S(1)} %copy-done.11, bf16[512,1024]{1,0:T(8,128)(2,1)S(1)} %copy-done.13, bf16[512,1024]{1,0:T(8,128)(2,1)S(1)} %copy-done.15), custom_call_target="tpu_custom_call" | custom-call | flops 2147483648 | bytes 8388608 | tf_op jit(solution)/shard_map/attend/pallas_call | solution.py:289
  162.4 7.4 %self_out.1 = (f32[512,1024]{1,0:T(8,128)}, bf16[512,1024]{1,0:T(8,128)(2,1)}) custom-call(bf16[512,1024]{1,0:T(8,128)(2,1)} %copy-done.4, bf16[512,1024]{1,0:T(8,128)(2,1)} %bitcast.356, f32[17,1024]{1,0:T(8,128)} %bitcast.359, bf16[2,4,136,512]{3,2,1,0:T(8,128)(2,1)} %copy-done.27, bf16[2,4,136,512]{3,2,1,0:T(8,128)(2,1)} %collective-permute-done.2.rest_1_.rest_9_, ...), custom_call_target="tpu_custom_call" | custom-call | flops 1073741824 | bytes 10747904 | tf_op jit(solution)/shard_map/self_out/pallas_call | solution.py:544
  175.8 12.1 %memory.1 = (bf16[1024,1024]{1,0:T(8,128)(2,1)}, bf16[1024,1024]{1,0:T(8,128)(2,1)}) custom-call(bf16[1024,1024]{1,0:T(8,128)(2,1)} %bitcast.403, f32[17,1024]{1,0:T(8,128)} %bitcast.360, bf16[2,4,128,512]{3,2,1,0:T(8,128)(2,1)} %copy-done.24, bf16[2,4,128,512]{3,2,1,0:T(8,128)(2,1)} %copy-done.28, bf16[2,4,128,512]{3,2,1,0:T(8,128)(2,1)} %copy-done.25, ...), custom_call_target="tpu_custom_call" | custom-call | flops 4294967296 | bytes 14680064 | tf_op jit(solution)/shard_map/memory/pallas_call | solution.py:603
  204.9 17.7 %attend.3 = (bf16[512,1024]{1,0:T(8,128)(2,1)S(1)}, bf16[2,16,256,512]{3,2,1,0:T(8,128)(2,1)}) custom-call(s32[2]{0:T(128)S(1)} %copy-done.10, bf16[512,1024]{1,0:T(8,128)(2,1)S(1)} %copy-done, bf16[1024,1024]{1,0:T(8,128)(2,1)S(1)} %copy-done.21, bf16[1024,1024]{1,0:T(8,128)(2,1)S(1)} %copy-done.22), custom_call_target="tpu_custom_call" | custom-call | flops 4294967296 | bytes 14680064 | tf_op jit(solution)/shard_map/attend/pallas_call | solution.py:289
  226.4 7.7 %cross_out.1 = (f32[512,1024]{1,0:T(8,128)}, bf16[512,1024]{1,0:T(8,128)(2,1)}) custom-call(bf16[512,1024]{1,0:T(8,128)(2,1)} %copy-done.5, f32[512,1024]{1,0:T(8,128)} %get-tuple-element.184.res_ref.mid_ref, f32[17,1024]{1,0:T(8,128)} %bitcast.362, bf16[2,4,128,512]{3,2,1,0:T(8,128)(2,1)} %copy-done.24, bf16[2,4,128,512]{3,2,1,0:T(8,128)(2,1)} %copy-done.28, ...), custom_call_target="tpu_custom_call" | custom-call | flops 1073741824 | bytes 10485760 | tf_op jit(solution)/shard_map/cross_out/pallas_call | solution.py:544
  234.1 27.0 %ffn.2 = (f32[512,1024]{1,0:T(8,128)}, f32[512,1024]{1,0:T(8,128)}, f32[4,1,512]{2,1,0:T(1,128)}, bf16[2,2,2,4,128,512]{5,4,3,2,1,0:T(8,128)(2,1)}, bf16[2,2,2,4,128,512]{5,4,3,2,1,0:T(8,128)(2,1)}) custom-call(bf16[512,1024]{1,0:T(8,128)(2,1)} %get-tuple-element.212.act_ref, bf16[512,1024]{1,0:T(8,128)(2,1)} %bitcast.406, ...), custom_call_target="tpu_custom_call" | custom-call | flops 12884901888 | bytes 20971520 | tf_op jit(solution)/shard_map/ffn/pallas_call | solution.py:948
  267.9 36.8 %ffn.3 = (bf16[512,1024]{1,0:T(8,128)(2,1)}, f32[512,1024]{1,0:T(8,128)}, bf16[512,1024]{1,0:T(8,128)(2,1)}, f32[8,1024]{1,0:T(8,128)}, f32[4,1,512]{2,1,0:T(1,1...) custom-call(bf16[512,1024]{1,0:T(8,128)(2,1)} %get-tuple-element.212.act_ref, ...), custom_call_target="tpu_custom_call" | custom-call | flops 12884901888 | bytes 20971520 | tf_op jit(solution)/shard_map/ffn/pallas_call | solution.py:948
  320.5 17.5 %attend_back.2 = (bf16[512,1024]{1,0:T(8,128)(2,1)S(1)}, bf16[1024,1024]{1,0:T(8,128)(2,1)S(1)}, bf16[1024,1024]{1,0:T(8,128)(2,1)S(1)}) custom-call(bf16[512,1024]{1,0:T(8,128)(2,1)S(1)} %copy-done.3, bf16[512,1024]{1,0:T(8,128)(2,1)S(1)} %copy-done.1, bf16[1024,1024]{1,0:T(8,128)(2,1)S(1)} %copy-done.21, bf16[1024,1024]{1,0:T(8,128)(2,1)S(1)} %copy-done.23, ...), custom_call_target="tpu_custom_call" | custom-call | flops 8589934592 | bytes 19922944 | tf_op jit(solution)/shard_map/attend_back/pallas_call | solution.py:341
  346.4 18.7 %cross_grads.1 = (bf16[2,2,2,4,128,512]{5,4,3,2,1,0:T(8,128)(2,1)}, bf16[2,2,2,4,128,512]{5,4,3,2,1,0:T(8,128)(2,1)}) custom-call(bf16[512,1024]{1,0:T(8,128)(2,1)} %get-tuple-element.229.a_ref.rest_0_, bf16[1024,1024]{1,0:T(8,128)(2,1)} %bitcast.404, bf16[512,1024]{1,0:T(8,128)(2,1)} %copy-done.5, bf16[512,1024]{1,0:T(8,128)(2,1)} %copy-done.2, ...), custom_call_target="tpu_custom_call" | custom-call | flops 6442450944 | bytes 23068672 | tf_op jit(solution)/shard_map/cross_grads/pallas_call | solution.py:814
  369.3 10.7 %collective-permute-done.37 = bf16[4,128,512]{2,1,0:T(8,128)(2,1)S(1)} collective-permute-done((bf16[4,128,512]{2,1,0:T(8,128)(2,1)S(1)}, bf16[4,128,512]{2,1,0:T(8,128)(2,1)S(1)}, u32[]{:S(2)}, u32[]{:S(2)}) %collective-permute-start.37) | collective-permute-done | bytes 524320 | tf_op jit(solution)/shard_map/ppermute | solution.py:34
  383.4 11.8 %cross_back.1 = (f32[512,1024]{1,0:T(8,128)}, bf16[512,1024]{1,0:T(8,128)(2,1)}, bf16[512,1024]{1,0:T(8,128)(2,1)}, f32[8,1024]{1,0:T(8,128)}) custom-call(bf16[512,1024]{1,0:T(8,128)(2,1)} %copy-done.2, f32[512,1024]{1,0:T(8,128)} %get-tuple-element.184.res_ref.mid_ref, f32[512,1024]{1,0:T(8,128)} %get-tuple-element.236.dmid_ref, f32[17,1024]{1,0:T(8,128)} %bitcast.365, ...), custom_call_target="tpu_custom_call" | custom-call | flops 2147483648 | bytes 13631488 | tf_op jit(solution)/shard_map/cross_back/pallas_call | solution.py:693
  395.2 7.7 %collective-permute-done.39 = bf16[2,4,128,512]{3,2,1,0:T(8,128)(2,1)} collective-permute-done((bf16[2,4,128,512]{3,2,1,0:T(8,128)(2,1)}, bf16[2,4,128,512]{3,2,1,0:T(8,128)(2,1)}, u32[]{:S(2)}, u32[]{:S(2)}) %collective-permute-start.39) | collective-permute-done | bytes 1048608 | tf_op jit(solution)/shard_map/ppermute | solution.py:37
  407.6 13.2 %attend_back.3 = (bf16[512,1024]{1,0:T(8,128)(2,1)S(1)}, bf16[512,1024]{1,0:T(8,128)(2,1)S(1)}, bf16[512,1024]{1,0:T(8,128)(2,1)S(1)}) custom-call(bf16[512,1024]{1,0:T(8,128)(2,1)S(1)} %copy-done.9, bf16[512,1024]{1,0:T(8,128)(2,1)S(1)} %copy-done.12, bf16[512,1024]{1,0:T(8,128)(2,1)S(1)} %copy-done.14, bf16[512,1024]{1,0:T(8,128)(2,1)S(1)} %copy-done.16, ...), custom_call_target="tpu_custom_call" | custom-call | flops 4294967296 | bytes 11534336 | tf_op jit(solution)/shard_map/attend_back/pallas_call | solution.py:341
  430.6 14.6 %self_grads.1 = (bf16[2,2,2,4,128,512]{5,4,3,2,1,0:T(8,128)(2,1)}, bf16[2,2,2,4,128,512]{5,4,3,2,1,0:T(8,128)(2,1)}) custom-call(bf16[512,1024]{1,0:T(8,128)(2,1)} %get-tuple-element.248.rest_0_, bf16[512,1024]{1,0:T(8,128)(2,1)} %copy-done.4, bf16[512,1024]{1,0:T(8,128)(2,1)} %copy-done.6, bf16[512,1024]{1,0:T(8,128)(2,1)} %copy-done.7, ...), custom_call_target="tpu_custom_call" | custom-call | flops 4294967296 | bytes 14680064 | tf_op jit(solution)/shard_map/self_grads/pallas_call | solution.py:814
  455.2 16.0 %collective-permute-done.45 = bf16[2,4,128,512]{3,2,1,0:T(8,128)(2,1)} collective-permute-done((bf16[2,4,128,512]{3,2,1,0:T(8,128)(2,1)}, bf16[2,4,128,512]{3,2,1,0:T(8,128)(2,1)}, u32[]{:S(2)}, u32[]{:S(2)}) %collective-permute-start.45) | collective-permute-done | bytes 1048608 | tf_op jit(solution)/shard_map/ppermute | solution.py:37
  476.7 11.5 %memory_back.1 = (f32[1024,1024]{1,0:T(8,128)}, f32[8,1024]{1,0:T(8,128)}) custom-call(bf16[1024,1024]{1,0:T(8,128)(2,1)} %copy-done.17, bf16[1024,1024]{1,0:T(8,128)(2,1)} %copy-done.18, bf16[2,4,128,512]{3,2,1,0:T(8,128)(2,1)} %copy-done.24, bf16[2,4,128,512]{3,2,1,0:T(8,128)(2,1)} %copy-done.28, bf16[2,4,128,512]{3,2,1,0:T(8,128)(2,1)} %copy-done.25, ...), custom_call_target="tpu_custom_call" | custom-call | flops 4294967296 | bytes 16777216 | tf_op jit(solution)/shard_map/memory_back/pallas_call | solution.py:637
  503.6 12.9 %self_back.1 = (f32[512,1024]{1,0:T(8,128)}, f32[8,1024]{1,0:T(8,128)}) custom-call(bf16[512,1024]{1,0:T(8,128)(2,1)} %copy-done.6, bf16[512,1024]{1,0:T(8,128)(2,1)} %copy-done.7, bf16[512,1024]{1,0:T(8,128)(2,1)} %copy-done.8, bf16[512,1024]{1,0:T(8,128)(2,1)} %bitcast.357, f32[512,1024]{1,0:T(8,128)} %get-tuple-element.238.dmid_ref, ...), custom_call_target="tpu_custom_call" | custom-call | flops 3221225472 | bytes 17301504 | tf_op jit(solution)/shard_map/self_back/pallas_call | solution.py:730
  529.4 8.4 %collective-permute-done.49 = bf16[4,128,512]{2,1,0:T(8,128)(2,1)} collective-permute-done((bf16[4,128,512]{2,1,0:T(8,128)(2,1)}, bf16[4,128,512]{2,1,0:T(8,128)(2,1)}, u32[]{:S(2)}, u32[]{:S(2)}) %collective-permute-start.49) | collective-permute-done | bytes 524320 | tf_op jit(solution)/shard_map/ppermute | solution.py:37
  545.3 7.4 %collective-permute-done.51 = bf16[4,128,512]{2,1,0:T(8,128)(2,1)} collective-permute-done((bf16[4,128,512]{2,1,0:T(8,128)(2,1)}, bf16[4,128,512]{2,1,0:T(8,128)(2,1)}, u32[]{:S(2)}, u32[]{:S(2)}) %collective-permute-start.51) | collective-permute-done | bytes 524320 | tf_op jit(solution)/shard_map/ppermute | solution.py:34
  589.2 8.8 %all_to_all.46 = bf16[4,17,128]{2,1,0:T(8,128)(2,1)S(1)} all-to-all(bf16[4,17,128]{2,1,0:T(8,128)(2,1)S(1)} %copy.161), channel_id=1, replica_groups={{0,2,4,6},{1,3,5,7},{8,10,12,14},{9,11,13,15},{16,18,20,22},{17,19,21,2..., dimensions={0} | all-to-all | bytes 34816 | tf_op jit(solution)/shard_map/all_to_all | solution.py:177
  (413 shorter events, 257.3 us)
Async XLA Ops:
  58.5 32.2 %all-to-all-start.1 = ((bf16[4,2,128,512]{3,2,1,0:T(8,128)(2,1)}), bf16[4,2,128,512]{3,2,1,0:T(8,128)(2,1)}, u32[]{:S(2)}, u32[]{:S(2)}) async-start(bf16[4,2,128,512]{3,2,1,0:T(8,128)(2,1)} %broadcast_in_dim.9), calls=%async_computation.1 | async-start | bytes 2097152 | tf_op jit(solution)/shard_map/all_to_all | solution.py:66
  67.1 34.0 %collective-permute-start.4 = (bf16[2,4,136,512]{3,2,1,0:T(8,128)(2,1)S(1)}, bf16[2,4,136,512]{3,2,1,0:T(8,128)(2,1)S(1)}, u32[]{:S(2)}, u32[]{:S(2)}) collective-permute-start(bf16[2,4,136,512]{3,2,1,0:T(8,128)(2,1)S(1)} %pad_maximum_fusion.rest_0_.rest_8_), channel_id=1, source_target_pairs={{0,8},{8,0},{16,24},{24,16},{1,9},{9,1},{17,25},{25,17},{2,10},{10... | collective-permute-start | bytes 3342344 | tf_op jit(solution)/shard_map/ppermute | solution.py:31
  68.9 48.1 %collective-permute-start.6 = (bf16[2,4,136,512]{3,2,1,0:T(8,128)(2,1)S(1)}, bf16[2,4,136,512]{3,2,1,0:T(8,128)(2,1)}, u32[]{:S(2)}, u32[]{:S(2)}) collective-permute-start(bf16[2,4,136,512]{3,2,1,0:T(8,128)(2,1)S(1)} %pad_maximum_fusion.1.rest_2_.rest_10_), channel_id=1, source_target_pairs={{0,8},{8,0},{16,24},{24,16},{1,9},{9,1},{17,25},{25,17},{2,10},{10... | collective-permute-start | bytes 3342344 | tf_op jit(solution)/shard_map/ppermute | solution.py:31
  90.1 26.9 %collective-permute-start.7 = (bf16[2,4,136,512]{3,2,1,0:T(8,128)(2,1)}, bf16[2,4,136,512]{3,2,1,0:T(8,128)(2,1)}, u32[]{:S(2)}, u32[]{:S(2)}) collective-permute-start(bf16[2,4,136,512]{3,2,1,0:T(8,128)(2,1)} %collective-permute-done.3.rest_3_.rest_11_), channel_id=1, source_target_pairs={{0,8},{8,0},{16,24},{24,16},{1,9},{9,1},{17,25},{25,17},{2,10},{10... | collective-permute-start | bytes 3342344 | tf_op jit(solution)/shard_map/ppermute | solution.py:31
  90.1 26.9 %collective-permute-start.5 = (bf16[2,4,136,512]{3,2,1,0:T(8,128)(2,1)}, bf16[2,4,136,512]{3,2,1,0:T(8,128)(2,1)}, u32[]{:S(2)}, u32[]{:S(2)}) collective-permute-start(bf16[2,4,136,512]{3,2,1,0:T(8,128)(2,1)} %collective-permute-done.2.rest_1_.rest_9_), channel_id=1, source_target_pairs={{0,8},{8,0},{16,24},{24,16},{1,9},{9,1},{17,25},{25,17},{2,10},{10... | collective-permute-start | bytes 3342344 | tf_op jit(solution)/shard_map/ppermute | solution.py:31
  92.7 58.6 %all-to-all-start.2 = ((bf16[4,2,128,512]{3,2,1,0:T(8,128)(2,1)}), bf16[4,2,128,512]{3,2,1,0:T(8,128)(2,1)}, u32[]{:S(2)}, u32[]{:S(2)}) async-start(bf16[4,2,128,512]{3,2,1,0:T(8,128)(2,1)} %broadcast_in_dim.10), calls=%async_computation.2 | async-start | bytes 2097152 | tf_op jit(solution)/shard_map/all_to_all | solution.py:66
  101.2 27.3 %collective-permute-start.9 = (bf16[4,128,512]{2,1,0:T(8,128)(2,1)}, bf16[4,128,512]{2,1,0:T(8,128)(2,1)}, u32[]{:S(2)}, u32[]{:S(2)}) collective-permute-start(bf16[4,128,512]{2,1,0:T(8,128)(2,1)} %get-tuple-element.165), channel_id=1, source_target_pairs={{0,16},{8,24},{16,0},{24,8},{1,17},{9,25},{17,1},{25,9},{2,18},{10... | collective-permute-start | bytes 1572872 | tf_op jit(solution)/shard_map/ppermute | solution.py:34
  131.2 40.8 %collective-permute-start.14 = (bf16[2,4,128,512]{3,2,1,0:T(8,128)(2,1)S(1)}, bf16[2,4,128,512]{3,2,1,0:T(8,128)(2,1)}, u32[]{:S(2)}, u32[]{:S(2)}) collective-permute-start(bf16[2,4,128,512]{3,2,1,0:T(8,128)(2,1)S(1)} %pad_maximum_fusion.3.rest_2_), channel_id=1, source_target_pairs={{0,8},{8,0},{16,24},{24,16},{1,9},{9,1},{17,25},{25,17},{2,10},{10... | collective-permute-start | bytes 3145736 | tf_op jit(solution)/shard_map/ppermute | solution.py:31
  157.8 41.9 %all-to-all-start.3 = ((bf16[4,2,128,512]{3,2,1,0:T(8,128)(2,1)}), bf16[4,2,128,512]{3,2,1,0:T(8,128)(2,1)S(1)}, u32[]{:S(2)}, u32[]{:S(2)}) async-start(bf16[4,2,128,512]{3,2,1,0:T(8,128)(2,1)} %broadcast_in_dim.11), calls=%async_computation.3 | async-start | bytes 2097152 | tf_op jit(solution)/shard_map/all_to_all | solution.py:66
  223.9 37.3 %collective-permute-start.27 = (bf16[2,4,128,512]{3,2,1,0:T(8,128)(2,1)S(1)}, bf16[2,4,128,512]{3,2,1,0:T(8,128)(2,1)S(1)}, u32[]{:S(2)}, u32[]{:S(2)}) collective-permute-start(bf16[2,4,128,512]{3,2,1,0:T(8,128)(2,1)S(1)} %pad_maximum_fusion.7.rest_4_), channel_id=1, source_target_pairs={{0,1},{1,0},{2,3},{3,2},{4,5},{5,4},{6,7},{7,6},{8,9},{9,8},{10,11... | collective-permute-start | bytes 3145736 | tf_op jit(solution)/shard_map/ppermute | solution.py:37
  225.4 35.8 %collective-permute-start.26 = (bf16[2,4,128,512]{3,2,1,0:T(8,128)(2,1)S(1)}, bf16[2,4,128,512]{3,2,1,0:T(8,128)(2,1)}, u32[]{:S(2)}, u32[]{:S(2)}) collective-permute-start(bf16[2,4,128,512]{3,2,1,0:T(8,128)(2,1)S(1)} %pad_maximum_fusion.6.rest_2_), channel_id=1, source_target_pairs={{0,16},{8,24},{16,0},{24,8},{1,17},{9,25},{17,1},{25,9},{2,18},{10... | collective-permute-start | bytes 3145736 | tf_op jit(solution)/shard_map/ppermute | solution.py:34
  225.9 35.9 %collective-permute-start.30 = (bf16[2,4,128,512]{3,2,1,0:T(8,128)(2,1)S(1)}, bf16[2,4,128,512]{3,2,1,0:T(8,128)(2,1)}, u32[]{:S(2)}, u32[]{:S(2)}) collective-permute-start(bf16[2,4,128,512]{3,2,1,0:T(8,128)(2,1)S(1)} %pad_maximum_fusion.7.rest_4_), channel_id=1, source_target_pairs={{0,8},{8,0},{16,24},{24,16},{1,9},{9,1},{17,25},{25,17},{2,10},{10... | collective-permute-start | bytes 3145736 | tf_op jit(solution)/shard_map/ppermute | solution.py:31
  225.9 35.9 %collective-permute-start.28 = (bf16[2,4,128,512]{3,2,1,0:T(8,128)(2,1)S(1)}, bf16[2,4,128,512]{3,2,1,0:T(8,128)(2,1)}, u32[]{:S(2)}, u32[]{:S(2)}) collective-permute-start(bf16[2,4,128,512]{3,2,1,0:T(8,128)(2,1)S(1)} %pad_maximum_fusion.6.rest_2_), channel_id=1, source_target_pairs={{0,8},{8,0},{16,24},{24,16},{1,9},{9,1},{17,25},{25,17},{2,10},{10... | collective-permute-start | bytes 3145736 | tf_op jit(solution)/shard_map/ppermute | solution.py:31
  261.8 43.4 %collective-permute-start.32 = (bf16[2,2,2,4,128,512]{5,4,3,2,1,0:T(8,128)(2,1)}, bf16[2,2,2,4,128,512]{5,4,3,2,1,0:T(8,128)(2,1)}, u32[]{:S(2)}, u32[]{:S(2)}) collective-permute-start(bf16[2,2,2,4,128,512]{5,4,3,2,1,0:T(8,128)(2,1)} %get-tuple-element.211), channel_id=1, source_target_pairs={{0,8},{8,0},{16,24},{24,16},{1,9},{9,1},{17,25},{25,17},{2,10},{10... | collective-permute-start | bytes 12582920 | tf_op jit(solution)/shard_map/ppermute | solution.py:31
  304.7 33.3 %collective-permute-start.35 = (bf16[2,2,2,4,128,512]{5,4,3,2,1,0:T(8,128)(2,1)}, bf16[2,2,2,4,128,512]{5,4,3,2,1,0:T(8,128)(2,1)}, u32[]{:S(2)}, u32[]{:S(2)}) collective-permute-start(bf16[2,2,2,4,128,512]{5,4,3,2,1,0:T(8,128)(2,1)} %get-tuple-element.220), channel_id=1, source_target_pairs={{0,8},{8,0},{16,24},{24,16},{1,9},{9,1},{17,25},{25,17},{2,10},{10... | collective-permute-start | bytes 12582920 | tf_op jit(solution)/shard_map/ppermute | solution.py:31
  309.8 34.6 %collective-permute-start.34 = (bf16[2,4,128,512]{3,2,1,0:T(8,128)(2,1)}, bf16[2,4,128,512]{3,2,1,0:T(8,128)(2,1)}, u32[]{:S(2)}, u32[]{:S(2)}) collective-permute-start(bf16[2,4,128,512]{3,2,1,0:T(8,128)(2,1)} %fusion.1), channel_id=1, source_target_pairs={{0,1},{1,0},{2,3},{3,2},{4,5},{5,4},{6,7},{7,6},{8,9},{9,8},{10,11... | collective-permute-start | bytes 3145736 | tf_op jit(solution)/shard_map/ppermute | solution.py:37
  311.0 33.4 %collective-permute-start.33 = (bf16[2,4,128,512]{3,2,1,0:T(8,128)(2,1)S(1)}, bf16[2,4,128,512]{3,2,1,0:T(8,128)(2,1)}, u32[]{:S(2)}, u32[]{:S(2)}) collective-permute-start(bf16[2,4,128,512]{3,2,1,0:T(8,128)(2,1)S(1)} %fusion), channel_id=1, source_target_pairs={{0,16},{8,24},{16,0},{24,8},{1,17},{9,25},{17,1},{25,9},{2,18},{10... | collective-permute-start | bytes 3145736 | tf_op jit(solution)/shard_map/ppermute | solution.py:34
  365.1 60.5 %collective-permute-start.40 = (bf16[2,2,2,4,128,512]{5,4,3,2,1,0:T(8,128)(2,1)}, bf16[2,2,2,4,128,512]{5,4,3,2,1,0:T(8,128)(2,1)}, u32[]{:S(2)}, u32[]{:S(2)}) collective-permute-start(bf16[2,2,2,4,128,512]{5,4,3,2,1,0:T(8,128)(2,1)} %get-tuple-element.233), channel_id=1, source_target_pairs={{0,8},{8,0},{16,24},{24,16},{1,9},{9,1},{17,25},{25,17},{2,10},{10... | collective-permute-start | bytes 12582920 | tf_op jit(solution)/shard_map/ppermute | solution.py:31
  367.3 35.7 %collective-permute-start.39 = (bf16[2,4,128,512]{3,2,1,0:T(8,128)(2,1)}, bf16[2,4,128,512]{3,2,1,0:T(8,128)(2,1)}, u32[]{:S(2)}, u32[]{:S(2)}) collective-permute-start(bf16[2,4,128,512]{3,2,1,0:T(8,128)(2,1)} %fusion.3), channel_id=1, source_target_pairs={{0,1},{1,0},{2,3},{3,2},{4,5},{5,4},{6,7},{7,6},{8,9},{9,8},{10,11... | collective-permute-start | bytes 3145736 | tf_op jit(solution)/shard_map/ppermute | solution.py:37
  368.4 34.5 %collective-permute-start.38 = (bf16[2,4,128,512]{3,2,1,0:T(8,128)(2,1)}, bf16[2,4,128,512]{3,2,1,0:T(8,128)(2,1)}, u32[]{:S(2)}, u32[]{:S(2)}) collective-permute-start(bf16[2,4,128,512]{3,2,1,0:T(8,128)(2,1)} %fusion.2), channel_id=1, source_target_pairs={{0,16},{8,24},{16,0},{24,8},{1,17},{9,25},{17,1},{25,9},{2,18},{10... | collective-permute-start | bytes 3145736 | tf_op jit(solution)/shard_map/ppermute | solution.py:34
  445.2 43.0 %collective-permute-start.43 = (bf16[2,2,2,4,128,512]{5,4,3,2,1,0:T(8,128)(2,1)}, bf16[2,2,2,4,128,512]{5,4,3,2,1,0:T(8,128)(2,1)}, u32[]{:S(2)}, u32[]{:S(2)}) collective-permute-start(bf16[2,2,2,4,128,512]{5,4,3,2,1,0:T(8,128)(2,1)} %get-tuple-element.254), channel_id=1, source_target_pairs={{0,8},{8,0},{16,24},{24,16},{1,9},{9,1},{17,25},{25,17},{2,10},{10... | collective-permute-start | bytes 12582920 | tf_op jit(solution)/shard_map/ppermute | solution.py:31
  448.1 44.4 %all-to-all-start.5 = ((bf16[4,2,128,512]{3,2,1,0:T(8,128)(2,1)}), bf16[4,2,128,512]{3,2,1,0:T(8,128)(2,1)S(1)}, u32[]{:S(2)}, u32[]{:S(2)}) async-start(bf16[4,2,128,512]{3,2,1,0:T(8,128)(2,1)} %copy.157), calls=%async_computation.5 | async-start | bytes 2097152 | tf_op jit(solution)/shard_map/all_to_all | solution.py:177
  492.5 29.5 %all-to-all-start.6 = ((bf16[4,2,128,512]{3,2,1,0:T(8,128)(2,1)}), bf16[4,2,128,512]{3,2,1,0:T(8,128)(2,1)S(1)}, u32[]{:S(2)}, u32[]{:S(2)}) async-start(bf16[4,2,128,512]{3,2,1,0:T(8,128)(2,1)} %copy.158), calls=%async_computation.6 | async-start | bytes 2097152 | tf_op jit(solution)/shard_map/all_to_all | solution.py:177
  522.0 33.8 %all-to-all-start.8 = ((bf16[4,2,128,512]{3,2,1,0:T(8,128)(2,1)}), bf16[4,2,128,512]{3,2,1,0:T(8,128)(2,1)S(1)}, u32[]{:S(2)}, u32[]{:S(2)}) async-start(bf16[4,2,128,512]{3,2,1,0:T(8,128)(2,1)} %copy.162), calls=%async_computation.8 | async-start | bytes 2097152 | tf_op jit(solution)/shard_map/all_to_all | solution.py:177
  (122 other events, 1648.7 us)

commit v3 on v2

--- a/solution.py
+++ b/solution.py
@@ -303,9 +303,9 @@
         ],
         compiler_params=pltpu.CompilerParams(vmem_limit_bytes=40 * 2**20),
         cost_estimate=pl.CostEstimate(
-            flops=16 * q.size * keys,
-            transcendentals=batch * H * rows * keys,
-            bytes_accessed=4 * q.size + 4 * k.size + 2 * batch * H * rows * keys,
+            flops=16 * q.size * keys * URGENT,
+            transcendentals=0,
+            bytes_accessed=(4 * q.size + 4 * k.size + 2 * batch * H * rows * keys) * URGENT,
         ),
         name="attend",
     )(prefix, q, k, v)
@@ -353,9 +353,9 @@
         ],
         compiler_params=pltpu.CompilerParams(vmem_limit_bytes=40 * 2**20),
         cost_estimate=pl.CostEstimate(
-            flops=32 * q.size * keys,
+            flops=32 * q.size * keys * URGENT,
             transcendentals=0,
-            bytes_accessed=6 * q.size + 8 * k.size + 2 * batch * H * rows * keys,
+            bytes_accessed=(6 * q.size + 8 * k.size + 2 * batch * H * rows * keys) * URGENT,
         ),
         name="attend_back",
     )(do, q, k, v, p)
@@ -380,30 +380,38 @@
     x, c, _, y = here()
     rows, half = w.shape[2], w.shape[3] // 2
     dx, dc = flip(x, number // 2), flip(c, number % 2)
-
-    def copy(ref, i, dy, g):
-        src, to = ref.at[i, :, pl.ds(0, rows)], w.at[:, flip(y, dy), :, pl.ds(g * half, half)]
+    halves = len(refs[0].shape) == 4
+
+    def copy(src, dy, g):
+        to = w.at[:, flip(y, dy), :, pl.ds(g * half, half)] if halves else w.at[:, flip(y, dy)]
+        src = src.at[:, pl.ds(0, rows)]
         getattr(pltpu.make_async_copy(src, to, sems.at[2 * dy + g]), act)()
 
     if act == "wait":
         for dy in range(2):
-            for g in range(2):
-                copy(refs[0], 0, dy, g)
+            for g in range(2 if halves else 1):
+                copy(refs[0].at[0] if halves else refs[0], dy, g)
         return
     for far in range(2):
-        p0, q0, p1, q1 = refs[4 * far : 4 * far + 4]
-
-        @pl.when(dc == far)
-        def _(p1=p1, q1=q1):
-            copy(p1, dx, 0, 1)
-            copy(q1, dx, 1, 1)
-
-        for ref, side in ((p0, 0), (q0, 1)):
+        group = refs[4 * far : 4 * far + 4]
+        if halves:
+            p0, q0, p1, q1 = group
+
+            @pl.when(dc == far)
+            def _(p1=p1, q1=q1):
+                copy(p1.at[dx], 0, 1)
+                copy(q1.at[dx], 1, 1)
+
+        for side in range(2):
 
             @pl.when((dc == far) & (dx == side))
-            def _(ref=ref):
-                copy(ref, 0, 0, 0)
-                copy(ref, 1, 1, 0)
+            def _(group=group, side=side):
+                if halves:
+                    copy(group[side].at[0], 0, 0)
+                    copy(group[side].at[1], 1, 0)
+                else:
+                    copy(group[2 * side], 0, 0)
+                    copy(group[2 * side + 1], 1, 0)
 
 
 def row_sum(v):
@@ -429,46 +437,69 @@
     return v.reshape(v.shape[-4] * v.shape[-3] * v.shape[-2], v.shape[-1])
 
 
-def times(a_ref, w_ref, put, tile=256):
-    def one(i, carry):
-        lanes = pl.ds(pl.multiple_of(i * tile, tile), tile)
-        w = w_ref[:, :, :, lanes]
-        w = w.reshape(w.shape[0] * w.shape[1] * w.shape[2], tile)
-        put(lanes, jnp.dot(a_ref[...], w, preferred_element_type=F32))
-        return carry
-
-    lax.fori_loop(0, w_ref.shape[3] // tile, one, 0)
+def times(a_ref, w_ref, put):
+    put(slice(None), jnp.dot(a_ref[...], weight(w_ref), preferred_element_type=F32))
 
 
 def times_t(pairs, put):
-    wide = pairs[0][1].shape[1] * pairs[0][1].shape[2]
-
-    def one(i, carry):
-        total = None
-        for a_ref, w_ref in pairs:
-            w = w_ref[i].reshape(wide, w_ref.shape[3])
-            part = dot_nt(a_ref[...], w)
-            total = part if total is None else total + part
-        put(pl.ds(pl.multiple_of(i * wide, wide), wide), total)
-        return carry
-
-    lax.fori_loop(0, pairs[0][1].shape[0], one, 0)
+    total = None
+    for a_ref, w_ref in pairs:
+        part = dot_nt(a_ref[...], weight(w_ref))
+        total = part if total is None else total + part
+    put(slice(None), total)
 
 
 def loaded(m, n, count):
     return [pltpu.VMEM((4, 2, m, n), BF)] * count + [pltpu.SemaphoreType.DMA((count, 4))]
 
 
+URGENT = 400
+
+
 def cost(flops, *arrays):
     return pl.CostEstimate(
-        flops=flops,
+        flops=flops * URGENT,
         transcendentals=0,
-        bytes_accessed=sum(a.size * a.dtype.itemsize for a in arrays),
+        bytes_accessed=sum(a.size * a.dtype.itemsize for a in arrays) * URGENT,
     )
 
 
 def shape(dims, dtype):
     return jax.ShapeDtypeStruct(dims, dtype)
+
+
+def pack_kernel(count, *rest):
+    mats, vectors, out = rest[:4], rest[4 : 4 + count], rest[-1]
+    x, c, _, _ = here()
+    m, n = mats[0].shape
+    half = n // 2
+    for number, mat in enumerate(mats):
+
+        @pl.when(2 * x + c == number)
+        def _(mat=mat):
+            for g in range(2):
+                out[g, :m, :] = mat[:, g * half : (g + 1) * half]
+
+    parts = []
+    for v in vectors:
+        parts += [v[i : i + m].reshape(1, m) for i in range(0, v.shape[0], m)]
+    parts += [jnp.zeros((1, m), BF)] * (8 * n // m - len(parts))
+    row = half // m
+    rows = [jnp.concatenate(parts[row * i : row * (i + 1)], 1) for i in range(16)]
+    for g in range(2):
+        out[g, m:, :] = jnp.concatenate(rows[8 * g : 8 * g + 8], 0)
+
+
+def pack(mats, vectors):
+    m, n = mats[0].shape
+    return pl.pallas_call(
+        partial(pack_kernel, len(vectors)),
+        in_specs=[WHOLE] * (4 + len(vectors)),
+        out_specs=WHOLE,
+        out_shape=shape((2, m + 8, n // 2), BF),
+        compiler_params=BIG,
+        name="pack",
+    )(*mats, *vectors)
 
 
 def first_kernel(x_ref, vec_ref, *rest):
@@ -774,33 +805,22 @@
         pltpu.make_async_copy(block, keep.at[(dx,) + spot], sem).start()
 
 
+def dot_tn(a, b):
+    return lax.dot_general(a, b, (((0,), (0,)), ((), ())), preferred_element_type=F32)
+
+
 def grads_kernel(sides, *rest):
-    lefts = sorted({l for l, _ in sides})
-    n_in = len(lefts) + len(sides)
-    left_refs, right_refs = rest[: len(lefts)], rest[len(lefts) : n_in]
-    away, keep = rest[n_in : n_in + 2]
-    out, sems = rest[-2], rest[-1]
-    turned = rest[n_in + 2 : -2]
+    count = 1 + max(sides)
+    left_refs, right_refs = rest[:count], rest[count : count + 4]
+    away, keep, out, sems = rest[count + 4 :]
     x, c, z, y = here()
-    done = set()
-    for number, (l, _) in enumerate(sides):
-        t_ref = turned[l]
-        if l not in done:
-            done.add(l)
-            for f in range(left_refs[l].shape[1] // 256):
-                t_ref[f * 256 : (f + 1) * 256, :] = left_refs[l][:, f * 256 : (f + 1) * 256].T
-        r_ref = right_refs[number]
-        half = out.shape[-1]
-        for g in range(2):
-
-            def one(zz, carry, g=g, number=number, t_ref=t_ref, r_ref=r_ref):
-                rows = t_ref[pl.ds(pl.multiple_of(zz * 256, 256), 256), :]
-                v = jnp.dot(rows, r_ref[:, g * half : (g + 1) * half], preferred_element_type=F32).astype(BF)
-                out[number, g, y, zz] = v[:128]
-                out[number, g, 1 - y, zz] = v[128:]
-                return carry
-
-            lax.fori_loop(0, 4, one, 0)
+    half = out.shape[-1]
+    for number, side in enumerate(sides):
+        for zz in range(4):
+            v = dot_tn(left_refs[side][:, zz * 256 : (zz + 1) * 256], right_refs[number][...]).astype(BF)
+            for yy in range(2):
+                for g in range(2):
+                    out[number, g, flip(y, yy), zz] = v[yy * 128 : (yy + 1) * 128, g * half : (g + 1) * half]
         dx, dc = flip(x, number // 2), flip(c, number % 2)
         send_off(out.at[number], away, keep, dx, dc, (), sems.at[number])
     for number in range(4):
@@ -810,18 +830,44 @@
 def grads(lefts, rights, sides, name):
     d, n = lefts[0].shape[1], rights[0].shape[1]
     dims = (2, 2, 2, 4, d // 8, n // 2)
-    sides = tuple((l, i) for i, l in enumerate(sides))
     return pl.pallas_call(
         partial(grads_kernel, sides),
         in_specs=[WHOLE] * (len(lefts) + 4),
         out_specs=[SPOT] * 2,
         out_shape=[shape(dims, BF)] * 2,
-        scratch_shapes=[pltpu.VMEM((d, l.shape[0]), BF) for l in lefts]
-        + [pltpu.VMEM((4,) + dims[1:], BF), pltpu.SemaphoreType.DMA((4,))],
+        scratch_shapes=[pltpu.VMEM((4,) + dims[1:], BF), pltpu.SemaphoreType.DMA((4,))],
         compiler_params=BIG,
         cost_estimate=cost(2 * sum(r.size for r in rights) * d, *lefts, *rights, *rights, *rights),
         name=name,
     )(*lefts, *rights)
+
+
+def sums_kernel(counts, *rest):
+    ins, outs = rest[: sum(counts)], rest[sum(counts) :]
+    at_in = 0
+    for out, count in zip(outs, counts):
+        total = ins[at_in][...].astype(F32)
+        for r in ins[at_in + 1 : at_in + count]:
+            total = total + r[...].astype(F32)
+        out[...] = total.astype(BF).reshape(out.shape)
+        at_in += count
+
+
+def sums(steps, *groups):
+    ins = [i for _, _, _, members in groups for i in members]
+    return pl.pallas_call(
+        partial(sums_kernel, tuple(len(g[3]) for g in groups)),
+        grid=(steps,),
+        in_specs=[pl.BlockSpec(block, to) for _, block, to in ins],
+        out_specs=[pl.BlockSpec(g[1], g[2]) for g in groups],
+        out_shape=[shape(g[0], BF) for g in groups],
+        cost_estimate=pl.CostEstimate(
+            flops=0,
+            transcendentals=0,
+            bytes_accessed=2 * URGENT * sum(int(np.prod(g[0])) * (1 + len(g[3])) for g in groups),
+        ),
+        name="sums",
+    )(*[v for v, _, _ in ins])
 
 
 def grads_of(left, lefts, rights, sides, name):
@@ -834,45 +880,24 @@
     refs, rest = rest[:8], rest[8:]
     outs, rest = rest[: 4 if last else 2], rest[4 if last else 2 :]
     dbe_ref, away, keep = rest[:3]
-    act_t, hid_ref, dexp_ref, acc, dact, out, we0, wd0, we1, wd1, sems, out_sems = rest[3:]
-    i = pl.program_id(0)
-    s = lax.rem(i, 2)
+    hid_ref, dexp_ref, acc, dact, out, we0, wd0, we1, wd1, sems, out_sems = rest[3:]
     rows, d = act_ref.shape
-    ff = d // 2
+    half_n = d // 2
     x, c, z, y = here()
     mats = ((we0, wd0), (we1, wd1))
-
-    @pl.when(i == 0)
-    def _():
-        for t in range(2):
-            for n in range(2):
-                pieces_of(refs, 2 * t + n, mats[t][n], sems.at[2 * t + n], "start")
-        for f in range(d // 256):
-            act_t[f * 256 : (f + 1) * 256, :] = act_ref[:, f * 256 : (f + 1) * 256].T
-        if last:
-            acc[...] = begin[0][...]
-            dact[...] = begin[1][...]
-            outs[3][...] = jnp.zeros_like(outs[3])
-        else:
-            acc[...] = jnp.zeros_like(acc)
-            dact[...] = jnp.zeros_like(dact)
-
+    for t in range(2):
+        for n in range(2):
+            pieces_of(refs, 2 * t + n, mats[t][n], sems.at[2 * t + n], "start")
     dbe_ref[...] = jnp.zeros_like(dbe_ref)
-
-    def block(t):
-        we_ref, wd_ref = mats[t]
-
-        @pl.when(s == 0)
-        def _():
-            for n in range(2):
-                pieces_of(refs, 2 * t + n, mats[t][n], sems.at[2 * t + n], "wait")
-
-        lanes = pl.ds(pl.multiple_of(s * ff, ff), ff)
-        bias = vec_ref[first_row + t : first_row + t + 1, lanes]
-
-        def half(r):
-            we = we_ref[:, :, :, lanes].reshape(d, ff)
-            wd = wd_ref[pl.ds(2 * s, 2)].reshape(ff, d)
+    if last:
+        outs[3][...] = jnp.zeros_like(outs[3])
+    for t in range(2):
+        for n in range(2):
+            pieces_of(refs, 2 * t + n, mats[t][n], sems.at[2 * t + n], "wait")
+        bias = vec_ref[first_row + t : first_row + t + 1]
+
+        def half(r, t=t, bias=bias):
+            we, wd = weight(mats[t][0]), weight(mats[t][1])
             u = jnp.dot(act_ref[r, :], we, preferred_element_type=F32) + bias
             cdf = 0.5 * (1.0 + lax.erf(u * np.float32(0.5**0.5)))
             pdf = jnp.exp(-0.5 * u * u) * np.float32((2 * np.pi) ** -0.5)
@@ -880,66 +905,51 @@
             hid_ref[r, :] = hid
             dexp = (dot_nt(dy_ref[r, :], wd) * (cdf + u * pdf)).astype(BF)
             dexp_ref[r, :] = dexp
-            dbe_ref[0] += row_sum(dexp.astype(F32))
-            acc[r, :] += jnp.dot(hid, wd, preferred_element_type=F32)
-            dact[r, :] += dot_nt(dexp, we)
+            dbe_ref[t : t + 1] += row_sum(dexp.astype(F32))
+            down, back = jnp.dot(hid, wd, preferred_element_type=F32), dot_nt(dexp, we)
+            if t == 0 and not last:
+                acc[r, :], dact[r, :] = down, back
+            elif t == 0:
+                acc[r, :], dact[r, :] = begin[0][r, :] + down, begin[1][r, :] + back
+            else:
+                acc[r, :] += down
+                dact[r, :] += back
 
         chunks(rows, 256, half)
-
-        def e_part(zz, carry):
-            at_rows = pl.ds(pl.multiple_of(zz * 256, 256), 256)
-            v = jnp.dot(act_t[at_rows, :], dexp_ref[...], preferred_element_type=F32).astype(BF)
-            out[2 * t, s, y, zz] = v[:128]
-            out[2 * t, s, 1 - y, zz] = v[128:]
-            return carry
-
-        lax.fori_loop(0, 4, e_part, 0)
-        hid_t = hid_ref[...].T
-        for zz in range(2):
-            for yy in range(2):
-                n = 2 * zz + yy
-                v = jnp.dot(hid_t[n * 128 : (n + 1) * 128], dy_ref[...], preferred_element_type=F32).astype(BF)
-                for g in range(2):
-                    out[2 * t + 1, g, flip(y, yy), 2 * s + zz] = v[:, g * ff : (g + 1) * ff]
-
-        @pl.when(s == 1)
-        def _():
-            for n in range(2):
-                number = 2 * t + n
-                dx, dc = flip(x, number // 2), flip(c, number % 2)
-                send_off(out.at[number], away, keep, dx, dc, (), out_sems.at[number])
-
-    for t in range(2):
-        pl.when(lax.div(i, 2) == t)(partial(block, t))
-
-    @pl.when(i == pl.num_programs(0) - 1)
-    def _():
-        if last:
-            out_ref, dmid_ref, low_ref, sum_ref = outs
-
-            def back(r):
-                mid = mid_ref[r, :]
-                out_ref[r, :] = (mid + (acc[r, :] + vec_ref[12:13])).astype(BF)
-                dy = dy_ref[r, :].astype(F32)
-                total = apply_norm_back(r, dact[r, :], mid, vec_ref[10:11], dy, sum_ref)
-                dmid_ref[r, :] = total
-                low = total.astype(BF)
-                low_ref[r, :] = low
-                sum_ref[2:3] += row_sum(dy)
-                sum_ref[3:4] += row_sum(low.astype(F32))
-
-            chunks(rows, CHUNK, back)
-        else:
-            outs[0][...] = acc[...]
-            outs[1][...] = dact[...]
-        for number in range(4):
-            pltpu.make_async_copy(out.at[number], keep.at[0], out_sems.at[number]).wait()
+        for number, (a_ref, b_ref) in ((2 * t, (act_ref, dexp_ref)), (2 * t + 1, (hid_ref, dy_ref))):
+            for zz in range(4):
+                v = dot_tn(a_ref[:, zz * 256 : (zz + 1) * 256], b_ref[...]).astype(BF)
+                for yy in range(2):
+                    for g in range(2):
+                        part = v[yy * 128 : (yy + 1) * 128, g * half_n : (g + 1) * half_n]
+                        out[number, g, flip(y, yy), zz] = part
+            dx, dc = flip(x, number // 2), flip(c, number % 2)
+            send_off(out.at[number], away, keep, dx, dc, (), out_sems.at[number])
+    if last:
+        out_ref, dmid_ref, low_ref, sum_ref = outs
+
+        def back(r):
+            mid = mid_ref[r, :]
+            out_ref[r, :] = (mid + (acc[r, :] + vec_ref[12:13])).astype(BF)
+            dy = dy_ref[r, :].astype(F32)
+            total = apply_norm_back(r, dact[r, :], mid, vec_ref[10:11], dy, sum_ref)
+            dmid_ref[r, :] = total
+            low = total.astype(BF)
+            low_ref[r, :] = low
+            sum_ref[2:3] += row_sum(dy)
+            sum_ref[3:4] += row_sum(low.astype(F32))
+
+        chunks(rows, CHUNK, back)
+    else:
+        outs[0][...] = acc[...]
+        outs[1][...] = dact[...]
+    for number in range(4):
+        pltpu.make_async_copy(out.at[number], keep.at[0], out_sems.at[number]).wait()
 
 
 def ffn(act, dy, mid, vecs, unit, m, begin, first_row):
     rows, d = act.shape
     last = bool(begin)
-    still = lambda s: pl.BlockSpec(s.shape, lambda j: (0,) * len(s.shape))
     dims = (2, 2, 2, 4, m, d // 2)
     if last:
         heads = [shape(act.shape, BF), shape(act.shape, F32), shape(act.shape, BF), shape((8, d), F32)]
@@ -947,16 +957,12 @@
         heads = [shape(act.shape, F32)] * 2
     return pl.pallas_call(
         partial(ffn_kernel, last, first_row),
-        grid=(4,),
-        in_specs=[still(v) for v in (act, dy, mid, vecs, *begin)] + [SPOT] * 8,
-        out_specs=[still(s) for s in heads]
-        + [pl.BlockSpec((1, 1, d // 2), lambda j: (j, 0, 0))]
-        + [SPOT] * 2,
-        out_shape=heads + [shape((4, 1, d // 2), F32)] + [shape(dims, BF)] * 2,
+        in_specs=[WHOLE] * (4 + len(begin)) + [SPOT] * 8,
+        out_specs=[WHOLE] * (len(heads) + 1) + [SPOT] * 2,
+        out_shape=heads + [shape((8, d), F32)] + [shape(dims, BF)] * 2,
         scratch_shapes=[
-            pltpu.VMEM((d, rows), BF),
-            pltpu.VMEM((rows, d // 2), BF),
-            pltpu.VMEM((rows, d // 2), BF),
+            pltpu.VMEM((rows, d), BF),
+            pltpu.VMEM((rows, d), BF),
             pltpu.VMEM((rows, d), F32),
             pltpu.VMEM((rows, d), F32),
             pltpu.VMEM((4,) + dims[1:], BF),
@@ -972,36 +978,34 @@
 def finish_kernel(count, *rest):
     units, outs, held = [rest[3 * i : 3 * i + 3] for i in range(count)], rest[3 * count : -1], rest[-1]
     x, c, _, _ = here()
-    half = units[0][0].shape[-1]
+    m, n = units[0][0].shape
     for i, (own_ref, x_ref, core_ref) in enumerate(units):
         held[0], held[2] = own_ref[...], x_ref[...]
         held[1], held[3] = core_ref[0], core_ref[1]
         for number in range(4):
             j = flip(x, number // 2) * 2 + flip(c, number % 2)
-            for g in range(2):
-                v = held[j, g].astype(F32)
-                if count == 1:
-                    outs[number][:, g * half : (g + 1) * half] = v
-                elif number % 2:
-                    t = 2 * i + number // 2
-                    outs[1][t * v.shape[0] : (t + 1) * v.shape[0], g * half : (g + 1) * half] = v
-                else:
-                    t = 2 * i + number // 2
-                    for f in range(half // 128):
-                        to = ((g * (half // 128) + f) * 4 + t) * 128
-                        outs[0][:, to : to + 128] = v[:, f * 128 : (f + 1) * 128]
-
-
-def finish(*units):
-    _, m, half = units[0][0].shape
-    n = 2 * half
+            v = held[j].astype(F32)
+            t = 2 * i + number // 2
+            if count == 1:
+                outs[number][...] = v
+            elif number % 2:
+                outs[1][t * m : (t + 1) * m] = v
+            else:
+                for f in range(n // 128):
+                    to = (f * 4 + t) * 128
+                    outs[0][:, to : to + 128] = v[:, f * 128 : (f + 1) * 128]
+
+
+def finish(own, from_x, from_core, parts=()):
+    units = ((own, from_x, from_core), *parts)
+    m, n = own.shape
     dims = [(m, n)] * 4 if len(units) == 1 else [(m, 4 * n), (4 * m, n)]
     return pl.pallas_call(
         partial(finish_kernel, len(units)),
         in_specs=[WHOLE] * (3 * len(units)),
         out_specs=[WHOLE] * len(dims),
         out_shape=[shape(s, F32) for s in dims],
-        scratch_shapes=[pltpu.VMEM((4, 2, m, half), BF)],
+        scratch_shapes=[pltpu.VMEM((4, m, n), BF)],
         compiler_params=BIG,
         cost_estimate=cost(0, *[v for u in units for v in u] * 3),
         name="finish",
@@ -1212,41 +1216,36 @@
 
 
 class Order:
-    def __init__(self, width):
-        self.width, self.past, self.sent, self.ran = width, [], [], []
-
-    def send(self, move, v):
-        after = list(self.ran)
-        if len(self.past) >= self.width:
-            after.append(self.past[-self.width])
-        if after:
-            v, *_ = lax.optimization_barrier((v, *after))
+    def __init__(self):
+        self.sent, self.ran, self.open = [], [], []
+
+    def send(self, move, v, hold=2):
+        v = self.see(v)
         got = move(v)
-        self.past.append(got)
         self.sent.append(v)
+        self.open.append([hold, got])
         return got
 
-    def swap(self, move, v):
-        if self.ran:
-            v, *_ = lax.optimization_barrier((v, *self.ran))
-        self.sent.append(v)
-        return move(v)
+    def see(self, v):
+        return lax.optimization_barrier((v, *self.ran))[0] if self.ran else v
 
     def run(self, kernel, v, *rest, **named):
-        if self.sent or self.ran:
-            v, *_ = lax.optimization_barrier((v, *self.sent, *self.ran))
+        due = [got for hold, got in self.open if hold == 0]
+        self.open = [[hold - 1, got] for hold, got in self.open if hold > 0]
+        before = (*self.sent, *self.ran, *due)
+        if before:
+            v, *_ = lax.optimization_barrier((v, *before))
         out = kernel(v, *rest, **named)
         self.sent, self.ran = [], [out[0] if isinstance(out, (list, tuple)) else out]
         return out
 
 
-class Unit:
+class HalfUnit:
     def __init__(self, place, order, piece):
         self.place, self.order, self.piece = place, order, piece
-        self.steps = [self.ring, self.one, self.two, self.core]
 
     def ring(self):
-        a = self.order.swap(partial(ring_gather, self.place), self.piece)
+        a = self.order.send(partial(ring_gather, self.place), self.piece)
         self.a0, self.a1 = a[:, 0], a[:, 1]
 
     def one(self):
@@ -1265,43 +1264,94 @@
         self.refs = (self.p0, self.q0, self.p1, self.q1, self.c0, d0, self.c1, d1)
 
 
-def low_sum(*parts):
-    total = parts[0].astype(F32)
-    for p in parts[1:]:
-        total = total + p.astype(F32)
-    return total.astype(BF)
+class Unit:
+    def __init__(self, place, order, piece, flat):
+        self.place, self.order, self.piece, self.flat = place, order, piece, flat
+
+    def ring(self):
+        self.a = self.order.send(partial(ring_gather, self.place), self.piece)
+
+    def pair(self):
+        self.b = self.order.send(self.place.pair, self.order.see(self.a))
+
+    def across(self):
+        self.ax = self.order.send(self.place.across, self.order.see(self.a))
+
+    def near(self):
+        self.ca = self.order.send(self.place.core, self.order.see(self.a), 1)
+
+    def two(self):
+        see, send = self.order.see, self.order.send
+        if self.flat:
+            self.bx = send(self.place.pair, see(self.ax))
+        else:
+            self.bx = send(self.place.across, see(self.b))
+
+    def both(self):
+        see, send = self.order.see, self.order.send
+        self.cb, self.cax = send(self.place.core, see(self.b), 1), send(self.place.core, see(self.ax), 1)
+
+    def core(self):
+        far = self.order.send(self.place.core, self.order.see(self.bx))
+        self.refs = (self.a, self.b, self.ax, self.bx, self.ca, self.cb, self.cax, far)
 
 
 class Sum:
     def __init__(self, place, order, away, keep):
         self.place, self.order = place, order
         self.away, self.keep = away, keep
-        self.steps = [self.core, self.one, self.two, self.ring, self.last_x, self.last_core]
 
     def core(self):
         self.came = self.order.send(self.place.core, self.away)
 
     def one(self):
+        see, k = self.order.see, self.keep
+        self.came = see(self.came)
+        block, dims = (None, None, None) + k.shape[3:], k.shape[2:]
+        half = (None,) + dims[1:]
+        first, second = (lambda i: (1, 0, i, 0, 0, 0)), (lambda i: (i, 1, 1, 0, 0, 0))
+        to = lambda i: (i, 0, 0, 0)
+        to_x, to_y = sums(
+            2,
+            (dims, half, to, [(k, block, first), (self.came, block, first)]),
+            (dims, half, to, [(k, block, second), (self.came, block, second)]),
+        )
+        self.from_x = self.order.send(self.place.across, to_x)
+        self.from_y = self.order.send(self.place.pair, to_y)
+
+    def rest(self, name, extra):
         k, r = self.keep, self.came
-        self.from_x = self.order.send(self.place.across, low_sum(k[1, 0], r[1, 0]))
-        self.from_y = self.order.send(self.place.pair, low_sum(k[:, 1, 1], r[:, 1, 1]))
+        _, m, half = k.shape[3:]
+        block, part = (None, None, None, 2, m, half), (None, 2, m, half)
+        first = (lambda i: (0, 0, 1, i, 0, 0)) if name == "go" else (lambda i: (0, 0, 0, i, 0, 0))
+        second = (lambda i: (1, 1, 0, i, 0, 0)) if name == "go" else (lambda i: (0, 1, 0, i, 0, 0))
+        side = 1 if name == "go" else 0
+        third = lambda i: (side, i, 0, 0)
+        plain = lambda i: (i, 0, 0)
+        groups = []
+        for at_k, came, more in ((first, self.from_x, extra[:1]), (second, self.from_y, extra[1:])):
+            members = [(k, block, at_k), (r, block, at_k), (came, part, third)]
+            members += [(v, (2, m, half), plain) for v in more]
+            groups.append(((4, m, half), (2, m, half), plain, members))
+        return sums(2, *groups)
 
     def two(self):
-        k, r, fx, fy = self.keep, self.came, self.from_x, self.from_y
-        self.next_y = self.order.send(self.place.pair, low_sum(k[0, 0, 1], r[0, 0, 1], fx[1]))
-        self.next_x = self.order.send(self.place.across, low_sum(k[1, 1, 0], r[1, 1, 0], fy[1]))
+        self.from_x, self.from_y = self.order.see(self.from_x), self.order.see(self.from_y)
+        to_y, to_x = self.rest("go", [])
+        self.next_y = self.order.send(self.place.pair, to_y)
+        self.next_x = self.order.send(self.place.across, to_x)
 
     def ring(self):
-        k, r, fx, fy = self.keep, self.came, self.from_x, self.from_y
-        first = low_sum(k[0, 0, 0], r[0, 0, 0], fx[0], self.next_y)
-        second = low_sum(k[0, 1, 0], r[0, 1, 0], fy[0], self.next_x)
-        self.own = self.order.swap(partial(ring_sum, self.place), jnp.stack([first, second], 1))
+        see = self.order.see
+        first, second = self.rest("stay", [see(self.next_y), see(self.next_x)])
+        self.own = self.order.send(partial(ring_sum, self.place), jnp.concatenate([first, second], 2))
 
     def last_x(self):
+        self.own = self.order.see(self.own)
         self.own_x = self.order.send(self.place.across, self.own)
 
     def last_core(self):
-        came = self.order.send(self.place.core, jnp.stack([self.own, self.own_x]))
+        came = self.order.send(self.place.core, jnp.stack([self.own, self.order.see(self.own_x)]))
         self.parts = (self.own, self.own_x, came)
 
 
@@ -1342,63 +1392,71 @@
     m = self_query.shape[0]
     ff = expand_weight.shape[1]
     rank = 2 * place.x + place.c
-    order = Order(5)
+    order = Order()
 
     small = [
         selfnorm_gain, selfnorm_bias, selfquery_bias, selfvalue_bias, self_attention_output_bias,
         crossnorm_gain, crossnorm_bias, crossquery_bias, crossvalue_bias, crossoutput_bias,
         finalnorm_gain, finalnorm_bias, reduce_bias, expand_bias,
     ]
-    packed = jnp.concatenate(small)
     count = 13 + ff // d
-    packed = jnp.pad(packed, (0, 8 * d - packed.shape[0])).reshape(2, 8, d // 2)
 
     def pick(*shards):
-        v = at(jnp.stack(shards), rank)
-        return v.reshape(m, 2, d // 2).transpose(1, 0, 2)
-
-    w_e = expand_weight.reshape(m, rows, 4, -1).transpose(2, 0, 1, 3).reshape(4, m, d)
-    w_d = down_projection_weight.reshape(4, m, d)
+        return at(jnp.stack(shards), rank)
+
+    u_self = HalfUnit(place, order, pack((self_query, self_key, self_value, self_output), small))
+    u_self.ring()
+    later = (cross_query, cross_key, cross_value, cross_output, expand_weight, down_projection_weight)
+    *later, _ = lax.optimization_barrier((*later, u_self.a0))
+    w_e = later[4].reshape(m, rows, 4, -1).transpose(2, 0, 1, 3).reshape(4, m, d)
+    w_d = later[5].reshape(4, m, d)
     unit = partial(Unit, place, order)
-    u_self = unit(jnp.concatenate([pick(self_query, self_key, self_value, self_output), packed], 1))
-    u_cross = unit(pick(cross_query, cross_key, cross_value, cross_output))
-    u_low = unit(pick(w_e[0], w_d[0], w_e[1], w_d[1]))
-    u_high = unit(pick(w_e[2], w_d[2], w_e[3], w_d[3]))
+    u_cross = unit(pick(*later[:4]), True)
+    u_low = unit(pick(w_e[0], w_d[0], w_e[1], w_d[1]), False)
+    u_high = unit(pick(w_e[2], w_d[2], w_e[3], w_d[3]), True)
 
     x = decoder_input.reshape(batch * seq, d)
     e = encoder_out.reshape(-1, d)
     dy = output_grad.reshape(batch * seq, d)
     run = order.run
 
-    u_self.ring()
     u_self.one()
     u_cross.ring()
     u_self.two()
+    u_self.core()
     u_low.ring()
-    u_self.core()
-    u_cross.one()
+    u_cross.pair()
+    u_cross.across()
+    u_cross.near()
     self_w = u_self.refs
-    both = jnp.stack([v[:, :, m:] for v in (u_self.p0[:, :, :], jnp.stack([u_self.p1[0], u_self.q1[0]]))])
+    both = jnp.stack([v[:, :, m:] for v in (u_self.p0, jnp.stack([u_self.p1[0], u_self.q1[0]]))])
     both = both.transpose(2, 1, 0, 3, 4)
-    both = jnp.where(place.y == 0, both, both[:, ::-1]).transpose(0, 1, 2, 3, 4).reshape(rows, -1)
+    both = jnp.where(place.y == 0, both, both[:, ::-1]).reshape(rows, -1)
     vecs = both[:, : count * m].reshape(rows, count, m).transpose(1, 0, 2).reshape(count, d).astype(F32)
     act1, q, k, v = run(first, x, vecs, self_w, m)
+    o, p = run(attend, q, k, v, prefix_length, batch, True)
     u_cross.two()
-    o, p = run(attend, q, k, v, prefix_length, batch, True)
+    u_low.across()
+    u_cross.both()
     u_high.ring()
+    mid1, act2 = run(project, o, x, vecs, (4, 5, 6, None), (self_w,), (3,), m, "self_out")
+    u_low.pair()
+    u_low.near()
     u_cross.core()
     cross_w = u_cross.refs
-    u_low.one()
-    mid1, act2 = run(project, o, x, vecs, (4, 5, 6, None), (self_w,), (3,), m, "self_out")
-    u_low.two()
     ck, cv = run(memory, e, vecs, cross_w, m)
     cq = run(query, act2, vecs, 7, cross_w, m)
-    u_low.core()
-    u_high.one()
+    u_high.across()
+    u_high.pair()
+    u_low.two()
     co, cp = run(attend, cq, ck, cv, prefix_length, batch, False)
     u_high.two()
+    u_low.both()
+    u_high.near()
     mid2, act3 = run(project, co, mid1, vecs, (9, 10, 11, None), (cross_w,), (3,), m, "cross_out")
+    u_low.core()
     low_w = u_low.refs
+    u_high.both()
 
     *begin, dbe_low, away, keep = run(ffn, act3, dy, mid2, vecs, low_w, m, (), 13)
     total = partial(Sum, place, order)
@@ -1413,58 +1471,58 @@
     g_high.core()
     dco = run(output_back, dcross, cross_w, m)
     dcq, dck, dcv = run(attend_back, dco, cq, ck, cv, cp, batch)
-    g_low.two()
     g_high.one()
     g_cross = total(*run(grads_of, act2, [e, co], [dcq, dck, dcv, dcross], (0, 1, 1, 2), "cross_grads"))
+    g_low.two()
     g_cross.core()
+    dmid1, dself, dao, sums2 = run(cross_back, dcq, mid1, dmid2, vecs, cross_w, self_w, m)
+    g_cross.one()
+    dq, dk, dv = run(attend_back, dao, q, k, v, p, batch)
+    g_high.two()
     g_low.ring()
-    dmid1, dself, dao, sums2 = run(cross_back, dcq, mid1, dmid2, vecs, cross_w, self_w, m)
-    g_high.two()
-    dq, dk, dv = run(attend_back, dao, q, k, v, p, batch)
-    g_cross.one()
-    g_high.ring()
     g_self = total(*run(grads_of, act1, [o], [dq, dk, dv, dself], (0, 0, 0, 1), "self_grads"))
     g_self.core()
-    g_cross.two()
-    encoder_grad, sums_e = run(memory_back, dck, dcv, cross_w, m)
-    g_self.one()
-    g_cross.ring()
     input_grad, sums1 = run(self_back, dq, dk, dv, x, dmid1, vecs, self_w, m)
-    g_self.two()
 
     def by_shard(v):
         return v.reshape(-1, rows, m).transpose(1, 0, 2)
 
-    dbe = jnp.concatenate([dbe_low, dbe_high]).reshape(4, d)
-    sums = by_shard(jnp.concatenate([sums1[:4], sums2[:4], sums3[:4], sums_e[:1], dbe]))
-    sums = (sums.astype(BF).astype(F32) + order.send(place.core, sums.astype(BF)).astype(F32)).astype(BF)
+    g_self.one()
+    g_cross.two()
+    g_high.ring()
+    encoder_grad, sums_e = run(memory_back, dck, dcv, cross_w, m)
+    dbe = jnp.concatenate([dbe_low[:2], dbe_high[:2]])
+    vec = by_shard(jnp.concatenate([sums1[:4], sums2[:4], sums3[:4], sums_e[:1], dbe]))
+    vec = (vec.astype(BF).astype(F32) + order.send(place.core, vec.astype(BF)).astype(F32)).astype(BF)
     g_low.last_x()
+    vec = (vec.astype(F32) + order.send(place.across, vec).astype(F32)).astype(BF)
+    g_self.two()
+    g_cross.ring()
     g_high.last_x()
-    sums = (sums.astype(F32) + order.send(place.across, sums).astype(F32)).astype(BF)
-    g_self.ring()
     g_low.last_core()
     g_high.last_core()
-    sums = sums.reshape((place.ring, 2) + sums.shape[1:])
-    came = order.send(place.pair, at(sums, 1 - place.y, 1))
-    sums = (at(sums, place.y, 1).astype(F32) + came.astype(F32)).astype(BF)
-    g_expand, g_down = finish(g_low.parts, g_high.parts)
+    vec = vec.reshape((place.ring, 2) + vec.shape[1:])
+    came = order.send(place.pair, at(vec, 1 - place.y, 1))
+    vec = (at(vec, place.y, 1).astype(F32) + came.astype(F32)).astype(BF)
+    g_self.ring()
     g_cross.last_x()
-    sums = order.swap(partial(ring_sum, place), sums).astype(F32)
+    vec = order.send(partial(ring_sum, place), vec).astype(F32)
+    g_expand, g_down = run(finish, *g_low.parts, parts=(g_high.parts,))
     g_cross.last_core()
-    g_cq, g_ck, g_cv, g_co = finish(g_cross.parts)
     g_self.last_x()
+    g_cq, g_ck, g_cv, g_co = run(finish, *g_cross.parts)
     g_self.last_core()
-    g_sq, g_sk, g_sv, g_so = finish(g_self.parts)
+    g_sq, g_sk, g_sv, g_so = run(finish, *g_self.parts)
     return (
         layer_out.reshape(batch, seq, d),
         input_grad.reshape(batch, seq, d),
         encoder_grad.reshape(encoder_out.shape),
         g_sq, g_sk, g_sv, g_so,
-        sums[2], sums[3], sums[7],
+        vec[2], vec[3], vec[7],
         g_cq, g_ck, g_cv, g_co,
-        sums[6], sums[12], sums[11],
-        g_expand, sums[13:].reshape(-1), g_down, sums[10],
-        sums[0], sums[1], sums[4], sums[5], sums[8], sums[9],
+        vec[6], vec[12], vec[11],
+        g_expand, vec[13:].reshape(-1), g_down, vec[10],
+        vec[0], vec[1], vec[4], vec[5], vec[8], vec[9],
     )
 
 

time: 619 us -> 542 us (0.88)
  other arithmetic: 65 us -> 18.7 us
  local copies, waits for them, and re-layouts: 57.4 us -> 41.9 us
  waiting for transfers between devices: 117 us -> 108 us
    ppermute x17 -> x16, waiting for transfers between devices: 66.2 us -> 32.8 us  [pair(): return lax.ppermute(v, 'fsdp', [(i, i ^ 1) for i in range(self.rows)])]
    convert_element_type x16 -> x5, other arithmetic: 31.6 us -> 0.11 us  [the longest x2 0.08 us: fast_body(): vec = (at(vec, place.y, 1).astype(F32) + came.astype(F32)).astype(BF)]
    pallas_call x2 -> x15, Pallas kernels: 63.8 us -> 86.7 us  [the longest x2 47.5 us: ffn(): pl.pallas_call(partial(ffn_kernel, last, first_row), in_specs=[WHOLE] * (...]
    another operation x19 -> x6, other arithmetic: 22.4 us -> 1.88 us  [the longest x4 1.86 us: last_core(): jnp.stack([self.own, self.order.see(self.own_x)])]
    pallas_call x2, Pallas kernels: 33.3 us -> 20.8 us  [grads(): pl.pallas_call(partial(grads_kernel, sides), in_specs=[WHOLE] * (len(left...]
    all_to_all x3, waiting for transfers between devices: 0.01 us -> 11.8 us  [ring_gather(): lax.all_to_all(copies, 'fsdp', 0, 0, axis_index_groups=place.ring_members())]
    concatenate x2 -> x4, other arithmetic: 0.15 us -> 9.15 us  [ring(): jnp.concatenate([first, second], 2)]
    all_to_all x4, waiting for transfers between devices: 4.42 us -> 12.7 us  [ring_sum(): lax.all_to_all(parts, 'fsdp', 0, 0, axis_index_groups=place.ring_members())]
  transfers between devices with their start and end apart: 70 -> 67, of which waited for: 22 -> 20; matrix products, arithmetic and copies ran while one was open for 14% -> 6% of each run, Pallas kernels for 35% -> 46%
where the time goes in v3:
time: 542 us; the launch traced here: 533 us
  Pallas kernels  249 us (46%)
  waiting for transfers between devices  108 us (20%)
  starting transfers between devices  71.3 us (13%)
  local copies, waits for them, and re-layouts  41.9 us (8%)
  blocking collectives  41.2 us (8%)
  other arithmetic  18.7 us (3%)
    pallas_call x2, Pallas kernels, ffn(): pl.pallas_call(partial(ffn_kernel, last, first_row), in_specs=[WHOLE] * (...  47.5 us
    ppermute x19, waiting for transfers between devices, across(): return lax.ppermute(v, 'replica', [(i, i ^ 2) for i in range(self.groups)])  45.7 us
    pallas_call x12, Pallas kernels, sums(): pl.pallas_call(partial(sums_kernel, tuple((len(g[3]) for g in groups))),...  37.1 us
    all_to_all x1, blocking collectives, ring_gather(): lax.all_to_all(copies, 'fsdp', 0, 0, axis_index_groups=place.ring_members())  33.2 us
    ppermute x16, waiting for transfers between devices, pair(): return lax.ppermute(v, 'fsdp', [(i, i ^ 1) for i in range(self.rows)])  32.8 us
    pallas_call x2, Pallas kernels, attend_back(): pl.pallas_call(partial(attend_back_kernel, (d // H) ** (-0.5)), grid=(bat...  30.5 us
    pallas_call x2, Pallas kernels, attend(): pl.pallas_call(partial(attend_kernel, masked, (d // H) ** (-0.5)), grid_s...  28 us
    unnamed x98, local copies, waits for them, and re-layouts  27 us
  transfers between devices with their start and end apart: 67, of which 20 were waited for; matrix products, arithmetic and copies ran while one was open for 6% of the time, Pallas kernels for 46%

profile of v3, /device:TPU:0, one launch (start us, length us, event | category | flops | bytes accessed | tf_op | source)
XLA Modules:
  0.0 533.0 jit_solution(13531762581019414733)
XLA Ops:
  3.8 33.2 %all_to_all.45 = bf16[4,2,136,512]{3,2,1,0:T(8,128)(2,1)S(1)} all-to-all(bf16[4,2,136,512]{3,2,1,0:T(8,128)(2,1)S(1)} %broadcast_in_dim.12), channel_id=1, replica_groups={{0,2,4,6},{1,3,5,7},{8,10,12,14},{9,11,13,15},{16,18,20,22},{17,19,21,2..., dimensions={0} | all-to-all | bytes 2228224 | tf_op jit(solution)/shard_map/all_to_all | solution.py:66
  40.3 10.5 %collective-permute-done.1 = bf16[4,136,512]{2,1,0:T(8,128)(2,1)S(1)} collective-permute-done((bf16[4,136,512]{2,1,0:T(8,128)(2,1)S(1)}, bf16[4,136,512]{2,1,0:T(8,128)(2,1)S(1)}, u32[]{:S(2)}, u32[]{:S(2)}) %collective-permute-start.1) | collective-permute-done | bytes 557088 | tf_op jit(solution)/shard_map/ppermute | solution.py:34
  64.2 12.5 %collective-permute-done.3.rest_3_.rest_11_ = bf16[2,4,136,512]{3,2,1,0:T(8,128)(2,1)} collective-permute-done((bf16[2,4,136,512]{3,2,1,0:T(8,128)(2,1)}, bf16[2,4,136,512]{3,2,1,0:T(8,128)(2,1)}, u32[]{:S(2)}, u32[]{:S(2)}) %collective-permute-start.3) | collective-permute-done | bytes 1114144 | tf_op jit(solution)/shard_map/ppermute | solution.py:37
  93.8 7.6 %first.1 = (bf16[512,1024]{1,0:T(8,128)(2,1)}, bf16[512,1024]{1,0:T(8,128)(2,1)}, bf16[512,1024]{1,0:T(8,128)(2,1)}, bf16[512,1024]{1,0:T(8,128)(2,1)}) custom-call(bf16[512,1024]{1,0:T(8,128)(2,1)} %bitcast.153, f32[17,1024]{1,0:T(8,128)} %bitcast.139, bf16[2,4,136,512]{3,2,1,0:T(8,128)(2,1)} %pad_maximum_fusion.rest_0_.rest_8_, ...), custom_call_target="tpu_custom_call" | custom-call | flops 1288490188800 | bytes 5662310400 | tf_op jit(solution)/shard_map/first/pallas_call | solution.py:528
  105.1 10.3 %attend.2 = (bf16[512,1024]{1,0:T(8,128)(2,1)S(1)}, bf16[2,16,256,256]{3,2,1,0:T(8,128)(2,1)S(1)}) custom-call(s32[2]{0:T(128)S(1)} %copy-done, bf16[512,1024]{1,0:T(8,128)(2,1)S(1)} %copy-done.11, bf16[512,1024]{1,0:T(8,128)(2,1)S(1)} %copy-done.13, bf16[512,1024]{1,0:T(8,128)(2,1)S(1)} %copy-done.15), custom_call_target="tpu_custom_call" | custom-call | flops 858993459200 | bytes 3355443200 | tf_op jit(solution)/shard_map/attend/pallas_call | solution.py:289
  120.4 6.8 %self_out.1 = (f32[512,1024]{1,0:T(8,128)}, bf16[512,1024]{1,0:T(8,128)(2,1)}) custom-call(bf16[512,1024]{1,0:T(8,128)(2,1)} %copy-done.3, bf16[512,1024]{1,0:T(8,128)(2,1)} %bitcast.154, f32[17,1024]{1,0:T(8,128)} %bitcast.140, bf16[2,4,136,512]{3,2,1,0:T(8,128)(2,1)} %pad_maximum_fusion.rest_0_.rest_8_, ...), custom_call_target="tpu_custom_call" | custom-call | flops 429496729600 | bytes 4299161600 | tf_op jit(solution)/shard_map/self_out/pallas_call | solution.py:575
  127.3 17.0 %collective-permute-done.11.rest_3_ = bf16[4,128,1024]{2,1,0:T(8,128)(2,1)} collective-permute-done((bf16[4,128,1024]{2,1,0:T(8,128)(2,1)}, bf16[4,128,1024]{2,1,0:T(8,128)(2,1)}, u32[]{:S(2)}, u32[]{:S(2)}) %collective-permute-start.11) | collective-permute-done | bytes 1048608 | tf_op jit(solution)/shard_map/ppermute | solution.py:37
  154.7 9.2 %memory.1 = (bf16[1024,1024]{1,0:T(8,128)(2,1)}, bf16[1024,1024]{1,0:T(8,128)(2,1)}) custom-call(bf16[1024,1024]{1,0:T(8,128)(2,1)} %bitcast.149, f32[17,1024]{1,0:T(8,128)} %bitcast.141, bf16[4,128,1024]{2,1,0:T(8,128)(2,1)} %all-to-all-done.1.rest_0_, bf16[4,128,1024]{2,1,0:T(8,128)(2,1)} %collective-permute-done.10.rest_1_, ...), custom_call_target="tpu_custom_call" | custom-call | flops 1717986918400 | bytes 5872025600 | tf_op jit(solution)/shard_map/memory/pallas_call | solution.py:634
  163.9 6.2 %collective-permute-done.15.rest_2_ = bf16[4,128,1024]{2,1,0:T(8,128)(2,1)} collective-permute-done((bf16[4,128,1024]{2,1,0:T(8,128)(2,1)}, bf16[4,128,1024]{2,1,0:T(8,128)(2,1)}, u32[]{:S(2)}, u32[]{:S(2)}) %collective-permute-start.15) | collective-permute-done | bytes 1048608 | tf_op jit(solution)/shard_map/ppermute | solution.py:34
  170.2 8.1 %all-to-all-done.3.rest_2_ = bf16[4,128,1024]{2,1,0:T(8,128)(2,1)} async-done(((bf16[4,128,1024]{2,1,0:T(8,128)(2,1)}), bf16[4,128,1024]{2,1,0:T(8,128)(2,1)}, u32[]{:S(2)}, u32[]{:S(2)}) %all-to-all-start.3) | async-done | bytes 1048608 | tf_op jit(solution)/shard_map/all_to_all | solution.py:66
  188.6 17.7 %attend.3 = (bf16[512,1024]{1,0:T(8,128)(2,1)S(1)}, bf16[2,16,256,512]{3,2,1,0:T(8,128)(2,1)}) custom-call(s32[2]{0:T(128)S(1)} %copy-done.1, bf16[512,1024]{1,0:T(8,128)(2,1)S(1)} %copy-done.4, bf16[1024,1024]{1,0:T(8,128)(2,1)S(1)} %copy-done.19, bf16[1024,1024]{1,0:T(8,128)(2,1)S(1)} %copy-done.21), custom_call_target="tpu_custom_call" | custom-call | flops 1717986918400 | bytes 5872025600 | tf_op jit(solution)/shard_map/attend/pallas_call | solution.py:289
  211.7 7.1 %cross_out.1 = (f32[512,1024]{1,0:T(8,128)}, bf16[512,1024]{1,0:T(8,128)(2,1)}) custom-call(bf16[512,1024]{1,0:T(8,128)(2,1)} %copy-done.2, f32[512,1024]{1,0:T(8,128)} %get-tuple-element.248.res_ref.mid_ref, f32[17,1024]{1,0:T(8,128)} %bitcast.143, bf16[4,128,1024]{2,1,0:T(8,128)(2,1)} %all-to-all-done.1.rest_0_, ...), custom_call_target="tpu_custom_call" | custom-call | flops 429496729600 | bytes 4194304000 | tf_op jit(solution)/shard_map/cross_out/pallas_call | solution.py:575
  218.9 13.2 %collective-permute-done.20.rest_3_ = bf16[4,128,1024]{2,1,0:T(8,128)(2,1)} collective-permute-done((bf16[4,128,1024]{2,1,0:T(8,128)(2,1)}, bf16[4,128,1024]{2,1,0:T(8,128)(2,1)}, u32[]{:S(2)}, u32[]{:S(2)}) %collective-permute-start.20) | collective-permute-done | bytes 1048608 | tf_op jit(solution)/shard_map/ppermute | solution.py:34
  235.9 22.8 %ffn.2 = (f32[512,1024]{1,0:T(8,128)}, f32[512,1024]{1,0:T(8,128)}, f32[8,1024]{1,0:T(8,128)}, bf16[2,2,2,4,128,512]{5,4,3,2,1,0:T(8,128)(2,1)}, bf16[2,2,2,4,128,512]{5,4,3,2,1,0:T(8,128)(2,1)}) custom-call(bf16[512,1024]{1,0:T(8,128)(2,1)} %get-tuple-element.286.act_ref, bf16[512,1024]{1,0:T(8,128)(2,1)} %bitcast.151, ...), custom_call_target="tpu_custom_call" | custom-call | flops 5153960755200 | bytes 8388608000 | tf_op jit(solution)/shard_map/ffn/pallas_call | solution.py:958
  262.6 24.7 %ffn.3 = (bf16[512,1024]{1,0:T(8,128)(2,1)}, f32[512,1024]{1,0:T(8,128)}, bf16[512,1024]{1,0:T(8,128)(2,1)}, f32[8,1024]{1,0:T(8,128)}, f32[8,1024]{1,0:T(8,128)...) custom-call(bf16[512,1024]{1,0:T(8,128)(2,1)} %get-tuple-element.286.act_ref, ...), custom_call_target="tpu_custom_call" | custom-call | flops 5153960755200 | bytes 8388608000 | tf_op jit(solution)/shard_map/ffn/pallas_call | solution.py:958
  298.8 17.3 %attend_back.2 = (bf16[512,1024]{1,0:T(8,128)(2,1)S(1)}, bf16[1024,1024]{1,0:T(8,128)(2,1)S(1)}, bf16[1024,1024]{1,0:T(8,128)(2,1)S(1)}) custom-call(bf16[512,1024]{1,0:T(8,128)(2,1)S(1)} %copy-done.6, bf16[512,1024]{1,0:T(8,128)(2,1)S(1)} %copy-done.5, bf16[1024,1024]{1,0:T(8,128)(2,1)S(1)} %copy-done.20, bf16[1024,1024]{1,0:T(8,128)(2,1)S(1)} %copy-done.22, ...), custom_call_target="tpu_custom_call" | custom-call | flops 3435973836800 | bytes 7969177600 | tf_op jit(solution)/shard_map/attend_back/pallas_call | solution.py:341
  326.2 12.1 %cross_grads.1 = (bf16[2,2,2,4,128,512]{5,4,3,2,1,0:T(8,128)(2,1)}, bf16[2,2,2,4,128,512]{5,4,3,2,1,0:T(8,128)(2,1)}) custom-call(bf16[512,1024]{1,0:T(8,128)(2,1)} %get-tuple-element.308.a_ref.rest_0_, bf16[1024,1024]{1,0:T(8,128)(2,1)} %bitcast.150, bf16[512,1024]{1,0:T(8,128)(2,1)} %copy-done.2, bf16[512,1024]{1,0:T(8,128)(2,1)} %copy-done.9, ...), custom_call_target="tpu_custom_call" | custom-call | flops 2576980377600 | bytes 9227468800 | tf_op jit(solution)/shard_map/cross_grads/pallas_call | solution.py:833
  342.3 9.7 %cross_back.1 = (f32[512,1024]{1,0:T(8,128)}, bf16[512,1024]{1,0:T(8,128)(2,1)}, bf16[512,1024]{1,0:T(8,128)(2,1)}, f32[8,1024]{1,0:T(8,128)}) custom-call(bf16[512,1024]{1,0:T(8,128)(2,1)} %copy-done.9, f32[512,1024]{1,0:T(8,128)} %get-tuple-element.248.res_ref.mid_ref, f32[512,1024]{1,0:T(8,128)} %get-tuple-element.320.dmid_ref, f32[17,1024]{1,0:T(8,128)} %bitcast.146, ...), custom_call_target="tpu_custom_call" | custom-call | flops 858993459200 | bytes 5452595200 | tf_op jit(solution)/shard_map/cross_back/pallas_call | solution.py:724
  362.0 13.2 %attend_back.3 = (bf16[512,1024]{1,0:T(8,128)(2,1)S(1)}, bf16[512,1024]{1,0:T(8,128)(2,1)S(1)}, bf16[512,1024]{1,0:T(8,128)(2,1)S(1)}) custom-call(bf16[512,1024]{1,0:T(8,128)(2,1)S(1)} %copy-done.10, bf16[512,1024]{1,0:T(8,128)(2,1)S(1)} %copy-done.12, bf16[512,1024]{1,0:T(8,128)(2,1)S(1)} %copy-done.14, bf16[512,1024]{1,0:T(8,128)(2,1)S(1)} %copy-done.16, ...), custom_call_target="tpu_custom_call" | custom-call | flops 1717986918400 | bytes 4613734400 | tf_op jit(solution)/shard_map/attend_back/pallas_call | solution.py:341
  391.6 8.7 %self_grads.1 = (bf16[2,2,2,4,128,512]{5,4,3,2,1,0:T(8,128)(2,1)}, bf16[2,2,2,4,128,512]{5,4,3,2,1,0:T(8,128)(2,1)}) custom-call(bf16[512,1024]{1,0:T(8,128)(2,1)} %get-tuple-element.343.rest_0_, bf16[512,1024]{1,0:T(8,128)(2,1)} %copy-done.3, bf16[512,1024]{1,0:T(8,128)(2,1)} %copy-done.23, bf16[512,1024]{1,0:T(8,128)(2,1)} %copy-done.24, ...), custom_call_target="tpu_custom_call" | custom-call | flops 1717986918400 | bytes 5872025600 | tf_op jit(solution)/shard_map/self_grads/pallas_call | solution.py:833
  400.5 12.3 %self_back.1 = (f32[512,1024]{1,0:T(8,128)}, f32[8,1024]{1,0:T(8,128)}) custom-call(bf16[512,1024]{1,0:T(8,128)(2,1)} %copy-done.23, bf16[512,1024]{1,0:T(8,128)(2,1)} %copy-done.24, bf16[512,1024]{1,0:T(8,128)(2,1)} %copy-done.25, bf16[512,1024]{1,0:T(8,128)(2,1)} %bitcast.155, f32[512,1024]{1,0:T(8,128)} %get-tuple-element.323.dmid_ref, ...), custom_call_target="tpu_custom_call" | custom-call | flops 1288490188800 | bytes 6920601600 | tf_op jit(solution)/shard_map/self_back/pallas_call | solution.py:761
  435.8 10.2 %memory_back.1 = (f32[1024,1024]{1,0:T(8,128)}, f32[8,1024]{1,0:T(8,128)}) custom-call(bf16[1024,1024]{1,0:T(8,128)(2,1)} %copy-done.17, bf16[1024,1024]{1,0:T(8,128)(2,1)} %copy-done.18, bf16[4,128,1024]{2,1,0:T(8,128)(2,1)} %all-to-all-done.1.rest_0_, bf16[4,128,1024]{2,1,0:T(8,128)(2,1)} %collective-permute-done.10.rest_1_, ...), custom_call_target="tpu_custom_call" | custom-call | flops 1717986918400 | bytes 6710886400 | tf_op jit(solution)/shard_map/memory_back/pallas_call | solution.py:668
  503.7 8.9 %all-to-all-done.5 = bf16[4,128,1024]{2,1,0:T(8,128)(2,1)S(1)} async-done(((bf16[4,128,1024]{2,1,0:T(8,128)(2,1)}), bf16[4,128,1024]{2,1,0:T(8,128)(2,1)S(1)}, u32[]{:S(2)}, u32[]{:S(2)}) %all-to-all-start.5) | async-done | bytes 1048608 | tf_op jit(solution)/shard_map/all_to_all | solution.py:177
  520.0 8.0 %all_to_all.46 = bf16[4,17,128]{2,1,0:T(8,128)(2,1)S(1)} all-to-all(bf16[4,17,128]{2,1,0:T(8,128)(2,1)S(1)} %copy.64), channel_id=1, replica_groups={{0,2,4,6},{1,3,5,7},{8,10,12,14},{9,11,13,15},{16,18,20,22},{17,19,21,2..., dimensions={0} | all-to-all | bytes 34816 | tf_op jit(solution)/shard_map/all_to_all | solution.py:177
  (298 shorter events, 223.5 us)
Async XLA Ops:
  63.6 29.6 %collective-permute-start.6 = (bf16[2,4,136,512]{3,2,1,0:T(8,128)(2,1)}, bf16[2,4,136,512]{3,2,1,0:T(8,128)(2,1)}, u32[]{:S(2)}, u32[]{:S(2)}) collective-permute-start(bf16[2,4,136,512]{3,2,1,0:T(8,128)(2,1)} %pad_maximum_fusion.1.rest_2_.rest_10_), channel_id=1, source_target_pairs={{0,8},{8,0},{16,24},{24,16},{1,9},{9,1},{17,25},{25,17},{2,10},{10... | collective-permute-start | bytes 3342344 | tf_op jit(solution)/shard_map/ppermute | solution.py:31
  63.7 30.0 %collective-permute-start.4 = (bf16[2,4,136,512]{3,2,1,0:T(8,128)(2,1)}, bf16[2,4,136,512]{3,2,1,0:T(8,128)(2,1)}, u32[]{:S(2)}, u32[]{:S(2)}) collective-permute-start(bf16[2,4,136,512]{3,2,1,0:T(8,128)(2,1)} %pad_maximum_fusion.rest_0_.rest_8_), channel_id=1, source_target_pairs={{0,8},{8,0},{16,24},{24,16},{1,9},{9,1},{17,25},{25,17},{2,10},{10... | collective-permute-start | bytes 3342344 | tf_op jit(solution)/shard_map/ppermute | solution.py:31
  86.4 34.0 %all-to-all-start.2 = ((bf16[4,128,1024]{2,1,0:T(8,128)(2,1)}), bf16[4,128,1024]{2,1,0:T(8,128)(2,1)}, u32[]{:S(2)}, u32[]{:S(2)}) async-start(bf16[4,128,1024]{2,1,0:T(8,128)(2,1)} %broadcast_in_dim.32), calls=%async_computation.2 | async-start | bytes 2097152 | tf_op jit(solution)/shard_map/all_to_all | solution.py:66
  90.7 29.7 %collective-permute-start.10 = (bf16[4,128,1024]{2,1,0:T(8,128)(2,1)}, bf16[4,128,1024]{2,1,0:T(8,128)(2,1)}, u32[]{:S(2)}, u32[]{:S(2)}) collective-permute-start(bf16[4,128,1024]{2,1,0:T(8,128)(2,1)} %all-to-all-done.1.rest_0_), channel_id=1, source_target_pairs={{0,1},{1,0},{2,3},{3,2},{4,5},{5,4},{6,7},{7,6},{8,9},{9,8},{10,11... | collective-permute-start | bytes 3145736 | tf_op jit(solution)/shard_map/ppermute | solution.py:37
  118.4 35.3 %collective-permute-start.13 = (bf16[4,128,1024]{2,1,0:T(8,128)(2,1)}, bf16[4,128,1024]{2,1,0:T(8,128)(2,1)}, u32[]{:S(2)}, u32[]{:S(2)}) collective-permute-start(bf16[4,128,1024]{2,1,0:T(8,128)(2,1)} %collective-permute-done.9.rest_2_), channel_id=1, source_target_pairs={{0,8},{8,0},{16,24},{24,16},{1,9},{9,1},{17,25},{25,17},{2,10},{10... | collective-permute-start | bytes 3145736 | tf_op jit(solution)/shard_map/ppermute | solution.py:31
  120.4 33.3 %collective-permute-start.12 = (bf16[4,128,1024]{2,1,0:T(8,128)(2,1)}, bf16[4,128,1024]{2,1,0:T(8,128)(2,1)}, u32[]{:S(2)}, u32[]{:S(2)}) collective-permute-start(bf16[4,128,1024]{2,1,0:T(8,128)(2,1)} %collective-permute-done.10.rest_1_), channel_id=1, source_target_pairs={{0,8},{8,0},{16,24},{24,16},{1,9},{9,1},{17,25},{25,17},{2,10},{10... | collective-permute-start | bytes 3145736 | tf_op jit(solution)/shard_map/ppermute | solution.py:31
  146.9 31.4 %all-to-all-start.3 = ((bf16[4,128,1024]{2,1,0:T(8,128)(2,1)}), bf16[4,128,1024]{2,1,0:T(8,128)(2,1)}, u32[]{:S(2)}, u32[]{:S(2)}) async-start(bf16[4,128,1024]{2,1,0:T(8,128)(2,1)} %broadcast_in_dim.33), calls=%async_computation.3 | async-start | bytes 2097152 | tf_op jit(solution)/shard_map/all_to_all | solution.py:66
  152.1 33.8 %collective-permute-start.17 = (bf16[4,128,1024]{2,1,0:T(8,128)(2,1)}, bf16[4,128,1024]{2,1,0:T(8,128)(2,1)}, u32[]{:S(2)}, u32[]{:S(2)}) collective-permute-start(bf16[4,128,1024]{2,1,0:T(8,128)(2,1)} %all-to-all-done.2.rest_0_), channel_id=1, source_target_pairs={{0,1},{1,0},{2,3},{3,2},{4,5},{5,4},{6,7},{7,6},{8,9},{9,8},{10,11... | collective-permute-start | bytes 3145736 | tf_op jit(solution)/shard_map/ppermute | solution.py:37
  183.7 48.3 %collective-permute-start.21 = (bf16[4,128,1024]{2,1,0:T(8,128)(2,1)}, bf16[4,128,1024]{2,1,0:T(8,128)(2,1)}, u32[]{:S(2)}, u32[]{:S(2)}) collective-permute-start(bf16[4,128,1024]{2,1,0:T(8,128)(2,1)} %all-to-all-done.3.rest_2_), channel_id=1, source_target_pairs={{0,1},{1,0},{2,3},{3,2},{4,5},{5,4},{6,7},{7,6},{8,9},{9,8},{10,11... | collective-permute-start | bytes 3145736 | tf_op jit(solution)/shard_map/ppermute | solution.py:37
  185.9 46.2 %collective-permute-start.20 = (bf16[4,128,1024]{2,1,0:T(8,128)(2,1)}, bf16[4,128,1024]{2,1,0:T(8,128)(2,1)}, u32[]{:S(2)}, u32[]{:S(2)}) collective-permute-start(bf16[4,128,1024]{2,1,0:T(8,128)(2,1)} %collective-permute-done.17.rest_1_), channel_id=1, source_target_pairs={{0,16},{8,24},{16,0},{24,8},{1,17},{9,25},{17,1},{25,9},{2,18},{10... | collective-permute-start | bytes 3145736 | tf_op jit(solution)/shard_map/ppermute | solution.py:34
  259.0 28.6 %collective-permute-start.29 = (bf16[2,2,2,4,128,512]{5,4,3,2,1,0:T(8,128)(2,1)}, bf16[2,2,2,4,128,512]{5,4,3,2,1,0:T(8,128)(2,1)}, u32[]{:S(2)}, u32[]{:S(2)}) collective-permute-start(bf16[2,2,2,4,128,512]{5,4,3,2,1,0:T(8,128)(2,1)} %get-tuple-element.285), channel_id=1, source_target_pairs={{0,8},{8,0},{16,24},{24,16},{1,9},{9,1},{17,25},{25,17},{2,10},{10... | collective-permute-start | bytes 12582920 | tf_op jit(solution)/shard_map/ppermute | solution.py:31
  287.3 32.6 %collective-permute-start.31 = (bf16[2,2,2,4,128,512]{5,4,3,2,1,0:T(8,128)(2,1)}, bf16[2,2,2,4,128,512]{5,4,3,2,1,0:T(8,128)(2,1)}, u32[]{:S(2)}, u32[]{:S(2)}) collective-permute-start(bf16[2,2,2,4,128,512]{5,4,3,2,1,0:T(8,128)(2,1)} %get-tuple-element.297), channel_id=1, source_target_pairs={{0,8},{8,0},{16,24},{24,16},{1,9},{9,1},{17,25},{25,17},{2,10},{10... | collective-permute-start | bytes 12582920 | tf_op jit(solution)/shard_map/ppermute | solution.py:31
  290.8 35.4 %collective-permute-start.32 = (bf16[2,4,128,512]{3,2,1,0:T(8,128)(2,1)}, bf16[2,4,128,512]{3,2,1,0:T(8,128)(2,1)}, u32[]{:S(2)}, u32[]{:S(2)}) collective-permute-start(bf16[2,4,128,512]{3,2,1,0:T(8,128)(2,1)} %get-tuple-element.295), channel_id=1, source_target_pairs={{0,1},{1,0},{2,3},{3,2},{4,5},{5,4},{6,7},{7,6},{8,9},{9,8},{10,11... | collective-permute-start | bytes 3145736 | tf_op jit(solution)/shard_map/ppermute | solution.py:37
  291.3 34.9 %collective-permute-start.30 = (bf16[2,4,128,512]{3,2,1,0:T(8,128)(2,1)}, bf16[2,4,128,512]{3,2,1,0:T(8,128)(2,1)}, u32[]{:S(2)}, u32[]{:S(2)}) collective-permute-start(bf16[2,4,128,512]{3,2,1,0:T(8,128)(2,1)} %get-tuple-element.293), channel_id=1, source_target_pairs={{0,16},{8,24},{16,0},{24,8},{1,17},{9,25},{17,1},{25,9},{2,18},{10... | collective-permute-start | bytes 3145736 | tf_op jit(solution)/shard_map/ppermute | solution.py:34
  323.2 33.9 %collective-permute-start.35 = (bf16[2,4,128,512]{3,2,1,0:T(8,128)(2,1)}, bf16[2,4,128,512]{3,2,1,0:T(8,128)(2,1)}, u32[]{:S(2)}, u32[]{:S(2)}) collective-permute-start(bf16[2,4,128,512]{3,2,1,0:T(8,128)(2,1)} %get-tuple-element.307), channel_id=1, source_target_pairs={{0,1},{1,0},{2,3},{3,2},{4,5},{5,4},{6,7},{7,6},{8,9},{9,8},{10,11... | collective-permute-start | bytes 3145736 | tf_op jit(solution)/shard_map/ppermute | solution.py:37
  324.7 33.9 %collective-permute-start.34 = (bf16[2,4,128,512]{3,2,1,0:T(8,128)(2,1)}, bf16[2,4,128,512]{3,2,1,0:T(8,128)(2,1)}, u32[]{:S(2)}, u32[]{:S(2)}) collective-permute-start(bf16[2,4,128,512]{3,2,1,0:T(8,128)(2,1)} %get-tuple-element.305), channel_id=1, source_target_pairs={{0,16},{8,24},{16,0},{24,8},{1,17},{9,25},{17,1},{25,9},{2,18},{10... | collective-permute-start | bytes 3145736 | tf_op jit(solution)/shard_map/ppermute | solution.py:34
  341.2 36.9 %collective-permute-start.37 = (bf16[4,128,512]{2,1,0:T(8,128)(2,1)}, bf16[4,128,512]{2,1,0:T(8,128)(2,1)}, u32[]{:S(2)}, u32[]{:S(2)}) collective-permute-start(bf16[4,128,512]{2,1,0:T(8,128)(2,1)} %get-tuple-element.317), channel_id=1, source_target_pairs={{0,16},{8,24},{16,0},{24,8},{1,17},{9,25},{17,1},{25,9},{2,18},{10... | collective-permute-start | bytes 1572872 | tf_op jit(solution)/shard_map/ppermute | solution.py:34
  341.8 36.3 %collective-permute-start.36 = (bf16[4,128,512]{2,1,0:T(8,128)(2,1)}, bf16[4,128,512]{2,1,0:T(8,128)(2,1)}, u32[]{:S(2)}, u32[]{:S(2)}) collective-permute-start(bf16[4,128,512]{2,1,0:T(8,128)(2,1)} %get-tuple-element.315), channel_id=1, source_target_pairs={{0,1},{1,0},{2,3},{3,2},{4,5},{5,4},{6,7},{7,6},{8,9},{9,8},{10,11... | collective-permute-start | bytes 1572872 | tf_op jit(solution)/shard_map/ppermute | solution.py:37
  355.5 44.9 %collective-permute-start.39 = (bf16[2,4,128,512]{3,2,1,0:T(8,128)(2,1)}, bf16[2,4,128,512]{3,2,1,0:T(8,128)(2,1)}, u32[]{:S(2)}, u32[]{:S(2)}) collective-permute-start(bf16[2,4,128,512]{3,2,1,0:T(8,128)(2,1)} %get-tuple-element.328), channel_id=1, source_target_pairs={{0,1},{1,0},{2,3},{3,2},{4,5},{5,4},{6,7},{7,6},{8,9},{9,8},{10,11... | collective-permute-start | bytes 3145736 | tf_op jit(solution)/shard_map/ppermute | solution.py:37
  357.1 43.4 %collective-permute-start.38 = (bf16[2,4,128,512]{3,2,1,0:T(8,128)(2,1)}, bf16[2,4,128,512]{3,2,1,0:T(8,128)(2,1)}, u32[]{:S(2)}, u32[]{:S(2)}) collective-permute-start(bf16[2,4,128,512]{3,2,1,0:T(8,128)(2,1)} %get-tuple-element.326), channel_id=1, source_target_pairs={{0,16},{8,24},{16,0},{24,8},{1,17},{9,25},{17,1},{25,9},{2,18},{10... | collective-permute-start | bytes 3145736 | tf_op jit(solution)/shard_map/ppermute | solution.py:34
  383.6 40.4 %all-to-all-start.4 = ((bf16[4,128,1024]{2,1,0:T(8,128)(2,1)}), bf16[4,128,1024]{2,1,0:T(8,128)(2,1)}, u32[]{:S(2)}, u32[]{:S(2)}) async-start(bf16[4,128,1024]{2,1,0:T(8,128)(2,1)} %pad_maximum_fusion.2), calls=%async_computation.4 | async-start | bytes 2097152 | tf_op jit(solution)/shard_map/all_to_all | solution.py:177
  400.4 31.1 %collective-permute-start.40 = (bf16[2,2,2,4,128,512]{5,4,3,2,1,0:T(8,128)(2,1)}, bf16[2,2,2,4,128,512]{5,4,3,2,1,0:T(8,128)(2,1)}, u32[]{:S(2)}, u32[]{:S(2)}) collective-permute-start(bf16[2,2,2,4,128,512]{5,4,3,2,1,0:T(8,128)(2,1)} %get-tuple-element.348), channel_id=1, source_target_pairs={{0,8},{8,0},{16,24},{24,16},{1,9},{9,1},{17,25},{25,17},{2,10},{10... | collective-permute-start | bytes 12582920 | tf_op jit(solution)/shard_map/ppermute | solution.py:31
  424.0 31.2 %all-to-all-start.6 = ((bf16[4,128,1024]{2,1,0:T(8,128)(2,1)}), bf16[4,128,1024]{2,1,0:T(8,128)(2,1)}, u32[]{:S(2)}, u32[]{:S(2)}) async-start(bf16[4,128,1024]{2,1,0:T(8,128)(2,1)} %pad_maximum_fusion.3), calls=%async_computation.6 | async-start | bytes 2097152 | tf_op jit(solution)/shard_map/all_to_all | solution.py:177
  455.2 29.6 %all-to-all-start.7 = ((bf16[4,128,1024]{2,1,0:T(8,128)(2,1)}), bf16[4,128,1024]{2,1,0:T(8,128)(2,1)S(1)}, u32[]{:S(2)}, u32[]{:S(2)}) async-start(bf16[4,128,1024]{2,1,0:T(8,128)(2,1)} %pad_maximum_fusion.5), calls=%async_computation.7 | async-start | bytes 2097152 | tf_op jit(solution)/shard_map/all_to_all | solution.py:177
  (90 other events, 999.3 us)

commit v4 on v3

--- a/solution.py
+++ b/solution.py
@@ -842,25 +842,34 @@
     )(*lefts, *rights)
 
 
-def sums_kernel(counts, *rest):
+def sums_kernel(counts, joined, *rest):
     ins, outs = rest[: sum(counts)], rest[sum(counts) :]
     at_in = 0
-    for out, count in zip(outs, counts):
+    for i, count in enumerate(counts):
         total = ins[at_in][...].astype(F32)
         for r in ins[at_in + 1 : at_in + count]:
             total = total + r[...].astype(F32)
-        out[...] = total.astype(BF).reshape(out.shape)
         at_in += count
-
-
-def sums(steps, *groups):
+        total = total.astype(BF)
+        if joined:
+            wide = total.shape[-1]
+            outs[0][:, :, i * wide : (i + 1) * wide] = total
+        else:
+            outs[i][...] = total.reshape(outs[i].shape)
+
+
+def sums(steps, *groups, joined=False):
     ins = [i for _, _, _, members in groups for i in members]
-    return pl.pallas_call(
-        partial(sums_kernel, tuple(len(g[3]) for g in groups)),
+    outs = [g[:3] for g in groups]
+    if joined:
+        (p, m, n), (q, _, _), to = outs[0]
+        outs = [((p, m, n * len(groups)), (q, m, n * len(groups)), to)]
+    out = pl.pallas_call(
+        partial(sums_kernel, tuple(len(g[3]) for g in groups), joined),
         grid=(steps,),
         in_specs=[pl.BlockSpec(block, to) for _, block, to in ins],
-        out_specs=[pl.BlockSpec(g[1], g[2]) for g in groups],
-        out_shape=[shape(g[0], BF) for g in groups],
+        out_specs=[pl.BlockSpec(o[1], o[2]) for o in outs],
+        out_shape=[shape(o[0], BF) for o in outs],
         cost_estimate=pl.CostEstimate(
             flops=0,
             transcendentals=0,
@@ -868,6 +877,7 @@
         ),
         name="sums",
     )(*[v for v, _, _ in ins])
+    return out[0] if joined else out
 
 
 def grads_of(left, lefts, rights, sides, name):
@@ -1333,7 +1343,7 @@
             members = [(k, block, at_k), (r, block, at_k), (came, part, third)]
             members += [(v, (2, m, half), plain) for v in more]
             groups.append(((4, m, half), (2, m, half), plain, members))
-        return sums(2, *groups)
+        return sums(2, *groups, joined=name == "stay")
 
     def two(self):
         self.from_x, self.from_y = self.order.see(self.from_x), self.order.see(self.from_y)
@@ -1343,8 +1353,8 @@
 
     def ring(self):
         see = self.order.see
-        first, second = self.rest("stay", [see(self.next_y), see(self.next_x)])
-        self.own = self.order.send(partial(ring_sum, self.place), jnp.concatenate([first, second], 2))
+        both = self.rest("stay", [see(self.next_y), see(self.next_x)])
+        self.own = self.order.send(partial(ring_sum, self.place), both)
 
     def last_x(self):
         self.own = self.order.see(self.own)
@@ -1405,9 +1415,8 @@
         return at(jnp.stack(shards), rank)
 
     u_self = HalfUnit(place, order, pack((self_query, self_key, self_value, self_output), small))
-    u_self.ring()
     later = (cross_query, cross_key, cross_value, cross_output, expand_weight, down_projection_weight)
-    *later, _ = lax.optimization_barrier((*later, u_self.a0))
+    *later, _ = lax.optimization_barrier((*later, u_self.piece))
     w_e = later[4].reshape(m, rows, 4, -1).transpose(2, 0, 1, 3).reshape(4, m, d)
     w_d = later[5].reshape(4, m, d)
     unit = partial(Unit, place, order)
@@ -1420,13 +1429,14 @@
     dy = output_grad.reshape(batch * seq, d)
     run = order.run
 
+    u_self.ring()
+    u_cross.ring()
     u_self.one()
-    u_cross.ring()
     u_self.two()
-    u_self.core()
-    u_low.ring()
     u_cross.pair()
     u_cross.across()
+    u_low.ring()
+    u_self.core()
     u_cross.near()
     self_w = u_self.refs
     both = jnp.stack([v[:, :, m:] for v in (u_self.p0, jnp.stack([u_self.p1[0], u_self.q1[0]]))])
@@ -1434,19 +1444,19 @@
     both = jnp.where(place.y == 0, both, both[:, ::-1]).reshape(rows, -1)
     vecs = both[:, : count * m].reshape(rows, count, m).transpose(1, 0, 2).reshape(count, d).astype(F32)
     act1, q, k, v = run(first, x, vecs, self_w, m)
+    u_cross.two()
     o, p = run(attend, q, k, v, prefix_length, batch, True)
-    u_cross.two()
+    u_high.ring()
     u_low.across()
     u_cross.both()
-    u_high.ring()
     mid1, act2 = run(project, o, x, vecs, (4, 5, 6, None), (self_w,), (3,), m, "self_out")
     u_low.pair()
     u_low.near()
     u_cross.core()
     cross_w = u_cross.refs
     ck, cv = run(memory, e, vecs, cross_w, m)
+    u_high.across()
     cq = run(query, act2, vecs, 7, cross_w, m)
-    u_high.across()
     u_high.pair()
     u_low.two()
     co, cp = run(attend, cq, ck, cv, prefix_length, batch, False)
@@ -1455,8 +1465,8 @@
     u_high.near()
     mid2, act3 = run(project, co, mid1, vecs, (9, 10, 11, None), (cross_w,), (3,), m, "cross_out")
     u_low.core()
+    u_high.both()
     low_w = u_low.refs
-    u_high.both()
 
     *begin, dbe_low, away, keep = run(ffn, act3, dy, mid2, vecs, low_w, m, (), 13)
     total = partial(Sum, place, order)

time: 542 us -> 531 us (0.980)
  other arithmetic: 18.7 us -> 9.58 us
    ppermute x16, waiting for transfers between devices: 32.8 us -> 15.4 us  [pair(): return lax.ppermute(v, 'fsdp', [(i, i ^ 1) for i in range(self.rows)])]
    concatenate x4 -> x0, other arithmetic: 9.15 us -> none  [ring(): jnp.concatenate([first, second], 2)]
    all_to_all x3, waiting for transfers between devices: 11.8 us -> 18.2 us  [ring_gather(): lax.all_to_all(copies, 'fsdp', 0, 0, axis_index_groups=place.ring_members())]
  transfers between devices with their start and end apart: 67 -> 67, of which waited for: 20 -> 19; matrix products, arithmetic and copies ran while one was open for 6% -> 5% of each run, Pallas kernels for 46% -> 47%
where the time goes in v4:
time: 531 us; the launch traced here: 522 us
  Pallas kernels  250 us (47%)
  waiting for transfers between devices  103 us (19%)
  starting transfers between devices  72.6 us (14%)
  local copies, waits for them, and re-layouts  43.5 us (8%)
  blocking collectives  41.2 us (8%)
  other arithmetic  9.58 us (2%)
    ppermute x19, waiting for transfers between devices, across(): return lax.ppermute(v, 'replica', [(i, i ^ 2) for i in range(self.groups)])  48.4 us
    pallas_call x2, Pallas kernels, ffn(): pl.pallas_call(partial(ffn_kernel, last, first_row), in_specs=[WHOLE] * (...  47.6 us
    pallas_call x12, Pallas kernels, sums(): pl.pallas_call(partial(sums_kernel, tuple((len(g[3]) for g in groups)), j...  37.5 us
    all_to_all x1, blocking collectives, ring_gather(): lax.all_to_all(copies, 'fsdp', 0, 0, axis_index_groups=place.ring_members())  33.2 us
    pallas_call x2, Pallas kernels, attend_back(): pl.pallas_call(partial(attend_back_kernel, (d // H) ** (-0.5)), grid=(bat...  30.5 us
    pallas_call x2, Pallas kernels, attend(): pl.pallas_call(partial(attend_kernel, masked, (d // H) ** (-0.5)), grid_s...  28 us
    unnamed x98, local copies, waits for them, and re-layouts  27 us
    ppermute x19, starting transfers between devices, across(): return lax.ppermute(v, 'replica', [(i, i ^ 2) for i in range(self.groups)])  22.1 us
  transfers between devices with their start and end apart: 67, of which 19 were waited for; matrix products, arithmetic and copies ran while one was open for 5% of the time, Pallas kernels for 47%

profile of v4, /device:TPU:0, one launch (start us, length us, event | category | flops | bytes accessed | tf_op | source)
XLA Modules:
  0.0 522.1 jit_solution(9832887083829470148)
XLA Ops:
  3.8 33.2 %all_to_all.45 = bf16[4,2,136,512]{3,2,1,0:T(8,128)(2,1)S(1)} all-to-all(bf16[4,2,136,512]{3,2,1,0:T(8,128)(2,1)S(1)} %broadcast_in_dim.12), channel_id=1, replica_groups={{0,2,4,6},{1,3,5,7},{8,10,12,14},{9,11,13,15},{16,18,20,22},{17,19,21,2..., dimensions={0} | all-to-all | bytes 2228224 | tf_op jit(solution)/shard_map/all_to_all | solution.py:66
  40.3 10.5 %collective-permute-done.1 = bf16[4,136,512]{2,1,0:T(8,128)(2,1)S(1)} collective-permute-done((bf16[4,136,512]{2,1,0:T(8,128)(2,1)S(1)}, bf16[4,136,512]{2,1,0:T(8,128)(2,1)S(1)}, u32[]{:S(2)}, u32[]{:S(2)}) %collective-permute-start.1) | collective-permute-done | bytes 557088 | tf_op jit(solution)/shard_map/ppermute | solution.py:34
  64.9 11.9 %collective-permute-done.3.rest_3_.rest_11_ = bf16[2,4,136,512]{3,2,1,0:T(8,128)(2,1)} collective-permute-done((bf16[2,4,136,512]{3,2,1,0:T(8,128)(2,1)}, bf16[2,4,136,512]{3,2,1,0:T(8,128)(2,1)}, u32[]{:S(2)}, u32[]{:S(2)}) %collective-permute-start.3) | collective-permute-done | bytes 1114144 | tf_op jit(solution)/shard_map/ppermute | solution.py:37
  93.9 7.6 %first.1 = (bf16[512,1024]{1,0:T(8,128)(2,1)}, bf16[512,1024]{1,0:T(8,128)(2,1)}, bf16[512,1024]{1,0:T(8,128)(2,1)}, bf16[512,1024]{1,0:T(8,128)(2,1)}) custom-call(bf16[512,1024]{1,0:T(8,128)(2,1)} %bitcast.153, f32[17,1024]{1,0:T(8,128)} %bitcast.139, bf16[2,4,136,512]{3,2,1,0:T(8,128)(2,1)} %pad_maximum_fusion.rest_0_.rest_8_, ...), custom_call_target="tpu_custom_call" | custom-call | flops 1288490188800 | bytes 5662310400 | tf_op jit(solution)/shard_map/first/pallas_call | solution.py:528
  101.5 17.7 %collective-permute-done.8.rest_2_ = bf16[4,128,1024]{2,1,0:T(8,128)(2,1)} collective-permute-done((bf16[4,128,1024]{2,1,0:T(8,128)(2,1)}, bf16[4,128,1024]{2,1,0:T(8,128)(2,1)}, u32[]{:S(2)}, u32[]{:S(2)}) %collective-permute-start.8) | collective-permute-done | bytes 1048608 | tf_op jit(solution)/shard_map/ppermute | solution.py:34
  124.3 10.3 %attend.2 = (bf16[512,1024]{1,0:T(8,128)(2,1)S(1)}, bf16[2,16,256,256]{3,2,1,0:T(8,128)(2,1)S(1)}) custom-call(s32[2]{0:T(128)S(1)} %copy-done, bf16[512,1024]{1,0:T(8,128)(2,1)S(1)} %copy-done.11, bf16[512,1024]{1,0:T(8,128)(2,1)S(1)} %copy-done.13, bf16[512,1024]{1,0:T(8,128)(2,1)S(1)} %copy-done.15), custom_call_target="tpu_custom_call" | custom-call | flops 858993459200 | bytes 3355443200 | tf_op jit(solution)/shard_map/attend/pallas_call | solution.py:289
  138.2 6.9 %self_out.1 = (f32[512,1024]{1,0:T(8,128)}, bf16[512,1024]{1,0:T(8,128)(2,1)}) custom-call(bf16[512,1024]{1,0:T(8,128)(2,1)} %copy-done.3, bf16[512,1024]{1,0:T(8,128)(2,1)} %bitcast.154, f32[17,1024]{1,0:T(8,128)} %bitcast.140, bf16[2,4,136,512]{3,2,1,0:T(8,128)(2,1)} %pad_maximum_fusion.rest_0_.rest_8_, ...), custom_call_target="tpu_custom_call" | custom-call | flops 429496729600 | bytes 4299161600 | tf_op jit(solution)/shard_map/self_out/pallas_call | solution.py:575
  153.7 9.2 %memory.1 = (bf16[1024,1024]{1,0:T(8,128)(2,1)}, bf16[1024,1024]{1,0:T(8,128)(2,1)}) custom-call(bf16[1024,1024]{1,0:T(8,128)(2,1)} %bitcast.149, f32[17,1024]{1,0:T(8,128)} %bitcast.141, bf16[4,128,1024]{2,1,0:T(8,128)(2,1)} %all-to-all-done.1.rest_0_, bf16[4,128,1024]{2,1,0:T(8,128)(2,1)} %collective-permute-done.10.rest_1_, ...), custom_call_target="tpu_custom_call" | custom-call | flops 1717986918400 | bytes 5872025600 | tf_op jit(solution)/shard_map/memory/pallas_call | solution.py:634
  162.9 15.3 %all-to-all-done.3.rest_2_ = bf16[4,128,1024]{2,1,0:T(8,128)(2,1)} async-done(((bf16[4,128,1024]{2,1,0:T(8,128)(2,1)}), bf16[4,128,1024]{2,1,0:T(8,128)(2,1)}, u32[]{:S(2)}, u32[]{:S(2)}) %all-to-all-start.3) | async-done | bytes 1048608 | tf_op jit(solution)/shard_map/all_to_all | solution.py:66
  187.5 17.7 %attend.3 = (bf16[512,1024]{1,0:T(8,128)(2,1)S(1)}, bf16[2,16,256,512]{3,2,1,0:T(8,128)(2,1)}) custom-call(s32[2]{0:T(128)S(1)} %copy-done.1, bf16[512,1024]{1,0:T(8,128)(2,1)S(1)} %copy-done.4, bf16[1024,1024]{1,0:T(8,128)(2,1)S(1)} %copy-done.19, bf16[1024,1024]{1,0:T(8,128)(2,1)S(1)} %copy-done.21), custom_call_target="tpu_custom_call" | custom-call | flops 1717986918400 | bytes 5872025600 | tf_op jit(solution)/shard_map/attend/pallas_call | solution.py:289
  206.7 7.1 %cross_out.1 = (f32[512,1024]{1,0:T(8,128)}, bf16[512,1024]{1,0:T(8,128)(2,1)}) custom-call(bf16[512,1024]{1,0:T(8,128)(2,1)} %copy-done.2, f32[512,1024]{1,0:T(8,128)} %get-tuple-element.246.res_ref.mid_ref, f32[17,1024]{1,0:T(8,128)} %bitcast.143, bf16[4,128,1024]{2,1,0:T(8,128)(2,1)} %all-to-all-done.1.rest_0_, ...), custom_call_target="tpu_custom_call" | custom-call | flops 429496729600 | bytes 4194304000 | tf_op jit(solution)/shard_map/cross_out/pallas_call | solution.py:575
  213.8 11.3 %collective-permute-done.20.rest_3_ = bf16[4,128,1024]{2,1,0:T(8,128)(2,1)} collective-permute-done((bf16[4,128,1024]{2,1,0:T(8,128)(2,1)}, bf16[4,128,1024]{2,1,0:T(8,128)(2,1)}, u32[]{:S(2)}, u32[]{:S(2)}) %collective-permute-start.20) | collective-permute-done | bytes 1048608 | tf_op jit(solution)/shard_map/ppermute | solution.py:34
  229.0 22.9 %ffn.2 = (f32[512,1024]{1,0:T(8,128)}, f32[512,1024]{1,0:T(8,128)}, f32[8,1024]{1,0:T(8,128)}, bf16[2,2,2,4,128,512]{5,4,3,2,1,0:T(8,128)(2,1)}, bf16[2,2,2,4,128,512]{5,4,3,2,1,0:T(8,128)(2,1)}) custom-call(bf16[512,1024]{1,0:T(8,128)(2,1)} %get-tuple-element.286.act_ref, bf16[512,1024]{1,0:T(8,128)(2,1)} %bitcast.151, ...), custom_call_target="tpu_custom_call" | custom-call | flops 5153960755200 | bytes 8388608000 | tf_op jit(solution)/shard_map/ffn/pallas_call | solution.py:968
  255.8 24.7 %ffn.3 = (bf16[512,1024]{1,0:T(8,128)(2,1)}, f32[512,1024]{1,0:T(8,128)}, bf16[512,1024]{1,0:T(8,128)(2,1)}, f32[8,1024]{1,0:T(8,128)}, f32[8,1024]{1,0:T(8,128)...) custom-call(bf16[512,1024]{1,0:T(8,128)(2,1)} %get-tuple-element.286.act_ref, ...), custom_call_target="tpu_custom_call" | custom-call | flops 5153960755200 | bytes 8388608000 | tf_op jit(solution)/shard_map/ffn/pallas_call | solution.py:968
  286.1 5.7 %output_back.1.do_ref = bf16[512,1024]{1,0:T(8,128)(2,1)} custom-call(bf16[512,1024]{1,0:T(8,128)(2,1)} %get-tuple-element.298.d_ref.rest_6_, bf16[4,128,1024]{2,1,0:T(8,128)(2,1)} %all-to-all-done.1.rest_0_, bf16[4,128,1024]{2,1,0:T(8,128)(2,1)} %collective-permute-done.10.rest_1_, bf16[4,128,1024]{2,1,0:T(8,128)(2,1)} %collective-permute-done.8.rest_2_, ...), custom_call_target="tpu_custom_call" | custom-call | flops 429496729600 | bytes 1677721600 | tf_op jit(solution)/shard_map/output_back/pallas_call | solution.py:786
  293.1 17.3 %attend_back.2 = (bf16[512,1024]{1,0:T(8,128)(2,1)S(1)}, bf16[1024,1024]{1,0:T(8,128)(2,1)S(1)}, bf16[1024,1024]{1,0:T(8,128)(2,1)S(1)}) custom-call(bf16[512,1024]{1,0:T(8,128)(2,1)S(1)} %copy-done.6, bf16[512,1024]{1,0:T(8,128)(2,1)S(1)} %copy-done.5, bf16[1024,1024]{1,0:T(8,128)(2,1)S(1)} %copy-done.20, bf16[1024,1024]{1,0:T(8,128)(2,1)S(1)} %copy-done.22, ...), custom_call_target="tpu_custom_call" | custom-call | flops 3435973836800 | bytes 7969177600 | tf_op jit(solution)/shard_map/attend_back/pallas_call | solution.py:341
  319.4 12.1 %cross_grads.1 = (bf16[2,2,2,4,128,512]{5,4,3,2,1,0:T(8,128)(2,1)}, bf16[2,2,2,4,128,512]{5,4,3,2,1,0:T(8,128)(2,1)}) custom-call(bf16[512,1024]{1,0:T(8,128)(2,1)} %get-tuple-element.308.a_ref.rest_0_, bf16[1024,1024]{1,0:T(8,128)(2,1)} %bitcast.150, bf16[512,1024]{1,0:T(8,128)(2,1)} %copy-done.2, bf16[512,1024]{1,0:T(8,128)(2,1)} %copy-done.9, ...), custom_call_target="tpu_custom_call" | custom-call | flops 2576980377600 | bytes 9227468800 | tf_op jit(solution)/shard_map/cross_grads/pallas_call | solution.py:833
  336.5 9.7 %cross_back.1 = (f32[512,1024]{1,0:T(8,128)}, bf16[512,1024]{1,0:T(8,128)(2,1)}, bf16[512,1024]{1,0:T(8,128)(2,1)}, f32[8,1024]{1,0:T(8,128)}) custom-call(bf16[512,1024]{1,0:T(8,128)(2,1)} %copy-done.9, f32[512,1024]{1,0:T(8,128)} %get-tuple-element.246.res_ref.mid_ref, f32[512,1024]{1,0:T(8,128)} %get-tuple-element.320.dmid_ref, f32[17,1024]{1,0:T(8,128)} %bitcast.146, ...), custom_call_target="tpu_custom_call" | custom-call | flops 858993459200 | bytes 5452595200 | tf_op jit(solution)/shard_map/cross_back/pallas_call | solution.py:724
  355.2 13.2 %attend_back.3 = (bf16[512,1024]{1,0:T(8,128)(2,1)S(1)}, bf16[512,1024]{1,0:T(8,128)(2,1)S(1)}, bf16[512,1024]{1,0:T(8,128)(2,1)S(1)}) custom-call(bf16[512,1024]{1,0:T(8,128)(2,1)S(1)} %copy-done.10, bf16[512,1024]{1,0:T(8,128)(2,1)S(1)} %copy-done.12, bf16[512,1024]{1,0:T(8,128)(2,1)S(1)} %copy-done.14, bf16[512,1024]{1,0:T(8,128)(2,1)S(1)} %copy-done.16, ...), custom_call_target="tpu_custom_call" | custom-call | flops 1717986918400 | bytes 4613734400 | tf_op jit(solution)/shard_map/attend_back/pallas_call | solution.py:341
  383.6 8.7 %self_grads.1 = (bf16[2,2,2,4,128,512]{5,4,3,2,1,0:T(8,128)(2,1)}, bf16[2,2,2,4,128,512]{5,4,3,2,1,0:T(8,128)(2,1)}) custom-call(bf16[512,1024]{1,0:T(8,128)(2,1)} %get-tuple-element.341.rest_0_, bf16[512,1024]{1,0:T(8,128)(2,1)} %copy-done.3, bf16[512,1024]{1,0:T(8,128)(2,1)} %copy-done.23, bf16[512,1024]{1,0:T(8,128)(2,1)} %copy-done.24, ...), custom_call_target="tpu_custom_call" | custom-call | flops 1717986918400 | bytes 5872025600 | tf_op jit(solution)/shard_map/self_grads/pallas_call | solution.py:833
  392.4 12.3 %self_back.1 = (f32[512,1024]{1,0:T(8,128)}, f32[8,1024]{1,0:T(8,128)}) custom-call(bf16[512,1024]{1,0:T(8,128)(2,1)} %copy-done.23, bf16[512,1024]{1,0:T(8,128)(2,1)} %copy-done.24, bf16[512,1024]{1,0:T(8,128)(2,1)} %copy-done.25, bf16[512,1024]{1,0:T(8,128)(2,1)} %bitcast.155, f32[512,1024]{1,0:T(8,128)} %get-tuple-element.323.dmid_ref, ...), custom_call_target="tpu_custom_call" | custom-call | flops 1288490188800 | bytes 6920601600 | tf_op jit(solution)/shard_map/self_back/pallas_call | solution.py:761
  425.6 10.2 %memory_back.1 = (f32[1024,1024]{1,0:T(8,128)}, f32[8,1024]{1,0:T(8,128)}) custom-call(bf16[1024,1024]{1,0:T(8,128)(2,1)} %copy-done.17, bf16[1024,1024]{1,0:T(8,128)(2,1)} %copy-done.18, bf16[4,128,1024]{2,1,0:T(8,128)(2,1)} %all-to-all-done.1.rest_0_, bf16[4,128,1024]{2,1,0:T(8,128)(2,1)} %collective-permute-done.10.rest_1_, ...), custom_call_target="tpu_custom_call" | custom-call | flops 1717986918400 | bytes 6710886400 | tf_op jit(solution)/shard_map/memory_back/pallas_call | solution.py:668
  491.5 9.9 %all-to-all-done.5 = bf16[4,128,1024]{2,1,0:T(8,128)(2,1)S(1)} async-done(((bf16[4,128,1024]{2,1,0:T(8,128)(2,1)}), bf16[4,128,1024]{2,1,0:T(8,128)(2,1)S(1)}, u32[]{:S(2)}, u32[]{:S(2)}) %all-to-all-start.5) | async-done | bytes 1048608 | tf_op jit(solution)/shard_map/all_to_all | solution.py:177
  509.1 8.0 %all_to_all.46 = bf16[4,17,128]{2,1,0:T(8,128)(2,1)S(1)} all-to-all(bf16[4,17,128]{2,1,0:T(8,128)(2,1)S(1)} %copy.64), channel_id=1, replica_groups={{0,2,4,6},{1,3,5,7},{8,10,12,14},{9,11,13,15},{16,18,20,22},{17,19,21,2..., dimensions={0} | all-to-all | bytes 34816 | tf_op jit(solution)/shard_map/all_to_all | solution.py:177
  (294 shorter events, 206.7 us)
Async XLA Ops:
  64.3 28.9 %collective-permute-start.6 = (bf16[2,4,136,512]{3,2,1,0:T(8,128)(2,1)}, bf16[2,4,136,512]{3,2,1,0:T(8,128)(2,1)}, u32[]{:S(2)}, u32[]{:S(2)}) collective-permute-start(bf16[2,4,136,512]{3,2,1,0:T(8,128)(2,1)} %pad_maximum_fusion.1.rest_2_.rest_10_), channel_id=1, source_target_pairs={{0,8},{8,0},{16,24},{24,16},{1,9},{9,1},{17,25},{25,17},{2,10},{10... | collective-permute-start | bytes 3342344 | tf_op jit(solution)/shard_map/ppermute | solution.py:31
  64.3 28.9 %collective-permute-start.4 = (bf16[2,4,136,512]{3,2,1,0:T(8,128)(2,1)}, bf16[2,4,136,512]{3,2,1,0:T(8,128)(2,1)}, u32[]{:S(2)}, u32[]{:S(2)}) collective-permute-start(bf16[2,4,136,512]{3,2,1,0:T(8,128)(2,1)} %pad_maximum_fusion.rest_0_.rest_8_), channel_id=1, source_target_pairs={{0,8},{8,0},{16,24},{24,16},{1,9},{9,1},{17,25},{25,17},{2,10},{10... | collective-permute-start | bytes 3342344 | tf_op jit(solution)/shard_map/ppermute | solution.py:31
  86.4 51.2 %all-to-all-start.2 = ((bf16[4,128,1024]{2,1,0:T(8,128)(2,1)}), bf16[4,128,1024]{2,1,0:T(8,128)(2,1)}, u32[]{:S(2)}, u32[]{:S(2)}) async-start(bf16[4,128,1024]{2,1,0:T(8,128)(2,1)} %broadcast_in_dim.32), calls=%async_computation.2 | async-start | bytes 2097152 | tf_op jit(solution)/shard_map/all_to_all | solution.py:66
  90.7 47.0 %collective-permute-start.10 = (bf16[4,128,1024]{2,1,0:T(8,128)(2,1)}, bf16[4,128,1024]{2,1,0:T(8,128)(2,1)}, u32[]{:S(2)}, u32[]{:S(2)}) collective-permute-start(bf16[4,128,1024]{2,1,0:T(8,128)(2,1)} %all-to-all-done.1.rest_0_), channel_id=1, source_target_pairs={{0,1},{1,0},{2,3},{3,2},{4,5},{5,4},{6,7},{7,6},{8,9},{9,8},{10,11... | collective-permute-start | bytes 3145736 | tf_op jit(solution)/shard_map/ppermute | solution.py:37
  145.2 34.5 %collective-permute-start.15 = (bf16[4,128,1024]{2,1,0:T(8,128)(2,1)}, bf16[4,128,1024]{2,1,0:T(8,128)(2,1)}, u32[]{:S(2)}, u32[]{:S(2)}) collective-permute-start(bf16[4,128,1024]{2,1,0:T(8,128)(2,1)} %all-to-all-done.2.rest_0_), channel_id=1, source_target_pairs={{0,16},{8,24},{16,0},{24,8},{1,17},{9,25},{17,1},{25,9},{2,18},{10... | collective-permute-start | bytes 3145736 | tf_op jit(solution)/shard_map/ppermute | solution.py:34
  146.9 31.3 %all-to-all-start.3 = ((bf16[4,128,1024]{2,1,0:T(8,128)(2,1)}), bf16[4,128,1024]{2,1,0:T(8,128)(2,1)}, u32[]{:S(2)}, u32[]{:S(2)}) async-start(bf16[4,128,1024]{2,1,0:T(8,128)(2,1)} %broadcast_in_dim.33), calls=%async_computation.3 | async-start | bytes 2097152 | tf_op jit(solution)/shard_map/all_to_all | solution.py:66
  152.1 33.1 %collective-permute-start.17 = (bf16[4,128,1024]{2,1,0:T(8,128)(2,1)}, bf16[4,128,1024]{2,1,0:T(8,128)(2,1)}, u32[]{:S(2)}, u32[]{:S(2)}) collective-permute-start(bf16[4,128,1024]{2,1,0:T(8,128)(2,1)} %all-to-all-done.2.rest_0_), channel_id=1, source_target_pairs={{0,1},{1,0},{2,3},{3,2},{4,5},{5,4},{6,7},{7,6},{8,9},{9,8},{10,11... | collective-permute-start | bytes 3145736 | tf_op jit(solution)/shard_map/ppermute | solution.py:37
  178.2 28.5 %collective-permute-start.18 = (bf16[4,128,1024]{2,1,0:T(8,128)(2,1)}, bf16[4,128,1024]{2,1,0:T(8,128)(2,1)}, u32[]{:S(2)}, u32[]{:S(2)}) collective-permute-start(bf16[4,128,1024]{2,1,0:T(8,128)(2,1)} %all-to-all-done.3.rest_2_), channel_id=1, source_target_pairs={{0,16},{8,24},{16,0},{24,8},{1,17},{9,25},{17,1},{25,9},{2,18},{10... | collective-permute-start | bytes 3145736 | tf_op jit(solution)/shard_map/ppermute | solution.py:34
  185.2 40.0 %collective-permute-start.21 = (bf16[4,128,1024]{2,1,0:T(8,128)(2,1)}, bf16[4,128,1024]{2,1,0:T(8,128)(2,1)}, u32[]{:S(2)}, u32[]{:S(2)}) collective-permute-start(bf16[4,128,1024]{2,1,0:T(8,128)(2,1)} %all-to-all-done.3.rest_2_), channel_id=1, source_target_pairs={{0,1},{1,0},{2,3},{3,2},{4,5},{5,4},{6,7},{7,6},{8,9},{9,8},{10,11... | collective-permute-start | bytes 3145736 | tf_op jit(solution)/shard_map/ppermute | solution.py:37
  185.7 39.4 %collective-permute-start.20 = (bf16[4,128,1024]{2,1,0:T(8,128)(2,1)}, bf16[4,128,1024]{2,1,0:T(8,128)(2,1)}, u32[]{:S(2)}, u32[]{:S(2)}) collective-permute-start(bf16[4,128,1024]{2,1,0:T(8,128)(2,1)} %collective-permute-done.17.rest_1_), channel_id=1, source_target_pairs={{0,16},{8,24},{16,0},{24,8},{1,17},{9,25},{17,1},{25,9},{2,18},{10... | collective-permute-start | bytes 3145736 | tf_op jit(solution)/shard_map/ppermute | solution.py:34
  252.1 28.6 %collective-permute-start.29 = (bf16[2,2,2,4,128,512]{5,4,3,2,1,0:T(8,128)(2,1)}, bf16[2,2,2,4,128,512]{5,4,3,2,1,0:T(8,128)(2,1)}, u32[]{:S(2)}, u32[]{:S(2)}) collective-permute-start(bf16[2,2,2,4,128,512]{5,4,3,2,1,0:T(8,128)(2,1)} %get-tuple-element.285), channel_id=1, source_target_pairs={{0,8},{8,0},{16,24},{24,16},{1,9},{9,1},{17,25},{25,17},{2,10},{10... | collective-permute-start | bytes 12582920 | tf_op jit(solution)/shard_map/ppermute | solution.py:31
  280.5 33.6 %collective-permute-start.31 = (bf16[2,2,2,4,128,512]{5,4,3,2,1,0:T(8,128)(2,1)}, bf16[2,2,2,4,128,512]{5,4,3,2,1,0:T(8,128)(2,1)}, u32[]{:S(2)}, u32[]{:S(2)}) collective-permute-start(bf16[2,2,2,4,128,512]{5,4,3,2,1,0:T(8,128)(2,1)} %get-tuple-element.297), channel_id=1, source_target_pairs={{0,8},{8,0},{16,24},{24,16},{1,9},{9,1},{17,25},{25,17},{2,10},{10... | collective-permute-start | bytes 12582920 | tf_op jit(solution)/shard_map/ppermute | solution.py:31
  284.1 35.4 %collective-permute-start.32 = (bf16[2,4,128,512]{3,2,1,0:T(8,128)(2,1)}, bf16[2,4,128,512]{3,2,1,0:T(8,128)(2,1)}, u32[]{:S(2)}, u32[]{:S(2)}) collective-permute-start(bf16[2,4,128,512]{3,2,1,0:T(8,128)(2,1)} %get-tuple-element.295), channel_id=1, source_target_pairs={{0,1},{1,0},{2,3},{3,2},{4,5},{5,4},{6,7},{7,6},{8,9},{9,8},{10,11... | collective-permute-start | bytes 3145736 | tf_op jit(solution)/shard_map/ppermute | solution.py:37
  284.6 34.8 %collective-permute-start.30 = (bf16[2,4,128,512]{3,2,1,0:T(8,128)(2,1)}, bf16[2,4,128,512]{3,2,1,0:T(8,128)(2,1)}, u32[]{:S(2)}, u32[]{:S(2)}) collective-permute-start(bf16[2,4,128,512]{3,2,1,0:T(8,128)(2,1)} %get-tuple-element.293), channel_id=1, source_target_pairs={{0,16},{8,24},{16,0},{24,8},{1,17},{9,25},{17,1},{25,9},{2,18},{10... | collective-permute-start | bytes 3145736 | tf_op jit(solution)/shard_map/ppermute | solution.py:34
  317.4 33.8 %collective-permute-start.35 = (bf16[2,4,128,512]{3,2,1,0:T(8,128)(2,1)}, bf16[2,4,128,512]{3,2,1,0:T(8,128)(2,1)}, u32[]{:S(2)}, u32[]{:S(2)}) collective-permute-start(bf16[2,4,128,512]{3,2,1,0:T(8,128)(2,1)} %get-tuple-element.307), channel_id=1, source_target_pairs={{0,1},{1,0},{2,3},{3,2},{4,5},{5,4},{6,7},{7,6},{8,9},{9,8},{10,11... | collective-permute-start | bytes 3145736 | tf_op jit(solution)/shard_map/ppermute | solution.py:37
  318.9 32.9 %collective-permute-start.34 = (bf16[2,4,128,512]{3,2,1,0:T(8,128)(2,1)}, bf16[2,4,128,512]{3,2,1,0:T(8,128)(2,1)}, u32[]{:S(2)}, u32[]{:S(2)}) collective-permute-start(bf16[2,4,128,512]{3,2,1,0:T(8,128)(2,1)} %get-tuple-element.305), channel_id=1, source_target_pairs={{0,16},{8,24},{16,0},{24,8},{1,17},{9,25},{17,1},{25,9},{2,18},{10... | collective-permute-start | bytes 3145736 | tf_op jit(solution)/shard_map/ppermute | solution.py:34
  334.4 36.9 %collective-permute-start.37 = (bf16[4,128,512]{2,1,0:T(8,128)(2,1)}, bf16[4,128,512]{2,1,0:T(8,128)(2,1)}, u32[]{:S(2)}, u32[]{:S(2)}) collective-permute-start(bf16[4,128,512]{2,1,0:T(8,128)(2,1)} %get-tuple-element.317), channel_id=1, source_target_pairs={{0,16},{8,24},{16,0},{24,8},{1,17},{9,25},{17,1},{25,9},{2,18},{10... | collective-permute-start | bytes 1572872 | tf_op jit(solution)/shard_map/ppermute | solution.py:34
  336.0 35.4 %collective-permute-start.36 = (bf16[4,128,512]{2,1,0:T(8,128)(2,1)}, bf16[4,128,512]{2,1,0:T(8,128)(2,1)}, u32[]{:S(2)}, u32[]{:S(2)}) collective-permute-start(bf16[4,128,512]{2,1,0:T(8,128)(2,1)} %get-tuple-element.315), channel_id=1, source_target_pairs={{0,1},{1,0},{2,3},{3,2},{4,5},{5,4},{6,7},{7,6},{8,9},{9,8},{10,11... | collective-permute-start | bytes 1572872 | tf_op jit(solution)/shard_map/ppermute | solution.py:37
  349.7 42.7 %collective-permute-start.39 = (bf16[2,4,128,512]{3,2,1,0:T(8,128)(2,1)}, bf16[2,4,128,512]{3,2,1,0:T(8,128)(2,1)}, u32[]{:S(2)}, u32[]{:S(2)}) collective-permute-start(bf16[2,4,128,512]{3,2,1,0:T(8,128)(2,1)} %get-tuple-element.328), channel_id=1, source_target_pairs={{0,1},{1,0},{2,3},{3,2},{4,5},{5,4},{6,7},{7,6},{8,9},{9,8},{10,11... | collective-permute-start | bytes 3145736 | tf_op jit(solution)/shard_map/ppermute | solution.py:37
  351.2 41.2 %collective-permute-start.38 = (bf16[2,4,128,512]{3,2,1,0:T(8,128)(2,1)}, bf16[2,4,128,512]{3,2,1,0:T(8,128)(2,1)}, u32[]{:S(2)}, u32[]{:S(2)}) collective-permute-start(bf16[2,4,128,512]{3,2,1,0:T(8,128)(2,1)} %get-tuple-element.326), channel_id=1, source_target_pairs={{0,16},{8,24},{16,0},{24,8},{1,17},{9,25},{17,1},{25,9},{2,18},{10... | collective-permute-start | bytes 3145736 | tf_op jit(solution)/shard_map/ppermute | solution.py:34
  374.6 38.2 %all-to-all-start.4 = ((bf16[4,128,1024]{2,1,0:T(8,128)(2,1)}), bf16[4,128,1024]{2,1,0:T(8,128)(2,1)}, u32[]{:S(2)}, u32[]{:S(2)}) async-start(bf16[4,128,1024]{2,1,0:T(8,128)(2,1)} %sums.17), calls=%async_computation.4 | async-start | bytes 2097152 | tf_op jit(solution)/shard_map/all_to_all | solution.py:177
  412.7 31.2 %all-to-all-start.6 = ((bf16[4,128,1024]{2,1,0:T(8,128)(2,1)}), bf16[4,128,1024]{2,1,0:T(8,128)(2,1)}, u32[]{:S(2)}, u32[]{:S(2)}) async-start(bf16[4,128,1024]{2,1,0:T(8,128)(2,1)} %sums.20), calls=%async_computation.6 | async-start | bytes 2097152 | tf_op jit(solution)/shard_map/all_to_all | solution.py:177
  443.9 28.7 %all-to-all-start.7 = ((bf16[4,128,1024]{2,1,0:T(8,128)(2,1)}), bf16[4,128,1024]{2,1,0:T(8,128)(2,1)S(1)}, u32[]{:S(2)}, u32[]{:S(2)}) async-start(bf16[4,128,1024]{2,1,0:T(8,128)(2,1)} %sums.23), calls=%async_computation.7 | async-start | bytes 2097152 | tf_op jit(solution)/shard_map/all_to_all | solution.py:177
  472.7 28.7 %all-to-all-start.5 = ((bf16[4,128,1024]{2,1,0:T(8,128)(2,1)}), bf16[4,128,1024]{2,1,0:T(8,128)(2,1)S(1)}, u32[]{:S(2)}, u32[]{:S(2)}) async-start(bf16[4,128,1024]{2,1,0:T(8,128)(2,1)} %sums.22), calls=%async_computation.5 | async-start | bytes 2097152 | tf_op jit(solution)/shard_map/all_to_all | solution.py:177
  (90 other events, 989.4 us)

commit v5 on v4

--- a/solution.py
+++ b/solution.py
@@ -282,7 +282,7 @@
         o_ref[:, lanes] = jnp.where(masks[0], both[0], both[1]).astype(BF)
 
 
-def attend(q, k, v, prefix, batch, masked, group=4):
+def attend(q, k, v, prefix, batch, masked, group=8):
     rows, keys, d = q.shape[0] // batch, k.shape[0] // batch, q.shape[1]
     wide = group * d // H
     spec = lambda n: pl.BlockSpec((n, wide), lambda b, g, *_: (b, g))
@@ -334,7 +334,7 @@
         dv_ref[:, lanes] = jnp.concatenate(dv_t, 0).astype(BF).T
 
 
-def attend_back(do, q, k, v, p, batch, group=4):
+def attend_back(do, q, k, v, p, batch, group=8):
     rows, keys, d = q.shape[0] // batch, k.shape[0] // batch, q.shape[1]
     wide = group * d // H
     spec = lambda n: pl.BlockSpec((n, wide), lambda b, g: (b, g))

time: 531 us -> 529 us (level)
  Pallas kernels: 250 us -> 244 us
  transfers between devices with their start and end apart: 67 -> 67, of which waited for: 19 -> 20; matrix products, arithmetic and copies ran while one was open for 5% -> 5% of each run, Pallas kernels for 47% -> 46%
where the time goes in v5:
time: 529 us; the launch traced here: 519 us
  Pallas kernels  244 us (46%)
  waiting for transfers between devices  103 us (19%)
  starting transfers between devices  75.4 us (14%)
  local copies, waits for them, and re-layouts  43.5 us (8%)
  blocking collectives  41.2 us (8%)
  other arithmetic  9.58 us (2%)
    ppermute x19, waiting for transfers between devices, across(): return lax.ppermute(v, 'replica', [(i, i ^ 2) for i in range(self.groups)])  49.6 us
    pallas_call x2, Pallas kernels, ffn(): pl.pallas_call(partial(ffn_kernel, last, first_row), in_specs=[WHOLE] * (...  47.6 us
    pallas_call x12, Pallas kernels, sums(): pl.pallas_call(partial(sums_kernel, tuple((len(g[3]) for g in groups)), j...  37.6 us
    all_to_all x1, blocking collectives, ring_gather(): lax.all_to_all(copies, 'fsdp', 0, 0, axis_index_groups=place.ring_members())  33.2 us
    pallas_call x2, Pallas kernels, attend_back(): pl.pallas_call(partial(attend_back_kernel, (d // H) ** (-0.5)), grid=(bat...  28.3 us
    unnamed x98, local copies, waits for them, and re-layouts  27 us
    pallas_call x2, Pallas kernels, attend(): pl.pallas_call(partial(attend_kernel, masked, (d // H) ** (-0.5)), grid_s...  24.1 us
    ppermute x19, starting transfers between devices, across(): return lax.ppermute(v, 'replica', [(i, i ^ 2) for i in range(self.groups)])  21.9 us
  transfers between devices with their start and end apart: 67, of which 20 were waited for; matrix products, arithmetic and copies ran while one was open for 5% of the time, Pallas kernels for 46%

profile of v5, /device:TPU:0, one launch (start us, length us, event | category | flops | bytes accessed | tf_op | source)
XLA Modules:
  0.0 519.1 jit_solution(12703879666876995404)
XLA Ops:
  3.8 33.2 %all_to_all.45 = bf16[4,2,136,512]{3,2,1,0:T(8,128)(2,1)S(1)} all-to-all(bf16[4,2,136,512]{3,2,1,0:T(8,128)(2,1)S(1)} %broadcast_in_dim.12), channel_id=1, replica_groups={{0,2,4,6},{1,3,5,7},{8,10,12,14},{9,11,13,15},{16,18,20,22},{17,19,21,2..., dimensions={0} | all-to-all | bytes 2228224 | tf_op jit(solution)/shard_map/all_to_all | solution.py:66
  40.3 10.5 %collective-permute-done.1 = bf16[4,136,512]{2,1,0:T(8,128)(2,1)S(1)} collective-permute-done((bf16[4,136,512]{2,1,0:T(8,128)(2,1)S(1)}, bf16[4,136,512]{2,1,0:T(8,128)(2,1)S(1)}, u32[]{:S(2)}, u32[]{:S(2)}) %collective-permute-start.1) | collective-permute-done | bytes 557088 | tf_op jit(solution)/shard_map/ppermute | solution.py:34
  64.9 11.9 %collective-permute-done.3.rest_3_.rest_11_ = bf16[2,4,136,512]{3,2,1,0:T(8,128)(2,1)} collective-permute-done((bf16[2,4,136,512]{3,2,1,0:T(8,128)(2,1)}, bf16[2,4,136,512]{3,2,1,0:T(8,128)(2,1)}, u32[]{:S(2)}, u32[]{:S(2)}) %collective-permute-start.3) | collective-permute-done | bytes 1114144 | tf_op jit(solution)/shard_map/ppermute | solution.py:37
  93.9 7.6 %first.1 = (bf16[512,1024]{1,0:T(8,128)(2,1)}, bf16[512,1024]{1,0:T(8,128)(2,1)}, bf16[512,1024]{1,0:T(8,128)(2,1)}, bf16[512,1024]{1,0:T(8,128)(2,1)}) custom-call(bf16[512,1024]{1,0:T(8,128)(2,1)} %bitcast.153, f32[17,1024]{1,0:T(8,128)} %bitcast.139, bf16[2,4,136,512]{3,2,1,0:T(8,128)(2,1)} %pad_maximum_fusion.rest_0_.rest_8_, ...), custom_call_target="tpu_custom_call" | custom-call | flops 1288490188800 | bytes 5662310400 | tf_op jit(solution)/shard_map/first/pallas_call | solution.py:528
  101.5 17.7 %collective-permute-done.8.rest_2_ = bf16[4,128,1024]{2,1,0:T(8,128)(2,1)} collective-permute-done((bf16[4,128,1024]{2,1,0:T(8,128)(2,1)}, bf16[4,128,1024]{2,1,0:T(8,128)(2,1)}, u32[]{:S(2)}, u32[]{:S(2)}) %collective-permute-start.8) | collective-permute-done | bytes 1048608 | tf_op jit(solution)/shard_map/ppermute | solution.py:34
  124.3 7.2 %attend.2 = (bf16[512,1024]{1,0:T(8,128)(2,1)S(1)}, bf16[2,16,256,256]{3,2,1,0:T(8,128)(2,1)S(1)}) custom-call(s32[2]{0:T(128)S(1)} %copy-done, bf16[512,1024]{1,0:T(8,128)(2,1)S(1)} %copy-done.11, bf16[512,1024]{1,0:T(8,128)(2,1)S(1)} %copy-done.13, bf16[512,1024]{1,0:T(8,128)(2,1)S(1)} %copy-done.15), custom_call_target="tpu_custom_call" | custom-call | flops 858993459200 | bytes 3355443200 | tf_op jit(solution)/shard_map/attend/pallas_call | solution.py:289
  135.1 6.9 %self_out.1 = (f32[512,1024]{1,0:T(8,128)}, bf16[512,1024]{1,0:T(8,128)(2,1)}) custom-call(bf16[512,1024]{1,0:T(8,128)(2,1)} %copy-done.3, bf16[512,1024]{1,0:T(8,128)(2,1)} %bitcast.154, f32[17,1024]{1,0:T(8,128)} %bitcast.140, bf16[2,4,136,512]{3,2,1,0:T(8,128)(2,1)} %pad_maximum_fusion.rest_0_.rest_8_, ...), custom_call_target="tpu_custom_call" | custom-call | flops 429496729600 | bytes 4299161600 | tf_op jit(solution)/shard_map/self_out/pallas_call | solution.py:575
  153.6 9.2 %memory.1 = (bf16[1024,1024]{1,0:T(8,128)(2,1)}, bf16[1024,1024]{1,0:T(8,128)(2,1)}) custom-call(bf16[1024,1024]{1,0:T(8,128)(2,1)} %bitcast.149, f32[17,1024]{1,0:T(8,128)} %bitcast.141, bf16[4,128,1024]{2,1,0:T(8,128)(2,1)} %all-to-all-done.1.rest_0_, bf16[4,128,1024]{2,1,0:T(8,128)(2,1)} %collective-permute-done.10.rest_1_, ...), custom_call_target="tpu_custom_call" | custom-call | flops 1717986918400 | bytes 5872025600 | tf_op jit(solution)/shard_map/memory/pallas_call | solution.py:634
  162.9 14.3 %all-to-all-done.3.rest_2_ = bf16[4,128,1024]{2,1,0:T(8,128)(2,1)} async-done(((bf16[4,128,1024]{2,1,0:T(8,128)(2,1)}), bf16[4,128,1024]{2,1,0:T(8,128)(2,1)}, u32[]{:S(2)}, u32[]{:S(2)}) %all-to-all-start.3) | async-done | bytes 1048608 | tf_op jit(solution)/shard_map/all_to_all | solution.py:66
  187.5 17.0 %attend.3 = (bf16[512,1024]{1,0:T(8,128)(2,1)S(1)}, bf16[2,16,256,512]{3,2,1,0:T(8,128)(2,1)}) custom-call(s32[2]{0:T(128)S(1)} %copy-done.1, bf16[512,1024]{1,0:T(8,128)(2,1)S(1)} %copy-done.4, bf16[1024,1024]{1,0:T(8,128)(2,1)S(1)} %copy-done.19, bf16[1024,1024]{1,0:T(8,128)(2,1)S(1)} %copy-done.21), custom_call_target="tpu_custom_call" | custom-call | flops 1717986918400 | bytes 5872025600 | tf_op jit(solution)/shard_map/attend/pallas_call | solution.py:289
  206.0 7.1 %cross_out.1 = (f32[512,1024]{1,0:T(8,128)}, bf16[512,1024]{1,0:T(8,128)(2,1)}) custom-call(bf16[512,1024]{1,0:T(8,128)(2,1)} %copy-done.2, f32[512,1024]{1,0:T(8,128)} %get-tuple-element.246.res_ref.mid_ref, f32[17,1024]{1,0:T(8,128)} %bitcast.143, bf16[4,128,1024]{2,1,0:T(8,128)(2,1)} %all-to-all-done.1.rest_0_, ...), custom_call_target="tpu_custom_call" | custom-call | flops 429496729600 | bytes 4194304000 | tf_op jit(solution)/shard_map/cross_out/pallas_call | solution.py:575
  213.1 11.1 %collective-permute-done.20.rest_3_ = bf16[4,128,1024]{2,1,0:T(8,128)(2,1)} collective-permute-done((bf16[4,128,1024]{2,1,0:T(8,128)(2,1)}, bf16[4,128,1024]{2,1,0:T(8,128)(2,1)}, u32[]{:S(2)}, u32[]{:S(2)}) %collective-permute-start.20) | collective-permute-done | bytes 1048608 | tf_op jit(solution)/shard_map/ppermute | solution.py:34
  228.0 22.7 %ffn.2 = (f32[512,1024]{1,0:T(8,128)}, f32[512,1024]{1,0:T(8,128)}, f32[8,1024]{1,0:T(8,128)}, bf16[2,2,2,4,128,512]{5,4,3,2,1,0:T(8,128)(2,1)}, bf16[2,2,2,4,128,512]{5,4,3,2,1,0:T(8,128)(2,1)}) custom-call(bf16[512,1024]{1,0:T(8,128)(2,1)} %get-tuple-element.286.act_ref, bf16[512,1024]{1,0:T(8,128)(2,1)} %bitcast.151, ...), custom_call_target="tpu_custom_call" | custom-call | flops 5153960755200 | bytes 8388608000 | tf_op jit(solution)/shard_map/ffn/pallas_call | solution.py:968
  254.6 24.9 %ffn.3 = (bf16[512,1024]{1,0:T(8,128)(2,1)}, f32[512,1024]{1,0:T(8,128)}, bf16[512,1024]{1,0:T(8,128)(2,1)}, f32[8,1024]{1,0:T(8,128)}, f32[8,1024]{1,0:T(8,128)...) custom-call(bf16[512,1024]{1,0:T(8,128)(2,1)} %get-tuple-element.286.act_ref, ...), custom_call_target="tpu_custom_call" | custom-call | flops 5153960755200 | bytes 8388608000 | tf_op jit(solution)/shard_map/ffn/pallas_call | solution.py:968
  286.1 5.7 %output_back.1.do_ref = bf16[512,1024]{1,0:T(8,128)(2,1)} custom-call(bf16[512,1024]{1,0:T(8,128)(2,1)} %get-tuple-element.298.d_ref.rest_6_, bf16[4,128,1024]{2,1,0:T(8,128)(2,1)} %all-to-all-done.1.rest_0_, bf16[4,128,1024]{2,1,0:T(8,128)(2,1)} %collective-permute-done.10.rest_1_, bf16[4,128,1024]{2,1,0:T(8,128)(2,1)} %collective-permute-done.8.rest_2_, ...), custom_call_target="tpu_custom_call" | custom-call | flops 429496729600 | bytes 1677721600 | tf_op jit(solution)/shard_map/output_back/pallas_call | solution.py:786
  293.1 16.4 %attend_back.2 = (bf16[512,1024]{1,0:T(8,128)(2,1)S(1)}, bf16[1024,1024]{1,0:T(8,128)(2,1)S(1)}, bf16[1024,1024]{1,0:T(8,128)(2,1)S(1)}) custom-call(bf16[512,1024]{1,0:T(8,128)(2,1)S(1)} %copy-done.6, bf16[512,1024]{1,0:T(8,128)(2,1)S(1)} %copy-done.5, bf16[1024,1024]{1,0:T(8,128)(2,1)S(1)} %copy-done.20, bf16[1024,1024]{1,0:T(8,128)(2,1)S(1)} %copy-done.22, ...), custom_call_target="tpu_custom_call" | custom-call | flops 3435973836800 | bytes 7969177600 | tf_op jit(solution)/shard_map/attend_back/pallas_call | solution.py:341
  317.7 12.1 %cross_grads.1 = (bf16[2,2,2,4,128,512]{5,4,3,2,1,0:T(8,128)(2,1)}, bf16[2,2,2,4,128,512]{5,4,3,2,1,0:T(8,128)(2,1)}) custom-call(bf16[512,1024]{1,0:T(8,128)(2,1)} %get-tuple-element.308.a_ref.rest_0_, bf16[1024,1024]{1,0:T(8,128)(2,1)} %bitcast.150, bf16[512,1024]{1,0:T(8,128)(2,1)} %copy-done.2, bf16[512,1024]{1,0:T(8,128)(2,1)} %copy-done.9, ...), custom_call_target="tpu_custom_call" | custom-call | flops 2576980377600 | bytes 9227468800 | tf_op jit(solution)/shard_map/cross_grads/pallas_call | solution.py:833
  335.5 9.7 %cross_back.1 = (f32[512,1024]{1,0:T(8,128)}, bf16[512,1024]{1,0:T(8,128)(2,1)}, bf16[512,1024]{1,0:T(8,128)(2,1)}, f32[8,1024]{1,0:T(8,128)}) custom-call(bf16[512,1024]{1,0:T(8,128)(2,1)} %copy-done.9, f32[512,1024]{1,0:T(8,128)} %get-tuple-element.246.res_ref.mid_ref, f32[512,1024]{1,0:T(8,128)} %get-tuple-element.320.dmid_ref, f32[17,1024]{1,0:T(8,128)} %bitcast.146, ...), custom_call_target="tpu_custom_call" | custom-call | flops 858993459200 | bytes 5452595200 | tf_op jit(solution)/shard_map/cross_back/pallas_call | solution.py:724
  353.2 11.9 %attend_back.3 = (bf16[512,1024]{1,0:T(8,128)(2,1)S(1)}, bf16[512,1024]{1,0:T(8,128)(2,1)S(1)}, bf16[512,1024]{1,0:T(8,128)(2,1)S(1)}) custom-call(bf16[512,1024]{1,0:T(8,128)(2,1)S(1)} %copy-done.10, bf16[512,1024]{1,0:T(8,128)(2,1)S(1)} %copy-done.12, bf16[512,1024]{1,0:T(8,128)(2,1)S(1)} %copy-done.14, bf16[512,1024]{1,0:T(8,128)(2,1)S(1)} %copy-done.16, ...), custom_call_target="tpu_custom_call" | custom-call | flops 1717986918400 | bytes 4613734400 | tf_op jit(solution)/shard_map/attend_back/pallas_call | solution.py:341
  381.5 8.7 %self_grads.1 = (bf16[2,2,2,4,128,512]{5,4,3,2,1,0:T(8,128)(2,1)}, bf16[2,2,2,4,128,512]{5,4,3,2,1,0:T(8,128)(2,1)}) custom-call(bf16[512,1024]{1,0:T(8,128)(2,1)} %get-tuple-element.341.rest_0_, bf16[512,1024]{1,0:T(8,128)(2,1)} %copy-done.3, bf16[512,1024]{1,0:T(8,128)(2,1)} %copy-done.23, bf16[512,1024]{1,0:T(8,128)(2,1)} %copy-done.24, ...), custom_call_target="tpu_custom_call" | custom-call | flops 1717986918400 | bytes 5872025600 | tf_op jit(solution)/shard_map/self_grads/pallas_call | solution.py:833
  390.3 12.3 %self_back.1 = (f32[512,1024]{1,0:T(8,128)}, f32[8,1024]{1,0:T(8,128)}) custom-call(bf16[512,1024]{1,0:T(8,128)(2,1)} %copy-done.23, bf16[512,1024]{1,0:T(8,128)(2,1)} %copy-done.24, bf16[512,1024]{1,0:T(8,128)(2,1)} %copy-done.25, bf16[512,1024]{1,0:T(8,128)(2,1)} %bitcast.155, f32[512,1024]{1,0:T(8,128)} %get-tuple-element.323.dmid_ref, ...), custom_call_target="tpu_custom_call" | custom-call | flops 1288490188800 | bytes 6920601600 | tf_op jit(solution)/shard_map/self_back/pallas_call | solution.py:761
  423.5 10.2 %memory_back.1 = (f32[1024,1024]{1,0:T(8,128)}, f32[8,1024]{1,0:T(8,128)}) custom-call(bf16[1024,1024]{1,0:T(8,128)(2,1)} %copy-done.17, bf16[1024,1024]{1,0:T(8,128)(2,1)} %copy-done.18, bf16[4,128,1024]{2,1,0:T(8,128)(2,1)} %all-to-all-done.1.rest_0_, bf16[4,128,1024]{2,1,0:T(8,128)(2,1)} %collective-permute-done.10.rest_1_, ...), custom_call_target="tpu_custom_call" | custom-call | flops 1717986918400 | bytes 6710886400 | tf_op jit(solution)/shard_map/memory_back/pallas_call | solution.py:668
  489.3 9.0 %all-to-all-done.5 = bf16[4,128,1024]{2,1,0:T(8,128)(2,1)S(1)} async-done(((bf16[4,128,1024]{2,1,0:T(8,128)(2,1)}), bf16[4,128,1024]{2,1,0:T(8,128)(2,1)S(1)}, u32[]{:S(2)}, u32[]{:S(2)}) %all-to-all-start.5) | async-done | bytes 1048608 | tf_op jit(solution)/shard_map/all_to_all | solution.py:177
  506.0 8.0 %all_to_all.46 = bf16[4,17,128]{2,1,0:T(8,128)(2,1)S(1)} all-to-all(bf16[4,17,128]{2,1,0:T(8,128)(2,1)S(1)} %copy.64), channel_id=1, replica_groups={{0,2,4,6},{1,3,5,7},{8,10,12,14},{9,11,13,15},{16,18,20,22},{17,19,21,2..., dimensions={0} | all-to-all | bytes 34816 | tf_op jit(solution)/shard_map/all_to_all | solution.py:177
  (294 shorter events, 211.9 us)
Async XLA Ops:
  64.3 28.9 %collective-permute-start.6 = (bf16[2,4,136,512]{3,2,1,0:T(8,128)(2,1)}, bf16[2,4,136,512]{3,2,1,0:T(8,128)(2,1)}, u32[]{:S(2)}, u32[]{:S(2)}) collective-permute-start(bf16[2,4,136,512]{3,2,1,0:T(8,128)(2,1)} %pad_maximum_fusion.1.rest_2_.rest_10_), channel_id=1, source_target_pairs={{0,8},{8,0},{16,24},{24,16},{1,9},{9,1},{17,25},{25,17},{2,10},{10... | collective-permute-start | bytes 3342344 | tf_op jit(solution)/shard_map/ppermute | solution.py:31
  64.3 28.9 %collective-permute-start.4 = (bf16[2,4,136,512]{3,2,1,0:T(8,128)(2,1)}, bf16[2,4,136,512]{3,2,1,0:T(8,128)(2,1)}, u32[]{:S(2)}, u32[]{:S(2)}) collective-permute-start(bf16[2,4,136,512]{3,2,1,0:T(8,128)(2,1)} %pad_maximum_fusion.rest_0_.rest_8_), channel_id=1, source_target_pairs={{0,8},{8,0},{16,24},{24,16},{1,9},{9,1},{17,25},{25,17},{2,10},{10... | collective-permute-start | bytes 3342344 | tf_op jit(solution)/shard_map/ppermute | solution.py:31
  86.4 48.1 %all-to-all-start.2 = ((bf16[4,128,1024]{2,1,0:T(8,128)(2,1)}), bf16[4,128,1024]{2,1,0:T(8,128)(2,1)}, u32[]{:S(2)}, u32[]{:S(2)}) async-start(bf16[4,128,1024]{2,1,0:T(8,128)(2,1)} %broadcast_in_dim.32), calls=%async_computation.2 | async-start | bytes 2097152 | tf_op jit(solution)/shard_map/all_to_all | solution.py:66
  90.7 43.9 %collective-permute-start.10 = (bf16[4,128,1024]{2,1,0:T(8,128)(2,1)}, bf16[4,128,1024]{2,1,0:T(8,128)(2,1)}, u32[]{:S(2)}, u32[]{:S(2)}) collective-permute-start(bf16[4,128,1024]{2,1,0:T(8,128)(2,1)} %all-to-all-done.1.rest_0_), channel_id=1, source_target_pairs={{0,1},{1,0},{2,3},{3,2},{4,5},{5,4},{6,7},{7,6},{8,9},{9,8},{10,11... | collective-permute-start | bytes 3145736 | tf_op jit(solution)/shard_map/ppermute | solution.py:37
  144.2 34.5 %collective-permute-start.15 = (bf16[4,128,1024]{2,1,0:T(8,128)(2,1)}, bf16[4,128,1024]{2,1,0:T(8,128)(2,1)}, u32[]{:S(2)}, u32[]{:S(2)}) collective-permute-start(bf16[4,128,1024]{2,1,0:T(8,128)(2,1)} %all-to-all-done.2.rest_0_), channel_id=1, source_target_pairs={{0,16},{8,24},{16,0},{24,8},{1,17},{9,25},{17,1},{25,9},{2,18},{10... | collective-permute-start | bytes 3145736 | tf_op jit(solution)/shard_map/ppermute | solution.py:34
  145.8 31.4 %all-to-all-start.3 = ((bf16[4,128,1024]{2,1,0:T(8,128)(2,1)}), bf16[4,128,1024]{2,1,0:T(8,128)(2,1)}, u32[]{:S(2)}, u32[]{:S(2)}) async-start(bf16[4,128,1024]{2,1,0:T(8,128)(2,1)} %broadcast_in_dim.33), calls=%async_computation.3 | async-start | bytes 2097152 | tf_op jit(solution)/shard_map/all_to_all | solution.py:66
  151.0 33.1 %collective-permute-start.17 = (bf16[4,128,1024]{2,1,0:T(8,128)(2,1)}, bf16[4,128,1024]{2,1,0:T(8,128)(2,1)}, u32[]{:S(2)}, u32[]{:S(2)}) collective-permute-start(bf16[4,128,1024]{2,1,0:T(8,128)(2,1)} %all-to-all-done.2.rest_0_), channel_id=1, source_target_pairs={{0,1},{1,0},{2,3},{3,2},{4,5},{5,4},{6,7},{7,6},{8,9},{9,8},{10,11... | collective-permute-start | bytes 3145736 | tf_op jit(solution)/shard_map/ppermute | solution.py:37
  177.2 28.8 %collective-permute-start.18 = (bf16[4,128,1024]{2,1,0:T(8,128)(2,1)}, bf16[4,128,1024]{2,1,0:T(8,128)(2,1)}, u32[]{:S(2)}, u32[]{:S(2)}) collective-permute-start(bf16[4,128,1024]{2,1,0:T(8,128)(2,1)} %all-to-all-done.3.rest_2_), channel_id=1, source_target_pairs={{0,16},{8,24},{16,0},{24,8},{1,17},{9,25},{17,1},{25,9},{2,18},{10... | collective-permute-start | bytes 3145736 | tf_op jit(solution)/shard_map/ppermute | solution.py:34
  184.1 40.0 %collective-permute-start.21 = (bf16[4,128,1024]{2,1,0:T(8,128)(2,1)}, bf16[4,128,1024]{2,1,0:T(8,128)(2,1)}, u32[]{:S(2)}, u32[]{:S(2)}) collective-permute-start(bf16[4,128,1024]{2,1,0:T(8,128)(2,1)} %all-to-all-done.3.rest_2_), channel_id=1, source_target_pairs={{0,1},{1,0},{2,3},{3,2},{4,5},{5,4},{6,7},{7,6},{8,9},{9,8},{10,11... | collective-permute-start | bytes 3145736 | tf_op jit(solution)/shard_map/ppermute | solution.py:37
  185.7 38.4 %collective-permute-start.20 = (bf16[4,128,1024]{2,1,0:T(8,128)(2,1)}, bf16[4,128,1024]{2,1,0:T(8,128)(2,1)}, u32[]{:S(2)}, u32[]{:S(2)}) collective-permute-start(bf16[4,128,1024]{2,1,0:T(8,128)(2,1)} %collective-permute-done.17.rest_1_), channel_id=1, source_target_pairs={{0,16},{8,24},{16,0},{24,8},{1,17},{9,25},{17,1},{25,9},{2,18},{10... | collective-permute-start | bytes 3145736 | tf_op jit(solution)/shard_map/ppermute | solution.py:34
  250.9 28.8 %collective-permute-start.29 = (bf16[2,2,2,4,128,512]{5,4,3,2,1,0:T(8,128)(2,1)}, bf16[2,2,2,4,128,512]{5,4,3,2,1,0:T(8,128)(2,1)}, u32[]{:S(2)}, u32[]{:S(2)}) collective-permute-start(bf16[2,2,2,4,128,512]{5,4,3,2,1,0:T(8,128)(2,1)} %get-tuple-element.285), channel_id=1, source_target_pairs={{0,8},{8,0},{16,24},{24,16},{1,9},{9,1},{17,25},{25,17},{2,10},{10... | collective-permute-start | bytes 12582920 | tf_op jit(solution)/shard_map/ppermute | solution.py:31
  279.5 33.6 %collective-permute-start.31 = (bf16[2,2,2,4,128,512]{5,4,3,2,1,0:T(8,128)(2,1)}, bf16[2,2,2,4,128,512]{5,4,3,2,1,0:T(8,128)(2,1)}, u32[]{:S(2)}, u32[]{:S(2)}) collective-permute-start(bf16[2,2,2,4,128,512]{5,4,3,2,1,0:T(8,128)(2,1)} %get-tuple-element.297), channel_id=1, source_target_pairs={{0,8},{8,0},{16,24},{24,16},{1,9},{9,1},{17,25},{25,17},{2,10},{10... | collective-permute-start | bytes 12582920 | tf_op jit(solution)/shard_map/ppermute | solution.py:31
  283.1 34.6 %collective-permute-start.32 = (bf16[2,4,128,512]{3,2,1,0:T(8,128)(2,1)}, bf16[2,4,128,512]{3,2,1,0:T(8,128)(2,1)}, u32[]{:S(2)}, u32[]{:S(2)}) collective-permute-start(bf16[2,4,128,512]{3,2,1,0:T(8,128)(2,1)} %get-tuple-element.295), channel_id=1, source_target_pairs={{0,1},{1,0},{2,3},{3,2},{4,5},{5,4},{6,7},{7,6},{8,9},{9,8},{10,11... | collective-permute-start | bytes 3145736 | tf_op jit(solution)/shard_map/ppermute | solution.py:37
  284.6 33.1 %collective-permute-start.30 = (bf16[2,4,128,512]{3,2,1,0:T(8,128)(2,1)}, bf16[2,4,128,512]{3,2,1,0:T(8,128)(2,1)}, u32[]{:S(2)}, u32[]{:S(2)}) collective-permute-start(bf16[2,4,128,512]{3,2,1,0:T(8,128)(2,1)} %get-tuple-element.293), channel_id=1, source_target_pairs={{0,16},{8,24},{16,0},{24,8},{1,17},{9,25},{17,1},{25,9},{2,18},{10... | collective-permute-start | bytes 3145736 | tf_op jit(solution)/shard_map/ppermute | solution.py:34
  316.6 32.7 %collective-permute-start.35 = (bf16[2,4,128,512]{3,2,1,0:T(8,128)(2,1)}, bf16[2,4,128,512]{3,2,1,0:T(8,128)(2,1)}, u32[]{:S(2)}, u32[]{:S(2)}) collective-permute-start(bf16[2,4,128,512]{3,2,1,0:T(8,128)(2,1)} %get-tuple-element.307), channel_id=1, source_target_pairs={{0,1},{1,0},{2,3},{3,2},{4,5},{5,4},{6,7},{7,6},{8,9},{9,8},{10,11... | collective-permute-start | bytes 3145736 | tf_op jit(solution)/shard_map/ppermute | solution.py:37
  317.1 32.6 %collective-permute-start.34 = (bf16[2,4,128,512]{3,2,1,0:T(8,128)(2,1)}, bf16[2,4,128,512]{3,2,1,0:T(8,128)(2,1)}, u32[]{:S(2)}, u32[]{:S(2)}) collective-permute-start(bf16[2,4,128,512]{3,2,1,0:T(8,128)(2,1)} %get-tuple-element.305), channel_id=1, source_target_pairs={{0,16},{8,24},{16,0},{24,8},{1,17},{9,25},{17,1},{25,9},{2,18},{10... | collective-permute-start | bytes 3145736 | tf_op jit(solution)/shard_map/ppermute | solution.py:34
  332.5 35.5 %collective-permute-start.37 = (bf16[4,128,512]{2,1,0:T(8,128)(2,1)}, bf16[4,128,512]{2,1,0:T(8,128)(2,1)}, u32[]{:S(2)}, u32[]{:S(2)}) collective-permute-start(bf16[4,128,512]{2,1,0:T(8,128)(2,1)} %get-tuple-element.317), channel_id=1, source_target_pairs={{0,16},{8,24},{16,0},{24,8},{1,17},{9,25},{17,1},{25,9},{2,18},{10... | collective-permute-start | bytes 1572872 | tf_op jit(solution)/shard_map/ppermute | solution.py:34
  334.0 34.1 %collective-permute-start.36 = (bf16[4,128,512]{2,1,0:T(8,128)(2,1)}, bf16[4,128,512]{2,1,0:T(8,128)(2,1)}, u32[]{:S(2)}, u32[]{:S(2)}) collective-permute-start(bf16[4,128,512]{2,1,0:T(8,128)(2,1)} %get-tuple-element.315), channel_id=1, source_target_pairs={{0,1},{1,0},{2,3},{3,2},{4,5},{5,4},{6,7},{7,6},{8,9},{9,8},{10,11... | collective-permute-start | bytes 1572872 | tf_op jit(solution)/shard_map/ppermute | solution.py:37
  348.7 41.6 %collective-permute-start.39 = (bf16[2,4,128,512]{3,2,1,0:T(8,128)(2,1)}, bf16[2,4,128,512]{3,2,1,0:T(8,128)(2,1)}, u32[]{:S(2)}, u32[]{:S(2)}) collective-permute-start(bf16[2,4,128,512]{3,2,1,0:T(8,128)(2,1)} %get-tuple-element.328), channel_id=1, source_target_pairs={{0,1},{1,0},{2,3},{3,2},{4,5},{5,4},{6,7},{7,6},{8,9},{9,8},{10,11... | collective-permute-start | bytes 3145736 | tf_op jit(solution)/shard_map/ppermute | solution.py:37
  349.2 41.1 %collective-permute-start.38 = (bf16[2,4,128,512]{3,2,1,0:T(8,128)(2,1)}, bf16[2,4,128,512]{3,2,1,0:T(8,128)(2,1)}, u32[]{:S(2)}, u32[]{:S(2)}) collective-permute-start(bf16[2,4,128,512]{3,2,1,0:T(8,128)(2,1)} %get-tuple-element.326), channel_id=1, source_target_pairs={{0,16},{8,24},{16,0},{24,8},{1,17},{9,25},{17,1},{25,9},{2,18},{10... | collective-permute-start | bytes 3145736 | tf_op jit(solution)/shard_map/ppermute | solution.py:34
  371.5 38.2 %all-to-all-start.4 = ((bf16[4,128,1024]{2,1,0:T(8,128)(2,1)}), bf16[4,128,1024]{2,1,0:T(8,128)(2,1)}, u32[]{:S(2)}, u32[]{:S(2)}) async-start(bf16[4,128,1024]{2,1,0:T(8,128)(2,1)} %sums.17), calls=%async_computation.4 | async-start | bytes 2097152 | tf_op jit(solution)/shard_map/all_to_all | solution.py:177
  409.7 31.2 %all-to-all-start.6 = ((bf16[4,128,1024]{2,1,0:T(8,128)(2,1)}), bf16[4,128,1024]{2,1,0:T(8,128)(2,1)}, u32[]{:S(2)}, u32[]{:S(2)}) async-start(bf16[4,128,1024]{2,1,0:T(8,128)(2,1)} %sums.20), calls=%async_computation.6 | async-start | bytes 2097152 | tf_op jit(solution)/shard_map/all_to_all | solution.py:177
  440.9 28.7 %all-to-all-start.7 = ((bf16[4,128,1024]{2,1,0:T(8,128)(2,1)}), bf16[4,128,1024]{2,1,0:T(8,128)(2,1)S(1)}, u32[]{:S(2)}, u32[]{:S(2)}) async-start(bf16[4,128,1024]{2,1,0:T(8,128)(2,1)} %sums.23), calls=%async_computation.7 | async-start | bytes 2097152 | tf_op jit(solution)/shard_map/all_to_all | solution.py:177
  469.6 28.7 %all-to-all-start.5 = ((bf16[4,128,1024]{2,1,0:T(8,128)(2,1)}), bf16[4,128,1024]{2,1,0:T(8,128)(2,1)S(1)}, u32[]{:S(2)}, u32[]{:S(2)}) async-start(bf16[4,128,1024]{2,1,0:T(8,128)(2,1)} %sums.22), calls=%async_computation.5 | async-start | bytes 2097152 | tf_op jit(solution)/shard_map/all_to_all | solution.py:177
  (90 other events, 997.4 us)
